TPU v7x, 256 devices: a whole 4x4x8 slice. The times are simulated.
256 devices in a mesh: dp: 4 (over y), vocab: 64 (over x, z, core).
Axes of the slice: x: 4, y: 4, z: 8, core: 2. Of those that a mesh axis runs over, the one named last changes fastest.
Arguments:
- hidden: bfloat16 [2048, 4096], P(('dp', 'vocab')), may hold values from -250 to 250
- targets: int32 [2048], P(('dp', 'vocab')), may hold values from 0 to 501759, as said below
- loss_weight: bfloat16 [2048], P(('dp', 'vocab')), may hold values from 0.5 to 2
- head_weight: bfloat16 [4096, 10240], P(None, 'vocab'), may hold values from -0.09375 to 0.09375
- cluster_weight: bfloat16 [4096, 64], P(None, 'vocab'), may hold values from -0.09375 to 0.09375
- tail_proj: bfloat16 [64, 4096, 1024], P('vocab', None, 'dp'), may hold values from -0.09375 to 0.09375
- tail_out: bfloat16 [64, 1024, 7680], P('vocab', 'dp'), may hold values from -0.1875 to 0.1875
Outputs:
- hidden_grad: bfloat16 [2048, 4096], P(('dp', 'vocab'))
- head_grad: bfloat16 [4096, 10240], P('dp', 'vocab')
- cluster_grad: bfloat16 [4096, 64], P('dp', 'vocab')
- proj_grad: bfloat16 [64, 4096, 1024], P('vocab', None, 'dp')
- out_grad: bfloat16 [64, 1024, 7680], P('vocab', 'dp')
Inputs may be any that keep to these rules, and one draw needn't show every extreme that they name: In each block of 512 consecutive tokens exactly 256 targets are at or above 10240; at most 16 of them fall in one cluster, and some cluster holds exactly 16 of them in every block.
All inputs are finite; a program needn't handle non-finite values.
Results may differ from a plain program's by a relative error of at most 0.012.
The roundings to bfloat16 on the way count: a program that leaves them out, or rounds other values in their place, can miss the bound.
Values may be sent and summed in bfloat16 or wider, within the bound.
No kernel may reach another device: no remote copies, remote signals or barrier semaphores. Data moves between devices by JAX's collectives and lax.ppermute only.
A program may use at most 128 MiB of HBM per device.

v0:
```python
import jax
import jax.numpy as jnp
from jax import lax
from jax.sharding import Mesh
from jax.sharding import PartitionSpec as P


HEAD = 10240
CV = 7680
CAP = 16
OWN = 8
NX, NZ, NDP = 4, 8, 4
META = 128


F32, BF16 = jnp.float32, jnp.bfloat16


def shift(value, axis, step):
    n = lax.axis_size(axis)
    return lax.ppermute(value, axis, [(j, (j + step) % n) for j in range(n)])


def dot(a, b, ca=1, cb=0):
    return lax.dot_general(a, b, (((ca,), (cb,)), ((), ())), preferred_element_type=F32)


def swapped(parts, axis):
    return lax.all_to_all(parts, axis, split_axis=0, concat_axis=0, tiled=True)


def from_everyone(value, axis):
    return swapped(jnp.broadcast_to(value, (lax.axis_size(axis), *value.shape)), axis)


def gathered(hidden, targets, loss_weight):
    digits = jnp.stack(
        [
            (targets >> 16).astype(BF16),
            ((targets >> 8) & 255).astype(BF16),
            (targets & 255).astype(BF16),
            loss_weight,
        ],
        axis=1,
    )
    pay = jnp.concatenate([hidden, jnp.pad(digits, ((0, 0), (0, META - 4)))], axis=1)
    pay = from_everyone(pay, "z").reshape(NZ * OWN, -1)
    row = pay[:, : hidden.shape[1]]
    digits = pay[:, hidden.shape[1] :].astype(F32)
    target = digits[:, 0] * 65536.0 + digits[:, 1] * 256.0 + digits[:, 2]
    meta = from_everyone(jnp.stack([target, digits[:, 3]]), ("dp", "x", "core"))
    own = jnp.concatenate([row] + [shift(row, "x", -k) for k in range(1, NX)], axis=0)
    other = shift(own, "core", 1)
    return own, other, meta.reshape(NDP, NX, 2, 2, NZ * OWN)


def joined_stats(top, total):
    first = lax.axis_index("core") == 0
    place = lax.axis_index("x")

    def turned(stats, start):
        stats = jnp.where(first, stats, stats[:, ::-1])
        return lax.dynamic_slice_in_dim(jnp.concatenate([stats] * 2, axis=2), start, NX, 2)

    shape = (2, 2, NX, NZ * OWN)
    stats = turned(jnp.stack([top, total]).reshape(shape), lax.rem(NX - place, NX))
    every = from_everyone(stats.reshape(2, -1), ("x", "z", "core"))
    top = jnp.max(every[:, 0], axis=0)
    total = jnp.sum(every[:, 1] * jnp.exp(every[:, 0] - top), axis=0)
    stats = turned(jnp.stack([top, total]).reshape(shape), place).reshape(2, -1)
    return stats[0], stats[1]


def step(hidden, targets, loss_weight, head_weight, cluster_weight, tail_proj, tail_out):
    x_index, z_index, core_index = (lax.axis_index(a) for a in ("x", "z", "core"))
    vocab_index = lax.axis_index(("x", "z", "core"))
    dp_index = lax.axis_index("dp")
    model, width = head_weight.shape
    weight = jnp.concatenate([head_weight, cluster_weight], axis=1)
    own, other, meta = gathered(hidden, targets, loss_weight)
    side = own.shape[0]

    out = tail_out[0]
    part = out.shape[1] // NDP
    outs = []
    for k in range(NDP):
        piece = lax.dynamic_slice_in_dim(out, lax.rem(dp_index + k, NDP) * part, part, 1)
        outs.append(shift(piece, "dp", k) if k else piece)

    every_target = meta[:, :, :, 0].reshape(NDP, -1).astype(jnp.int32)
    every_gain = meta[:, :, :, 1].reshape(NDP, -1)
    offset = every_target - HEAD
    cluster = jnp.where(offset >= 0, offset // CV, -1)
    at = jnp.arange(cluster.shape[1], dtype=jnp.int32)
    earlier = (cluster[:, :, None] == cluster[:, None, :]) & (at[:, None] < at[None, :])
    rank = jnp.sum(earlier.astype(jnp.int32), axis=1)
    every_slot = jnp.where(cluster >= 0, cluster * CAP + rank, -1)
    caps = jnp.arange(CAP, dtype=jnp.int32)
    holds = every_slot[:, None, :] == vocab_index * CAP + caps[None, :, None]
    words = jnp.sum(jnp.where(holds, (offset % CV)[:, None, :], 0), axis=2).reshape(-1)
    gain_tail = jnp.sum(jnp.where(holds, every_gain[:, None, :], 0.0), axis=2).reshape(-1)

    block = jnp.stack([every_target.astype(F32), every_gain, every_slot.astype(F32)])
    block = lax.dynamic_index_in_dim(block, dp_index, 1, keepdims=False)
    block = block.reshape(3, NX, 2, NZ * OWN)
    block = lax.dynamic_slice_in_dim(jnp.concatenate([block] * 2, axis=1), x_index, NX, 1)
    block = jnp.where(core_index == 0, block, block[:, :, ::-1])
    block = jnp.swapaxes(block, 1, 2).reshape(3, -1)
    target = block[0].astype(jnp.int32)
    gain = block[1]
    slot = block[2].astype(jnp.int32)
    offset = target - HEAD

    select = (slot[None, :] == vocab_index * CAP + caps[:, None]).astype(BF16)
    picked = (dot(select[:, :side], own) + dot(select[:, side:], other)).astype(BF16)
    rows = from_everyone(picked, "dp").reshape(NDP * CAP, -1)
    proj = tail_proj[0]
    reduced = dot(rows, proj).astype(BF16)
    inner = [reduced] + [shift(reduced, "dp", k) for k in range(1, NDP)]
    share = dot(inner[0], outs[0])
    for k in range(1, NDP):
        share = share + dot(inner[k], outs[k])
    top = jnp.max(share, axis=1)
    total = jnp.sum(jnp.exp(share - top[:, None]), axis=1)
    every = from_everyone(jnp.stack([top, total]), "dp")
    top = jnp.max(every[:, 0], axis=0)
    total = jnp.sum(every[:, 1] * jnp.exp(every[:, 0] - top), axis=0)
    columns = dp_index * part + jnp.arange(part, dtype=jnp.int32)
    hot = (columns[None, :] == words[:, None]).astype(F32)
    share_delta = (
        gain_tail[:, None] * (jnp.exp(share - top[:, None]) / total[:, None] - hot)
    ).astype(BF16)
    reduced_grad = dot(share_delta, outs[0], 1, 1)
    for k in range(1, NDP):
        reduced_grad = reduced_grad + shift(dot(share_delta, outs[k], 1, 1), "dp", -k)
    reduced_grad = reduced_grad.astype(BF16)
    tail_partial = dot(reduced_grad, proj, 1, 1).astype(BF16)
    tail_sum = jnp.sum(
        swapped(tail_partial.reshape(NDP, CAP, model), "dp").astype(F32), axis=0
    ).astype(BF16)

    (own, other), _ = lax.optimization_barrier(((own, other), picked))
    logits = jnp.concatenate([dot(own, weight), dot(other, weight)], axis=0)
    lane = jnp.arange(width + 1, dtype=jnp.int32)
    columns = jnp.where(lane < width, vocab_index * width + lane, HEAD + vocab_index)
    target_column = jnp.where(offset >= 0, HEAD + offset // CV, target)
    top = jnp.max(logits, axis=1)
    total = jnp.sum(jnp.exp(logits - top[:, None]), axis=1)
    top, total = joined_stats(top, total)
    hot = (columns[None, :] == target_column[:, None]).astype(F32)
    delta = (
        gain[:, None] * (jnp.exp(logits - top[:, None]) / total[:, None] - hot)
    ).astype(BF16)
    near, far = delta[:side], delta[side:]
    far_part = dot(far, weight, 1, 1).astype(BF16)
    from_core = shift(far_part, "core", 1)
    pair = (dot(near, weight, 1, 1) + from_core.astype(F32)).reshape(NX, NZ * OWN, model)
    pair_16 = pair.astype(BF16)
    from_x = [shift(pair_16[k], "x", k) for k in range(1, NX)]
    chip = pair[0]
    for piece in from_x:
        chip = chip + piece.astype(F32)

    tail_all = [tail_sum] + [shift(tail_sum, "x", -k) for k in range(1, NX)]
    near_slot = slot.reshape(2, NX, NZ * OWN)[:, 0].reshape(-1)
    source_x = lax.rem(x_index + jnp.arange(NX, dtype=jnp.int32), NX)
    source = (source_x * NZ + z_index) * 2 + core_index
    source_slot = (source[:, None] * CAP + caps[None, :]).reshape(-1)
    place = (source_slot[:, None] == near_slot[None, :]).astype(BF16)
    tail_all = jnp.concatenate(tail_all, axis=0)
    rest = NZ * OWN
    far_tail = dot(place[:, rest:], tail_all, 0, 0).astype(BF16)
    tail_from_core = shift(far_tail, "core", 1)
    chip = chip + dot(place[:, :rest], tail_all, 0, 0) + tail_from_core.astype(F32)
    last = swapped(chip.reshape(NZ, OWN, model).astype(BF16), "z")
    hidden_grad = jnp.sum(last.astype(F32), axis=0).astype(BF16)

    grad_t = (dot(near, own, 0, 0) + dot(far, other, 0, 0)).astype(BF16)
    block = model // NDP
    pieces = [
        lax.dynamic_slice_in_dim(grad_t, lax.rem(dp_index + k, NDP) * block, block, 1)
        for k in range(NDP)
    ]
    arrived = [shift(pieces[k], "dp", k) for k in range(1, NDP)]
    head_sum = sum((p.astype(F32) for p in arrived), pieces[0].astype(F32)).astype(BF16)
    word_delta = from_everyone(share_delta, "dp")
    word_delta = jnp.swapaxes(word_delta, 0, 1).reshape(NDP * CAP, -1)
    out_grad = dot(reduced, word_delta, 0, 0).astype(BF16)
    proj_grad = dot(rows, reduced_grad, 0, 0).astype(BF16)
    return (
        hidden_grad,
        head_sum[:width].T,
        head_sum[width:].T,
        proj_grad[None],
        out_grad[None],
    )


def solution(mesh):
    fine = Mesh(mesh.devices.reshape(NDP, NX, NZ, 2), ("dp", "x", "z", "core"))
    vocab = ("x", "z", "core")
    return jax.shard_map(
        step,
        mesh=fine,
        in_specs=(
            P(("dp", *vocab), None),
            P(("dp", *vocab)),
            P(("dp", *vocab)),
            P(None, vocab),
            P(None, vocab),
            P(vocab, None, "dp"),
            P(vocab, "dp", None),
        ),
        out_specs=(
            P(("dp", *vocab), None),
            P("dp", vocab),
            P("dp", vocab),
            P(vocab, None, "dp"),
            P(vocab, "dp", None),
        ),
        check_vma=False,
    )
```

profile of v0, /device:TPU:8, one launch (start us, length us, event | category | flops | bytes accessed | tf_op | source)
XLA Modules:
  0.0 256.3 jit_solution(13434950382186077768)
XLA Ops:
  3.9 8.5 %all-to-all-start = ((bf16[8,8,4224]{2,1,0:T(8,128)(2,1)}), bf16[8,8,4224]{2,1,0:T(8,128)(2,1)}, u32[]{:S(2)}, u32[]{:S(2)}) async-start(bf16[8,8,4224]{2,1,0:T(8,128)(2,1)} %broadcast_in_dim.78), calls=%async_computation | async-start | bytes 1081344 | tf_op jit(solution)/shard_map/all_to_all | solution.py:29
  12.4 3.5 %dynamic-slice_bitcast_fusion.1 = (bf16[256,1920]{1,0:T(8,128)(2,1)}, bf16[256,1920]{1,0:T(8,128)(2,1)}, bf16[256,1920]{1,0:T(8,128)(2,1)}) fusion(bf16[1,256,7680]{2,1,0:T(8,128)(2,1)} %param.13, s32[]{:T(128)S(6)} %select_n.183, s32[]{:T(128)S(6)} %select_n.182, s32[]{:T(128)S(6)} %select_n.184), kind=kLoop, calls=%fused_computation.33 | loop fusion | bytes 5898252 | tf_op jit(solution)/shard_map/dynamic_slice | solution.py:87
  15.8 2.3 collective-permute-start.11
  21.5 8.8 %all-to-all-done = bf16[8,8,4224]{2,1,0:T(8,128)(2,1)} async-done(((bf16[8,8,4224]{2,1,0:T(8,128)(2,1)}), bf16[8,8,4224]{2,1,0:T(8,128)(2,1)}, u32[]{:S(2)}, u32[]{:S(2)}) %all-to-all-start) | async-done | bytes 540704 | tf_op jit(solution)/shard_map/all_to_all | solution.py:29
  32.0 7.5 %all-to-all-start.1 = ((f32[32,1,128]{2,1,0:T(1,128)}), f32[32,1,128]{2,1,0:T(1,128)S(1)}, u32[]{:S(2)}, u32[]{:S(2)}) async-start(f32[32,1,128]{2,1,0:T(1,128)} %reshape.374), calls=%async_computation.1 | async-start | bytes 32768 | tf_op jit(solution)/shard_map/all_to_all | solution.py:29
  40.1 1.9 slice.139
  43.5 2.7 %collective-permute-start.1 = (bf16[64,4096]{1,0:T(8,128)(2,1)}, bf16[64,4096]{1,0:T(8,128)(2,1)}, u32[]{:S(2)}, u32[]{:S(2)}) collective-permute-start(bf16[64,4096]{1,0:T(8,128)(2,1)} %slice.139), channel_id=1, source_target_pairs={{0,32},{16,48},{32,0},{48,16},{1,33},{17,49},{33,1},{49,17},{2,34}... | collective-permute-start | bytes 1572872 | tf_op jit(solution)/shard_map/ppermute | solution.py:21
  47.6 14.6 %all-to-all-done.1 = f32[32,1,128]{2,1,0:T(1,128)S(1)} async-done(((f32[32,1,128]{2,1,0:T(1,128)}), f32[32,1,128]{2,1,0:T(1,128)S(1)}, u32[]{:S(2)}, u32[]{:S(2)}) %all-to-all-start.1) | async-done | bytes 16416 | tf_op jit(solution)/shard_map/all_to_all | solution.py:29
  69.9 3.1 %pad_maximum_fusion = bf16[256,4096]{1,0:T(8,128)(2,1)} fusion(bf16[64,4096]{1,0:T(8,128)(2,1)} %collective-permute-done.2, bf16[64,4096]{1,0:T(8,128)(2,1)} %collective-permute-done.1, bf16[64,4096]{1,0:T(8,128)(2,1)} %collective-permute-done, bf16[64,4096]{1,0:T(8,128)(2,1)} %slice.139), kind=kLoop, calls=%fused_computation.16 | loop fusion | flops 8388608 | bytes 4194304 | tf_op jit(solution)/shard_map/concatenate | solution.py:52
  79.1 2.0 fusion.45
  81.1 2.6 %fusion.3 = bf16[16,4096]{1,0:T(8,128)(2,1)} fusion(f32[16,4096]{1,0:T(8,128)S(1)} %fusion.45, bf16[256,4096]{1,0:T(8,128)(2,1)} %pad_maximum_fusion, pred[16,512]{1,0:T(8,128)(4,1)S(1)} %broadcast_compare_fusion.1), kind=kOutput, calls=%fused_computation.10 | convolution fusion | flops 33685504 | bytes 2494464 | tf_op jit(solution)/shard_map/dot_general | solution.py:25
  83.7 2.4 fusion.79
  86.2 2.5 fusion.80
  89.6 1.8 broadcast_in_dim.85
  91.4 5.1 %all-to-all-start.3 = ((bf16[4,16,4096]{2,1,0:T(8,128)(2,1)}), bf16[4,16,4096]{2,1,0:T(8,128)(2,1)}, u32[]{:S(2)}, u32[]{:S(2)}) async-start(bf16[4,16,4096]{2,1,0:T(8,128)(2,1)} %broadcast_in_dim.85), calls=%async_computation.3 | async-start | bytes 1048576 | tf_op jit(solution)/shard_map/all_to_all | solution.py:29
  96.5 8.9 %all-to-all-done.3 = bf16[4,16,4096]{2,1,0:T(8,128)(2,1)} async-done(((bf16[4,16,4096]{2,1,0:T(8,128)(2,1)}), bf16[4,16,4096]{2,1,0:T(8,128)(2,1)}, u32[]{:S(2)}, u32[]{:S(2)}) %all-to-all-start.3) | async-done | bytes 524320 | tf_op jit(solution)/shard_map/all_to_all | solution.py:29
  110.5 2.8 %collective-permute-start.10 = (bf16[64,256]{1,0:T(8,128)(2,1)S(1)}, bf16[64,256]{1,0:T(8,128)(2,1)S(1)}, u32[]{:S(2)}, u32[]{:S(2)}) collective-permute-start(bf16[64,256]{1,0:T(8,128)(2,1)S(1)} %fusion.8), channel_id=1, source_target_pairs={{0,128},{64,192},{128,0},{192,64},{1,129},{65,193},{129,1},{193,65... | collective-permute-start | bytes 98312 | tf_op jit(solution)/shard_map/ppermute | solution.py:21
  116.4 1.6 fusion.77
  119.7 4.8 %all-to-all-start.4 = ((f32[4,1,128]{2,1,0:T(1,128)}), f32[4,1,128]{2,1,0:T(1,128)S(1)}, u32[]{:S(2)}, u32[]{:S(2)}) async-start(f32[4,1,128]{2,1,0:T(1,128)} %reshape.376), calls=%async_computation.4 | async-start | bytes 4096 | tf_op jit(solution)/shard_map/all_to_all | solution.py:29
  124.6 3.6 %all-to-all-done.4 = f32[4,1,128]{2,1,0:T(1,128)S(1)} async-done(((f32[4,1,128]{2,1,0:T(1,128)}), f32[4,1,128]{2,1,0:T(1,128)S(1)}, u32[]{:S(2)}, u32[]{:S(2)}) %all-to-all-start.4) | async-done | bytes 2080 | tf_op jit(solution)/shard_map/all_to_all | solution.py:29
  129.0 10.7 %all-to-all-start.2 = ((f32[64,2,512]{2,1,0:T(2,128)}), f32[64,2,512]{2,1,0:T(2,128)}, u32[]{:S(2)}, u32[]{:S(2)}) async-start(f32[64,2,512]{2,1,0:T(2,128)} %broadcast_in_dim.80), calls=%async_computation.2 | async-start | bytes 524288 | tf_op jit(solution)/shard_map/all_to_all | solution.py:29
  141.8 2.3 fusion.82
  145.6 2.3 fusion.83
  148.4 3.1 %all-to-all-done.2 = f32[64,2,512]{2,1,0:T(2,128)} async-done(((f32[64,2,512]{2,1,0:T(2,128)}), f32[64,2,512]{2,1,0:T(2,128)}, u32[]{:S(2)}, u32[]{:S(2)}) %all-to-all-start.2) | async-done | bytes 262176 | tf_op jit(solution)/shard_map/all_to_all | solution.py:29
  151.5 2.0 fusion.72
  156.1 2.1 convolution_convert_fusion.2
  158.2 1.6 fusion.84
  160.5 1.6 fusion.16
  162.2 2.2 collective-permute-done.16
  166.8 6.8 %all-to-all-start.5 = ((bf16[4,16,4096]{2,1,0:T(8,128)(2,1)}), bf16[4,16,4096]{2,1,0:T(8,128)(2,1)}, u32[]{:S(2)}, u32[]{:S(2)}) async-start(bf16[4,16,4096]{2,1,0:T(8,128)(2,1)} %bitcast.125), calls=%async_computation.5 | async-start | bytes 1048576 | tf_op jit(solution)/shard_map/all_to_all | solution.py:29
  174.6 7.2 %all-to-all-done.5 = bf16[4,16,4096]{2,1,0:T(8,128)(2,1)} async-done(((bf16[4,16,4096]{2,1,0:T(8,128)(2,1)}), bf16[4,16,4096]{2,1,0:T(8,128)(2,1)}, u32[]{:S(2)}, u32[]{:S(2)}) %all-to-all-start.5) | async-done | bytes 524320 | tf_op jit(solution)/shard_map/all_to_all | solution.py:29
  181.8 2.0 broadcast_in_dim.90
  183.8 5.7 %all-to-all-start.7 = ((bf16[4,64,1920]{2,1,0:T(8,128)(2,1)}), bf16[4,64,1920]{2,1,0:T(8,128)(2,1)}, u32[]{:S(2)}, u32[]{:S(2)}) async-start(bf16[4,64,1920]{2,1,0:T(8,128)(2,1)} %broadcast_in_dim.90), calls=%async_computation.7 | async-start | bytes 1966080 | tf_op jit(solution)/shard_map/all_to_all | solution.py:29
  189.4 1.8 reduce_sum.97
  192.3 2.9 %collective-permute-start.18 = (bf16[16,4096]{1,0:T(8,128)(2,1)}, bf16[16,4096]{1,0:T(8,128)(2,1)S(1)}, u32[]{:S(2)}, u32[]{:S(2)}) collective-permute-start(bf16[16,4096]{1,0:T(8,128)(2,1)} %reduce_sum.97), channel_id=1, source_target_pairs={{0,32},{16,48},{32,0},{48,16},{1,33},{17,49},{33,1},{49,17},{2,34}... | collective-permute-start | bytes 393224 | tf_op jit(solution)/shard_map/ppermute | solution.py:21
  196.6 2.2 fusion.32
  201.2 2.3 fusion.78
  203.6 1.6 collective-permute-start.5
  205.2 1.7 collective-permute-start.7
  208.0 2.2 fusion.2
  213.6 5.6 %collective-permute-done.5 = bf16[64,4096]{1,0:T(8,128)(2,1)S(1)} collective-permute-done((bf16[64,4096]{1,0:T(8,128)(2,1)S(1)}, bf16[64,4096]{1,0:T(8,128)(2,1)S(1)}, u32[]{:S(2)}, u32[]{:S(2)}) %collective-permute-start.5) | collective-permute-done | bytes 524320 | tf_op jit(solution)/shard_map/ppermute | solution.py:21
  219.2 2.1 collective-permute-start.22
  221.3 9.9 %collective-permute-done.6 = bf16[64,4096]{1,0:T(8,128)(2,1)S(1)} collective-permute-done((bf16[64,4096]{1,0:T(8,128)(2,1)S(1)}, bf16[64,4096]{1,0:T(8,128)(2,1)S(1)}, u32[]{:S(2)}, u32[]{:S(2)}) %collective-permute-start.6) | collective-permute-done | bytes 524320 | tf_op jit(solution)/shard_map/ppermute | solution.py:21
  232.4 4.7 %all-to-all-start.6 = ((bf16[8,8,4096]{2,1,0:T(8,128)(2,1)}), bf16[8,8,4096]{2,1,0:T(8,128)(2,1)}, u32[]{:S(2)}, u32[]{:S(2)}) async-start(bf16[8,8,4096]{2,1,0:T(8,128)(2,1)} %fusion.22), calls=%async_computation.6 | async-start | bytes 1048576 | tf_op jit(solution)/shard_map/all_to_all | solution.py:29
  237.1 3.1 %fusion.1 = bf16[1,4096,256]{2,1,0:T(8,128)(2,1)} fusion(bf16[64,4096]{1,0:T(8,128)(2,1)} %bitcast.10, bf16[64,256]{1,0:T(8,128)(2,1)S(1)} %add_convert_fusion.1), kind=kOutput, calls=%fused_computation.5 | convolution fusion | flops 135266304 | bytes 2654208 | tf_op jit(solution)/shard_map/dot_general | solution.py:25
  244.3 3.1 %fusion = bf16[1,256,7680]{2,1,0:T(8,128)(2,1)} fusion(bf16[64,256]{1,0:T(8,128)(2,1)S(1)} %fusion.8, bf16[64,7680]{1,0:T(8,128)(2,1)S(1)} %bitcast.124), kind=kOutput, calls=%fused_computation.1 | convolution fusion | flops 253624320 | bytes 4947968 | tf_op jit(solution)/shard_map/dot_general | solution.py:25
  247.4 7.1 %all-to-all-done.6 = bf16[8,8,4096]{2,1,0:T(8,128)(2,1)} async-done(((bf16[8,8,4096]{2,1,0:T(8,128)(2,1)}), bf16[8,8,4096]{2,1,0:T(8,128)(2,1)}, u32[]{:S(2)}, u32[]{:S(2)}) %all-to-all-start.6) | async-done | bytes 524320 | tf_op jit(solution)/shard_map/all_to_all | solution.py:29
  254.5 1.8 reduce_sum.98
  (191 shorter events, 62.5 us)
Async XLA Ops:
  0.6 104.7 %copy-start = (bf16[1,4096,256]{2,1,0:T(8,128)(2,1)S(1)}, bf16[1,4096,256]{2,1,0:T(8,128)(2,1)}, u32[]{:S(2)}) copy-start(bf16[1,4096,256]{2,1,0:T(8,128)(2,1)} %param.12) | copy-start | bytes 6291460
  3.9 26.4 %all-to-all-start = ((bf16[8,8,4224]{2,1,0:T(8,128)(2,1)}), bf16[8,8,4224]{2,1,0:T(8,128)(2,1)}, u32[]{:S(2)}, u32[]{:S(2)}) async-start(bf16[8,8,4224]{2,1,0:T(8,128)(2,1)} %broadcast_in_dim.78), calls=%async_computation | async-start | bytes 1081344 | tf_op jit(solution)/shard_map/all_to_all | solution.py:29
  15.8 5.7 %copy-start.13 = (bf16[4096,1]{0,1:T(2,128)(2,1)S(1)}, bf16[4096,1]{0,1:T(2,128)(2,1)}, u32[]{:S(2)}) copy-start(bf16[4096,1]{0,1:T(2,128)(2,1)} %param.11) | copy-start | bytes 24580
  15.8 100.5 %collective-permute-start.11 = (bf16[256,1920]{1,0:T(8,128)(2,1)}, bf16[256,1920]{1,0:T(8,128)(2,1)}, u32[]{:S(2)}, u32[]{:S(2)}) collective-permute-start(bf16[256,1920]{1,0:T(8,128)(2,1)} %get-tuple-element.13), channel_id=1, source_target_pairs={{0,128},{64,192},{128,0},{192,64},{1,129},{65,193},{129,1},{193,65... | collective-permute-start | bytes 2949128 | tf_op jit(solution)/shard_map/ppermute | solution.py:21
  18.1 92.3 %collective-permute-start.9 = (bf16[256,1920]{1,0:T(8,128)(2,1)}, bf16[256,1920]{1,0:T(8,128)(2,1)}, u32[]{:S(2)}, u32[]{:S(2)}) collective-permute-start(bf16[256,1920]{1,0:T(8,128)(2,1)} %get-tuple-element.14), channel_id=1, source_target_pairs={{0,64},{64,128},{128,192},{192,0},{1,65},{65,129},{129,193},{193,1... | collective-permute-start | bytes 2949128 | tf_op jit(solution)/shard_map/ppermute | solution.py:21
  32.0 30.3 %all-to-all-start.1 = ((f32[32,1,128]{2,1,0:T(1,128)}), f32[32,1,128]{2,1,0:T(1,128)S(1)}, u32[]{:S(2)}, u32[]{:S(2)}) async-start(f32[32,1,128]{2,1,0:T(1,128)} %reshape.374), calls=%async_computation.1 | async-start | bytes 32768 | tf_op jit(solution)/shard_map/all_to_all | solution.py:29
  42.0 27.4 %collective-permute-start.2 = (bf16[64,4096]{1,0:T(8,128)(2,1)}, bf16[64,4096]{1,0:T(8,128)(2,1)}, u32[]{:S(2)}, u32[]{:S(2)}) collective-permute-start(bf16[64,4096]{1,0:T(8,128)(2,1)} %slice.139), channel_id=1, source_target_pairs={{0,16},{16,32},{32,48},{48,0},{1,17},{17,33},{33,49},{49,1},{2,18}... | collective-permute-start | bytes 1572872 | tf_op jit(solution)/shard_map/ppermute | solution.py:21
  43.5 26.4 %collective-permute-start.1 = (bf16[64,4096]{1,0:T(8,128)(2,1)}, bf16[64,4096]{1,0:T(8,128)(2,1)}, u32[]{:S(2)}, u32[]{:S(2)}) collective-permute-start(bf16[64,4096]{1,0:T(8,128)(2,1)} %slice.139), channel_id=1, source_target_pairs={{0,32},{16,48},{32,0},{48,16},{1,33},{17,49},{33,1},{49,17},{2,34}... | collective-permute-start | bytes 1572872 | tf_op jit(solution)/shard_map/ppermute | solution.py:21
  46.1 23.7 %collective-permute-start = (bf16[64,4096]{1,0:T(8,128)(2,1)}, bf16[64,4096]{1,0:T(8,128)(2,1)}, u32[]{:S(2)}, u32[]{:S(2)}) collective-permute-start(bf16[64,4096]{1,0:T(8,128)(2,1)} %slice.139), channel_id=1, source_target_pairs={{0,48},{16,0},{32,16},{48,32},{1,49},{17,1},{33,17},{49,33},{2,50}... | collective-permute-start | bytes 1572872 | tf_op jit(solution)/shard_map/ppermute | solution.py:21
  69.4 4.3 %copy-start.19 = (s32[16]{0:T(128)S(1)}, s32[16]{0:T(128)}, u32[]{:S(2)}) copy-start(s32[16]{0:T(128)} %iota_add_fusion.2) | copy-start | bytes 196
  69.4 6.7 %copy-start.16 = (pred[1,4,512]{2,1,0:T(4,128)(4,1)S(1)}, pred[1,4,512]{2,1,0:T(4,128)(4,1)}, u32[]{:S(2)}) copy-start(pred[1,4,512]{2,1,0:T(4,128)(4,1)} %ge.54) | copy-start | bytes 6148
  69.5 6.7 %copy-start.17 = (pred[1,4,512]{2,1,0:T(4,128)(4,1)S(1)}, pred[1,4,512]{2,1,0:T(4,128)(4,1)}, u32[]{:S(2)}) copy-start(pred[1,4,512]{2,1,0:T(4,128)(4,1)} %reshape.363) | copy-start | bytes 6148
  69.5 6.7 %copy-start.10 = (f32[1,4,512]{2,1,0:T(4,128)S(1)}, f32[1,4,512]{2,1,0:T(4,128)}, u32[]{:S(2)}) copy-start(f32[1,4,512]{2,1,0:T(4,128)} %stack_reshape_squeeze.3) | copy-start | bytes 24580
  69.5 6.7 %copy-start.11 = (f32[1,4,512]{2,1,0:T(4,128)S(1)}, f32[1,4,512]{2,1,0:T(4,128)}, u32[]{:S(2)}) copy-start(f32[1,4,512]{2,1,0:T(4,128)} %convert_element_type.185) | copy-start | bytes 24580
  69.5 45.3 %collective-permute-start.13 = (bf16[256,1920]{1,0:T(8,128)(2,1)}, bf16[256,1920]{1,0:T(8,128)(2,1)}, u32[]{:S(2)}, u32[]{:S(2)}) collective-permute-start(bf16[256,1920]{1,0:T(8,128)(2,1)} %get-tuple-element.15), channel_id=1, source_target_pairs={{0,192},{64,0},{128,64},{192,128},{1,193},{65,1},{129,65},{193,129... | collective-permute-start | bytes 2949128 | tf_op jit(solution)/shard_map/ppermute | solution.py:21
  72.9 6.2 %collective-permute-start.3 = (bf16[256,4096]{1,0:T(8,128)(2,1)}, bf16[256,4096]{1,0:T(8,128)(2,1)}, u32[]{:S(2)}, u32[]{:S(2)}) collective-permute-start(bf16[256,4096]{1,0:T(8,128)(2,1)} %pad_maximum_fusion), channel_id=1, source_target_pairs={{0,1},{1,0},{2,3},{3,2},{4,5},{5,4},{6,7},{7,6},{8,9},{9,8},{10,11... | collective-permute-start | bytes 6291464 | tf_op jit(solution)/shard_map/ppermute | solution.py:21
  91.4 13.9 %all-to-all-start.3 = ((bf16[4,16,4096]{2,1,0:T(8,128)(2,1)}), bf16[4,16,4096]{2,1,0:T(8,128)(2,1)}, u32[]{:S(2)}, u32[]{:S(2)}) async-start(bf16[4,16,4096]{2,1,0:T(8,128)(2,1)} %broadcast_in_dim.85), calls=%async_computation.3 | async-start | bytes 1048576 | tf_op jit(solution)/shard_map/all_to_all | solution.py:29
  106.8 8.0 %collective-permute-start.12 = (bf16[64,256]{1,0:T(8,128)(2,1)S(1)}, bf16[64,256]{1,0:T(8,128)(2,1)S(1)}, u32[]{:S(2)}, u32[]{:S(2)}) collective-permute-start(bf16[64,256]{1,0:T(8,128)(2,1)S(1)} %fusion.8), channel_id=1, source_target_pairs={{0,192},{64,0},{128,64},{192,128},{1,193},{65,1},{129,65},{193,129... | collective-permute-start | bytes 98312 | tf_op jit(solution)/shard_map/ppermute | solution.py:21
  108.3 5.0 %collective-permute-start.8 = (bf16[64,256]{1,0:T(8,128)(2,1)S(1)}, bf16[64,256]{1,0:T(8,128)(2,1)S(1)}, u32[]{:S(2)}, u32[]{:S(2)}) collective-permute-start(bf16[64,256]{1,0:T(8,128)(2,1)S(1)} %fusion.8), channel_id=1, source_target_pairs={{0,64},{64,128},{128,192},{192,0},{1,65},{65,129},{129,193},{193,1... | collective-permute-start | bytes 98312 | tf_op jit(solution)/shard_map/ppermute | solution.py:21
  110.5 5.9 %collective-permute-start.10 = (bf16[64,256]{1,0:T(8,128)(2,1)S(1)}, bf16[64,256]{1,0:T(8,128)(2,1)S(1)}, u32[]{:S(2)}, u32[]{:S(2)}) collective-permute-start(bf16[64,256]{1,0:T(8,128)(2,1)S(1)} %fusion.8), channel_id=1, source_target_pairs={{0,128},{64,192},{128,0},{192,64},{1,129},{65,193},{129,1},{193,65... | collective-permute-start | bytes 98312 | tf_op jit(solution)/shard_map/ppermute | solution.py:21
  116.3 24.1 %copy-start.22 = (f32[64]{0:T(128)S(1)}, f32[64]{0:T(128)}, u32[]{:S(2)}) copy-start(f32[64]{0:T(128)} %mul.156) | copy-start | bytes 772
  116.3 24.1 %copy-start.23 = (s32[64]{0:T(128)S(1)}, s32[64]{0:T(128)}, u32[]{:S(2)}) copy-start(s32[64]{0:T(128)} %eq.106) | copy-start | bytes 772
  119.7 8.5 %all-to-all-start.4 = ((f32[4,1,128]{2,1,0:T(1,128)}), f32[4,1,128]{2,1,0:T(1,128)S(1)}, u32[]{:S(2)}, u32[]{:S(2)}) async-start(f32[4,1,128]{2,1,0:T(1,128)} %reshape.376), calls=%async_computation.4 | async-start | bytes 4096 | tf_op jit(solution)/shard_map/all_to_all | solution.py:29
  129.0 22.5 %all-to-all-start.2 = ((f32[64,2,512]{2,1,0:T(2,128)}), f32[64,2,512]{2,1,0:T(2,128)}, u32[]{:S(2)}, u32[]{:S(2)}) async-start(f32[64,2,512]{2,1,0:T(2,128)} %broadcast_in_dim.80), calls=%async_computation.2 | async-start | bytes 524288 | tf_op jit(solution)/shard_map/all_to_all | solution.py:29
  140.5 14.4 %copy-start.14 = (f32[512]{0:T(512)S(1)}, f32[512]{0:T(512)}, u32[]{:S(2)}) copy-start(f32[512]{0:T(512)} %mul.143) | copy-start | bytes 6148
  140.5 14.4 %copy-start.15 = (s32[512]{0:T(512)S(1)}, s32[512]{0:T(512)}, u32[]{:S(2)}) copy-start(s32[512]{0:T(512)} %add_select_fusion.5) | copy-start | bytes 6148
  140.5 14.4 %copy-start.20 = (s32[161]{0:T(256)S(1)}, s32[161]{0:T(256)}, u32[]{:S(2)}) copy-start(s32[161]{0:T(256)} %compare_select_fusion.4) | copy-start | bytes 1936
  141.8 3.8 %copy-start.1 = (bf16[64,1920]{1,0:T(8,128)(2,1)}, bf16[64,1920]{1,0:T(8,128)(2,1)S(1)}, u32[]{:S(2)}) copy-start(bf16[64,1920]{1,0:T(8,128)(2,1)S(1)} %multiply_convert_fusion) | copy-start | bytes 737284
  144.1 18.0 %collective-permute-start.14 = (f32[64,256]{1,0:T(8,128)}, f32[64,256]{1,0:T(8,128)}, u32[]{:S(2)}, u32[]{:S(2)}) collective-permute-start(f32[64,256]{1,0:T(8,128)} %fusion.82), channel_id=1, source_target_pairs={{0,192},{64,0},{128,64},{192,128},{1,193},{65,1},{129,65},{193,129... | collective-permute-start | bytes 196616 | tf_op jit(solution)/shard_map/ppermute | solution.py:21
  147.9 14.3 %collective-permute-start.15 = (f32[64,256]{1,0:T(8,128)}, f32[64,256]{1,0:T(8,128)}, u32[]{:S(2)}, u32[]{:S(2)}) collective-permute-start(f32[64,256]{1,0:T(8,128)} %fusion.83), channel_id=1, source_target_pairs={{0,128},{64,192},{128,0},{192,64},{1,129},{65,193},{129,1},{193,65... | collective-permute-start | bytes 196616 | tf_op jit(solution)/shard_map/ppermute | solution.py:21
  158.2 43.0 %collective-permute-start.4 = (bf16[256,4096]{1,0:T(8,128)(2,1)}, bf16[256,4096]{1,0:T(8,128)(2,1)}, u32[]{:S(2)}, u32[]{:S(2)}) collective-permute-start(bf16[256,4096]{1,0:T(8,128)(2,1)} %convolution_convert_fusion.2), channel_id=1, source_target_pairs={{0,1},{1,0},{2,3},{3,2},{4,5},{5,4},{6,7},{7,6},{8,9},{9,8},{10,11... | collective-permute-start | bytes 6291464 | tf_op jit(solution)/shard_map/ppermute | solution.py:21
  159.9 4.5 %collective-permute-start.16 = (f32[64,256]{1,0:T(8,128)S(1)}, f32[64,256]{1,0:T(8,128)S(1)}, u32[]{:S(2)}, u32[]{:S(2)}) collective-permute-start(f32[64,256]{1,0:T(8,128)S(1)} %fusion.84), channel_id=1, source_target_pairs={{0,64},{64,128},{128,192},{192,0},{1,65},{65,129},{129,193},{193,1... | collective-permute-start | bytes 196616 | tf_op jit(solution)/shard_map/ppermute | solution.py:21
  162.1 11.5 %copy-start.21 = (s32[4]{0:T(128)S(1)}, s32[4]{0:T(128)}, u32[]{:S(2)}) copy-start(s32[4]{0:T(128)} %fusion.67) | copy-start | bytes 52
  166.8 14.9 %all-to-all-start.5 = ((bf16[4,16,4096]{2,1,0:T(8,128)(2,1)}), bf16[4,16,4096]{2,1,0:T(8,128)(2,1)}, u32[]{:S(2)}, u32[]{:S(2)}) async-start(bf16[4,16,4096]{2,1,0:T(8,128)(2,1)} %bitcast.125), calls=%async_computation.5 | async-start | bytes 1048576 | tf_op jit(solution)/shard_map/all_to_all | solution.py:29
  183.8 48.6 %all-to-all-start.7 = ((bf16[4,64,1920]{2,1,0:T(8,128)(2,1)}), bf16[4,64,1920]{2,1,0:T(8,128)(2,1)}, u32[]{:S(2)}, u32[]{:S(2)}) async-start(bf16[4,64,1920]{2,1,0:T(8,128)(2,1)} %broadcast_in_dim.90), calls=%async_computation.7 | async-start | bytes 1966080 | tf_op jit(solution)/shard_map/all_to_all | solution.py:29
  191.3 9.1 %copy-start.9 = (bf16[16,4096]{1,0:T(8,128)(2,1)S(1)}, bf16[16,4096]{1,0:T(8,128)(2,1)}, u32[]{:S(2)}) copy-start(bf16[16,4096]{1,0:T(8,128)(2,1)} %reduce_sum.97) | copy-start | bytes 393220
  191.3 9.9 %copy-start.7 = (bf16[512,161]{0,1:T(8,128)(2,1)S(1)}, bf16[512,161]{0,1:T(8,128)(2,1)}, u32[]{:S(2)}) copy-start(bf16[512,161]{0,1:T(8,128)(2,1)} %copy-done.6) | copy-start | bytes 494596
  191.3 7.5 %collective-permute-start.19 = (bf16[16,4096]{1,0:T(8,128)(2,1)}, bf16[16,4096]{1,0:T(8,128)(2,1)S(1)}, u32[]{:S(2)}, u32[]{:S(2)}) collective-permute-start(bf16[16,4096]{1,0:T(8,128)(2,1)} %reduce_sum.97), channel_id=1, source_target_pairs={{0,16},{16,32},{32,48},{48,0},{1,17},{17,33},{33,49},{49,1},{2,18}... | collective-permute-start | bytes 393224 | tf_op jit(solution)/shard_map/ppermute | solution.py:21
  192.3 7.5 %collective-permute-start.18 = (bf16[16,4096]{1,0:T(8,128)(2,1)}, bf16[16,4096]{1,0:T(8,128)(2,1)S(1)}, u32[]{:S(2)}, u32[]{:S(2)}) collective-permute-start(bf16[16,4096]{1,0:T(8,128)(2,1)} %reduce_sum.97), channel_id=1, source_target_pairs={{0,32},{16,48},{32,0},{48,16},{1,33},{17,49},{33,1},{49,17},{2,34}... | collective-permute-start | bytes 393224 | tf_op jit(solution)/shard_map/ppermute | solution.py:21
  195.2 5.2 %collective-permute-start.17 = (bf16[16,4096]{1,0:T(8,128)(2,1)}, bf16[16,4096]{1,0:T(8,128)(2,1)S(1)}, u32[]{:S(2)}, u32[]{:S(2)}) collective-permute-start(bf16[16,4096]{1,0:T(8,128)(2,1)} %reduce_sum.97), channel_id=1, source_target_pairs={{0,48},{16,0},{32,16},{48,32},{1,49},{17,1},{33,17},{49,33},{2,50}... | collective-permute-start | bytes 393224 | tf_op jit(solution)/shard_map/ppermute | solution.py:21
  200.8 12.2 %collective-permute-start.20 = (bf16[64,4096]{1,0:T(8,128)(2,1)S(1)}, bf16[64,4096]{1,0:T(8,128)(2,1)S(1)}, u32[]{:S(2)}, u32[]{:S(2)}) collective-permute-start(bf16[64,4096]{1,0:T(8,128)(2,1)S(1)} %convolution_convert_fusion.3), channel_id=1, source_target_pairs={{0,1},{1,0},{2,3},{3,2},{4,5},{5,4},{6,7},{7,6},{8,9},{9,8},{10,11... | collective-permute-start | bytes 1572872 | tf_op jit(solution)/shard_map/ppermute | solution.py:21
  203.6 15.6 %collective-permute-start.5 = (bf16[64,4096]{1,0:T(8,128)(2,1)S(1)}, bf16[64,4096]{1,0:T(8,128)(2,1)S(1)}, u32[]{:S(2)}, u32[]{:S(2)}) collective-permute-start(bf16[64,4096]{1,0:T(8,128)(2,1)S(1)} %get-tuple-element.16), channel_id=1, source_target_pairs={{0,16},{16,32},{32,48},{48,0},{1,17},{17,33},{33,49},{49,1},{2,18}... | collective-permute-start | bytes 1572872 | tf_op jit(solution)/shard_map/ppermute | solution.py:21
  205.2 16.0 %collective-permute-start.7 = (bf16[64,4096]{1,0:T(8,128)(2,1)S(1)}, bf16[64,4096]{1,0:T(8,128)(2,1)S(1)}, u32[]{:S(2)}, u32[]{:S(2)}) collective-permute-start(bf16[64,4096]{1,0:T(8,128)(2,1)S(1)} %get-tuple-element.17), channel_id=1, source_target_pairs={{0,48},{16,0},{32,16},{48,32},{1,49},{17,1},{33,17},{49,33},{2,50}... | collective-permute-start | bytes 1572872 | tf_op jit(solution)/shard_map/ppermute | solution.py:21
  206.9 24.3 %collective-permute-start.6 = (bf16[64,4096]{1,0:T(8,128)(2,1)S(1)}, bf16[64,4096]{1,0:T(8,128)(2,1)S(1)}, u32[]{:S(2)}, u32[]{:S(2)}) collective-permute-start(bf16[64,4096]{1,0:T(8,128)(2,1)S(1)} %get-tuple-element.18), channel_id=1, source_target_pairs={{0,32},{16,48},{32,0},{48,16},{1,33},{17,49},{33,1},{49,17},{2,34}... | collective-permute-start | bytes 1572872 | tf_op jit(solution)/shard_map/ppermute | solution.py:21
  211.1 29.1 %collective-permute-start.21 = (bf16[161,1024]{1,0:T(8,128)(2,1)}, bf16[161,1024]{1,0:T(8,128)(2,1)}, u32[]{:S(2)}, u32[]{:S(2)}) collective-permute-start(bf16[161,1024]{1,0:T(8,128)(2,1)} %get-tuple-element.19), channel_id=1, source_target_pairs={{0,64},{64,128},{128,192},{192,0},{1,65},{65,129},{129,193},{193,1... | collective-permute-start | bytes 989192 | tf_op jit(solution)/shard_map/ppermute | solution.py:21
  213.0 27.3 %collective-permute-start.23 = (bf16[161,1024]{1,0:T(8,128)(2,1)}, bf16[161,1024]{1,0:T(8,128)(2,1)}, u32[]{:S(2)}, u32[]{:S(2)}) collective-permute-start(bf16[161,1024]{1,0:T(8,128)(2,1)} %get-tuple-element.20), channel_id=1, source_target_pairs={{0,192},{64,0},{128,64},{192,128},{1,193},{65,1},{129,65},{193,129... | collective-permute-start | bytes 989192 | tf_op jit(solution)/shard_map/ppermute | solution.py:21
  219.2 21.0 %collective-permute-start.22 = (bf16[161,1024]{1,0:T(8,128)(2,1)}, bf16[161,1024]{1,0:T(8,128)(2,1)}, u32[]{:S(2)}, u32[]{:S(2)}) collective-permute-start(bf16[161,1024]{1,0:T(8,128)(2,1)} %get-tuple-element.21), channel_id=1, source_target_pairs={{0,128},{64,192},{128,0},{192,64},{1,129},{65,193},{129,1},{193,65... | collective-permute-start | bytes 989192 | tf_op jit(solution)/shard_map/ppermute | solution.py:21
  232.4 22.1 %all-to-all-start.6 = ((bf16[8,8,4096]{2,1,0:T(8,128)(2,1)}), bf16[8,8,4096]{2,1,0:T(8,128)(2,1)}, u32[]{:S(2)}, u32[]{:S(2)}) async-start(bf16[8,8,4096]{2,1,0:T(8,128)(2,1)} %fusion.22), calls=%async_computation.6 | async-start | bytes 1048576 | tf_op jit(solution)/shard_map/all_to_all | solution.py:29
  (8 other events, 21.7 us)
where the time goes:
time: 259 us; the launch traced here: 256 us
  starting transfers between devices  83.7 us (32%)
  waiting for transfers between devices  72.7 us (28%)
  matrix products  42.4 us (16%)
  local copies, waits for them, and re-layouts  28.4 us (11%)
  other arithmetic  27.8 us (11%)
    all_to_all x8, starting transfers between devices, swapped(): return lax.all_to_all(parts, axis, split_axis=0, concat_axis=0, tiled=True)  53.7 us
    all_to_all x8, waiting for transfers between devices, swapped(): return lax.all_to_all(parts, axis, split_axis=0, concat_axis=0, tiled=True)  53.2 us
    dot_general x22, matrix products, dot(): lax.dot_general(a, b, (((ca,), (cb,)), ((), ())), preferred_element_type=...  42.4 us
    ppermute x24, starting transfers between devices, shift(): return lax.ppermute(value, axis, [(j, (j + step) % n) for j in range(n)])  30 us
    ppermute x24, waiting for transfers between devices, shift(): return lax.ppermute(value, axis, [(j, (j + step) % n) for j in range(n)])  19.5 us
    broadcast_in_dim x6, local copies, waits for them, and re-layouts, from_everyone(): jnp.broadcast_to(value, (lax.axis_size(axis), *value.shape))  5.39 us
  transfers between devices with their start and end apart: 32, of which 12 were waited for; matrix products, arithmetic and copies ran while one was open for 35% of the time, Pallas kernels for 0%

commit v1 on v0

v1 whole, which is shorter than its diff:
```python
import jax
import jax.numpy as jnp
from jax import lax
from jax.sharding import Mesh
from jax.sharding import PartitionSpec as P


HEAD = 10240
CV = 7680
CAP = 16
OWN = 8
NX, NZ, NDP = 4, 8, 4
META = 128
CA = 1408


F32, BF16 = jnp.float32, jnp.bfloat16


def shift(value, axis, step):
    n = lax.axis_size(axis)
    return lax.ppermute(value, axis, [(j, (j + step) % n) for j in range(n)])


def dot(a, b, ca=1, cb=0):
    return lax.dot_general(a, b, (((ca,), (cb,)), ((), ())), preferred_element_type=F32)


def swapped(parts, axis):
    return lax.all_to_all(parts, axis, split_axis=0, concat_axis=0, tiled=True)


def from_everyone(value, axis):
    return swapped(jnp.broadcast_to(value, (lax.axis_size(axis), *value.shape)), axis)


def gathered(hidden, targets, loss_weight):
    digits = jnp.stack(
        [
            (targets >> 16).astype(BF16),
            ((targets >> 8) & 255).astype(BF16),
            (targets & 255).astype(BF16),
            loss_weight,
        ],
        axis=1,
    )
    model = hidden.shape[1]
    rest = model - CA
    a1 = hidden[:, :CA]
    pay = jnp.concatenate([hidden[:, CA:], jnp.pad(digits, ((0, 0), (0, META - 4)))], axis=1)
    a1 = jnp.concatenate([a1] + [shift(a1, "x", -k) for k in range(1, NX)], axis=0)
    b1 = from_everyone(pay, "z").reshape(NZ * OWN, -1)
    a1, b1 = lax.optimization_barrier((a1, b1))
    a2 = from_everyone(a1, "z").reshape(NZ, NX, OWN, CA)
    b2 = [b1] + [shift(b1, "x", -k) for k in range(1, NX)]
    digits = jnp.stack([b[:, rest : rest + 4] for b in b2]).astype(F32)
    target = digits[..., 0] * 65536.0 + digits[..., 1] * 256.0 + digits[..., 2]
    meta = jnp.stack([target, digits[..., 3]])
    meta = jnp.stack([meta, shift(meta, "core", 1)], axis=1)
    own = jnp.zeros((NX * NZ * OWN, model), BF16)
    for k in range(NX):
        own = own.at[k * NZ * OWN : (k + 1) * NZ * OWN, CA:].set(b2[k][:, :rest])
    own = own.at[:, :CA].set(jnp.swapaxes(a2, 0, 1).reshape(-1, CA))
    other = shift(own, "core", 1)
    return own, other, meta.reshape(2, -1)


def joined_stats(top, total):
    first = lax.axis_index("core") == 0
    place = lax.axis_index("x")

    def turned(stats, start):
        stats = jnp.where(first, stats, stats[:, ::-1])
        return lax.dynamic_slice_in_dim(jnp.concatenate([stats] * 2, axis=2), start, NX, 2)

    shape = (2, 2, NX, NZ * OWN)
    stats = turned(jnp.stack([top, total]).reshape(shape), lax.rem(NX - place, NX))
    every = from_everyone(stats.reshape(2, -1), ("x", "z", "core"))
    top = jnp.max(every[:, 0], axis=0)
    total = jnp.sum(every[:, 1] * jnp.exp(every[:, 0] - top), axis=0)
    stats = turned(jnp.stack([top, total]).reshape(shape), place).reshape(2, -1)
    return stats[0], stats[1]


def step(hidden, targets, loss_weight, head_weight, cluster_weight, tail_proj, tail_out):
    x_index, z_index, core_index = (lax.axis_index(a) for a in ("x", "z", "core"))
    vocab_index = lax.axis_index(("x", "z", "core"))
    model, width = head_weight.shape
    weight = jnp.concatenate([head_weight, cluster_weight], axis=1)
    own, other, meta = gathered(hidden, targets, loss_weight)
    side = own.shape[0]

    target = meta[0].astype(jnp.int32)
    gain = meta[1]
    offset = target - HEAD
    cluster = jnp.where(offset >= 0, offset // CV, -1)
    core_at, x_at, z_at, row_at = jnp.unravel_index(jnp.arange(2 * side), (2, NX, NZ, OWN))
    x_at = lax.rem(x_at + x_index, NX)
    token = ((x_at * NZ + z_at) * 2 + lax.bitwise_xor(core_at, core_index)) * OWN + row_at
    earlier = (cluster[:, None] == cluster[None, :]) & (token[:, None] < token[None, :])
    rank = jnp.sum(earlier.astype(jnp.int32), axis=0)
    slot = jnp.where(cluster >= 0, cluster * CAP + rank, -1)
    caps = jnp.arange(CAP, dtype=jnp.int32)
    holds = slot[None, :] == vocab_index * CAP + caps[:, None]
    words = jnp.sum(jnp.where(holds, (offset % CV)[None, :], 0), axis=1)
    gain_tail = jnp.sum(jnp.where(holds, gain[None, :], 0.0), axis=1)

    select = holds.astype(BF16)
    picked = (dot(select[:, :side], own) + dot(select[:, side:], other)).astype(BF16)
    rows = from_everyone(picked, "dp")
    rows = lax.dynamic_slice_in_dim(jnp.concatenate([rows] * 2), lax.axis_index("dp"), NDP)
    rows = rows.reshape(NDP * CAP, -1)
    proj = tail_proj[0]
    out = tail_out[0]
    reduced = dot(rows, proj).astype(BF16)
    partial = dot(reduced, out)
    share = partial[:CAP]
    for k in range(1, NDP):
        share = share + shift(partial[k * CAP : (k + 1) * CAP], "dp", k)
    top = jnp.max(share, axis=1, keepdims=True)
    share_exp = jnp.exp(share - top)
    total = jnp.sum(share_exp, axis=1, keepdims=True)
    hot = (jnp.arange(CV, dtype=jnp.int32)[None, :] == words[:, None]).astype(F32)
    share_delta = (gain_tail[:, None] * (share_exp / total - hot)).astype(BF16)
    word_delta = jnp.concatenate(
        [share_delta] + [shift(share_delta, "dp", -k) for k in range(1, NDP)], axis=0
    )
    reduced_grad = dot(word_delta, out, 1, 1).astype(BF16)
    tail_partial = dot(reduced_grad, proj, 1, 1)
    tail_sum = tail_partial[:CAP]
    for k in range(1, NDP):
        piece = tail_partial[k * CAP : (k + 1) * CAP].astype(BF16)
        tail_sum = tail_sum + shift(piece, "dp", k).astype(F32)
    tail_sum = tail_sum.astype(BF16)

    (own, other), _ = lax.optimization_barrier(((own, other), picked))
    logits = jnp.concatenate([dot(own, weight), dot(other, weight)], axis=0)
    lane = jnp.arange(width + 1, dtype=jnp.int32)
    columns = jnp.where(lane < width, vocab_index * width + lane, HEAD + vocab_index)
    target_column = jnp.where(offset >= 0, HEAD + offset // CV, target)
    top = jnp.max(logits, axis=1)
    total = jnp.sum(jnp.exp(logits - top[:, None]), axis=1)
    top, total = joined_stats(top, total)
    hot = (columns[None, :] == target_column[:, None]).astype(F32)
    delta = (
        gain[:, None] * (jnp.exp(logits - top[:, None]) / total[:, None] - hot)
    ).astype(BF16)
    near, far = delta[:side], delta[side:]
    far_part = dot(far, weight, 1, 1).astype(BF16)
    from_core = shift(far_part, "core", 1)
    pair = (dot(near, weight, 1, 1) + from_core.astype(F32)).reshape(NX, NZ * OWN, model)
    pair_16 = pair.astype(BF16)
    from_x = [shift(pair_16[k], "x", k) for k in range(1, NX)]
    chip = pair[0]
    for piece in from_x:
        chip = chip + piece.astype(F32)

    tail_all = [tail_sum] + [shift(tail_sum, "x", -k) for k in range(1, NX)]
    near_slot = slot.reshape(2, NX, NZ * OWN)[:, 0].reshape(-1)
    source_x = lax.rem(x_index + jnp.arange(NX, dtype=jnp.int32), NX)
    source = (source_x * NZ + z_index) * 2 + core_index
    source_slot = (source[:, None] * CAP + caps[None, :]).reshape(-1)
    place = (source_slot[:, None] == near_slot[None, :]).astype(BF16)
    tail_all = jnp.concatenate(tail_all, axis=0)
    rest = NZ * OWN
    far_tail = dot(place[:, rest:], tail_all, 0, 0).astype(BF16)
    tail_from_core = shift(far_tail, "core", 1)
    chip = chip + dot(place[:, :rest], tail_all, 0, 0) + tail_from_core.astype(F32)
    last = swapped(chip.reshape(NZ, OWN, model).astype(BF16), "z")
    hidden_grad = jnp.sum(last.astype(F32), axis=0).astype(BF16)

    grad_t = (dot(near, own, 0, 0) + dot(far, other, 0, 0)).astype(BF16)
    grad_t = jnp.moveaxis(grad_t.reshape(width + 1, NDP, -1), 1, 0)
    grad_t = swapped(grad_t, "dp")
    head_sum = jnp.sum(grad_t.astype(F32), axis=0).astype(BF16)
    out_grad = dot(reduced, word_delta, 0, 0).astype(BF16)
    proj_grad = dot(rows, reduced_grad, 0, 0).astype(BF16)
    return (
        hidden_grad,
        head_sum[:width].T,
        head_sum[width:].T,
        proj_grad[None],
        out_grad[None],
    )


def solution(mesh):
    fine = Mesh(mesh.devices.reshape(NDP, NX, NZ, 2), ("dp", "x", "z", "core"))
    vocab = ("x", "z", "core")
    return jax.shard_map(
        step,
        mesh=fine,
        in_specs=(
            P(("dp", *vocab), None),
            P(("dp", *vocab)),
            P(("dp", *vocab)),
            P(None, vocab),
            P(None, vocab),
            P(vocab, None, "dp"),
            P(vocab, "dp", None),
        ),
        out_specs=(
            P(("dp", *vocab), None),
            P("dp", vocab),
            P("dp", vocab),
            P(vocab, None, "dp"),
            P(vocab, "dp", None),
        ),
        check_vma=False,
    )
```

time: 259 us -> 239 us (0.923)
  matrix products: 42.4 us -> 27.1 us
  starting transfers between devices: 83.7 us -> 70.4 us
  local copies, waits for them, and re-layouts: 28.4 us -> 39.8 us
  other arithmetic: 27.8 us -> 24.4 us
    ppermute x24 -> x25, waiting for transfers between devices: 19.5 us -> 46.3 us  [shift(): return lax.ppermute(value, axis, [(j, (j + step) % n) for j in range(n)])]
    all_to_all x8 -> x6, waiting for transfers between devices: 53.2 us -> 27.9 us  [swapped(): return lax.all_to_all(parts, axis, split_axis=0, concat_axis=0, tiled=True)]
    all_to_all x8 -> x6, starting transfers between devices: 53.7 us -> 36.3 us  [swapped(): return lax.all_to_all(parts, axis, split_axis=0, concat_axis=0, tiled=True)]
    dot_general x22 -> x16, matrix products: 42.4 us -> 27.1 us  [dot(): lax.dot_general(a, b, (((ca,), (cb,)), ((), ())), preferred_element_type=...]
    scatter x0 -> x4, local copies, waits for them, and re-layouts: none -> 10.6 us  [gathered(): own = own.at[k * NZ * OWN:(k + 1) * NZ * OWN, CA:].set(b2[k][:, :rest])]
    dynamic_slice x2 -> x0, local copies, waits for them, and re-layouts: 4.46 us -> none  [the longest x1 3.46 us: step(): lax.dynamic_slice_in_dim(out, lax.rem(dp_index + k, NDP) * part, part, 1)]
    another operation x2 -> x6, other arithmetic: 0.02 us -> 4.35 us  [the longest x1 0.01 us: gathered(): meta = from_everyone(jnp.stack([target, digits[:, 3]]), ('dp', 'x', 'core'))]
    ppermute x24 -> x25, starting transfers between devices: 30 us -> 34.1 us  [shift(): return lax.ppermute(value, axis, [(j, (j + step) % n) for j in range(n)])]
  transfers between devices with their start and end apart: 32 -> 31, of which waited for: 12 -> 19; matrix products, arithmetic and copies ran while one was open for 35% -> 30% of each run, Pallas kernels for 0% -> 0%
where the time goes in v1:
time: 239 us; the launch traced here: 237 us
  waiting for transfers between devices  74.1 us (31%)
  starting transfers between devices  70.4 us (29%)
  local copies, waits for them, and re-layouts  39.8 us (17%)
  matrix products  27.1 us (11%)
  other arithmetic  24.4 us (10%)
    ppermute x25, waiting for transfers between devices, shift(): return lax.ppermute(value, axis, [(j, (j + step) % n) for j in range(n)])  46.3 us
    all_to_all x6, starting transfers between devices, swapped(): return lax.all_to_all(parts, axis, split_axis=0, concat_axis=0, tiled=True)  36.3 us
    ppermute x25, starting transfers between devices, shift(): return lax.ppermute(value, axis, [(j, (j + step) % n) for j in range(n)])  34.1 us
    all_to_all x6, waiting for transfers between devices, swapped(): return lax.all_to_all(parts, axis, split_axis=0, concat_axis=0, tiled=True)  27.9 us
    dot_general x16, matrix products, dot(): lax.dot_general(a, b, (((ca,), (cb,)), ((), ())), preferred_element_type=...  27.1 us
    scatter x4, local copies, waits for them, and re-layouts, gathered(): own = own.at[k * NZ * OWN:(k + 1) * NZ * OWN, CA:].set(b2[k][:, :rest])  10.6 us
    broadcast_in_dim x4, local copies, waits for them, and re-layouts, from_everyone(): jnp.broadcast_to(value, (lax.axis_size(axis), *value.shape))  5.07 us
  transfers between devices with their start and end apart: 31, of which 19 were waited for; matrix products, arithmetic and copies ran while one was open for 30% of the time, Pallas kernels for 0%

profile of v1, /device:TPU:8, one launch (start us, length us, event | category | flops | bytes accessed | tf_op | source)
XLA Modules:
  0.0 237.0 jit_solution(11131088778846432239)
XLA Ops:
  3.0 2.7 %collective-permute-start.1 = (bf16[8,1408]{1,0:T(8,128)(2,1)S(1)}, bf16[8,1408]{1,0:T(8,128)(2,1)S(1)}, u32[]{:S(2)}, u32[]{:S(2)}) collective-permute-start(bf16[8,1408]{1,0:T(8,128)(2,1)S(1)} %slice.249), channel_id=1, source_target_pairs={{0,32},{16,48},{32,0},{48,16},{1,33},{17,49},{33,1},{49,17},{2,34}... | collective-permute-start | bytes 67592 | tf_op jit(solution)/shard_map/ppermute | solution.py:22
  10.2 8.5 %all-to-all-start = ((bf16[8,8,2816]{2,1,0:T(8,128)(2,1)}), bf16[8,8,2816]{2,1,0:T(8,128)(2,1)}, u32[]{:S(2)}, u32[]{:S(2)}) async-start(bf16[8,8,2816]{2,1,0:T(8,128)(2,1)} %broadcast_in_dim.83), calls=%async_computation | async-start | bytes 720896 | tf_op jit(solution)/shard_map/all_to_all | solution.py:30
  24.2 7.7 %all-to-all-done = bf16[8,8,2816]{2,1,0:T(8,128)(2,1)} async-done(((bf16[8,8,2816]{2,1,0:T(8,128)(2,1)}), bf16[8,8,2816]{2,1,0:T(8,128)(2,1)}, u32[]{:S(2)}, u32[]{:S(2)}) %all-to-all-start) | async-done | bytes 360480 | tf_op jit(solution)/shard_map/all_to_all | solution.py:30
  35.2 2.4 %slice_select_fusion.1 = bf16[64,2688]{1,0:T(8,128)(2,1)} fusion(bf16[64,2816]{1,0:T(8,128)(2,1)} %bitcast.4, pred[]{:T(512)} %and_reduce_fusion), kind=kLoop, calls=%fused_computation.50 | loop fusion | flops 172032 | bytes 688129 | tf_op jit(solution)/shard_map/select.5
  38.4 1.8 broadcast_in_dim.85
  40.2 4.2 %all-to-all-start.1 = ((bf16[8,32,1408]{2,1,0:T(8,128)(2,1)}), bf16[8,32,1408]{2,1,0:T(8,128)(2,1)}, u32[]{:S(2)}, u32[]{:S(2)}) async-start(bf16[8,32,1408]{2,1,0:T(8,128)(2,1)} %broadcast_in_dim.85), calls=%async_computation.1 | async-start | bytes 1441792 | tf_op jit(solution)/shard_map/all_to_all | solution.py:30
  45.9 5.4 %scatter.16 = bf16[256,4096]{1,0:T(8,128)(2,1)} dynamic-update-slice(bf16[256,4096]{1,0:T(8,128)(2,1)} %broadcast_in_dim.84, bf16[64,2688]{1,0:T(8,128)(2,1)} %slice_select_fusion.1, s32[]{:T(128)} %bitcast.13, s32[]{:T(128)} %bitcast.14) | dynamic-update-slice | bytes 688132 | tf_op jit(solution)/shard_map/scatter | solution.py:62
  53.8 1.7 slice_dynamic-update-slice_fusion.2
  55.6 1.7 slice_dynamic-update-slice_fusion.1
  57.3 1.7 slice_dynamic-update-slice_fusion
  59.0 4.3 %all-to-all-done.1 = bf16[8,32,1408]{2,1,0:T(8,128)(2,1)} async-done(((bf16[8,32,1408]{2,1,0:T(8,128)(2,1)}), bf16[8,32,1408]{2,1,0:T(8,128)(2,1)}, u32[]{:S(2)}, u32[]{:S(2)}) %all-to-all-start.1) | async-done | bytes 720928 | tf_op jit(solution)/shard_map/all_to_all | solution.py:30
  64.5 2.8 %fusion.23 = bf16[256,4096]{1,0:T(8,128)(2,1)} fusion(bf16[256,4096]{1,0:T(8,128)(2,1)} %slice_dynamic-update-slice_fusion, bf16[256,1408]{1,0:T(8,128)(2,1)S(1)} %bitcast.119, pred[]{:T(512)} %compare_reduce_fusion), kind=kLoop, calls=%fused_computation.33 | loop fusion | flops 360448 | bytes 2163200 | tf_op jit(solution)/shard_map/scatter | solution.py:63
  68.5 3.3 %collective-permute-done.6 = f32[2,4,64]{2,1,0:T(4,128)S(1)} collective-permute-done((f32[2,4,64]{2,1,0:T(4,128)S(1)}, f32[2,4,64]{2,1,0:T(4,128)S(1)}, u32[]{:S(2)}, u32[]{:S(2)}) %collective-permute-start.6) | collective-permute-done | bytes 2080 | tf_op jit(solution)/shard_map/ppermute | solution.py:22
  73.0 2.1 fusion.50
  77.0 2.5 %fusion.119 = f32[256,161]{0,1:T(8,128)S(1)} fusion(bf16[256,4096]{1,0:T(8,128)(2,1)} %collective-permute-done.7, bf16[4096,161]{0,1:T(8,128)(2,1)S(1)} %constant_dynamic-update-slice_fusion), kind=kOutput, calls=%fused_computation.221 | convolution fusion | flops 337641472 | bytes 3580928 | tf_op jit(solution)/shard_map/dot_general | solution.py:26
  80.4 1.7 broadcast_in_dim.92
  82.1 4.9 %all-to-all-start.3 = ((bf16[4,16,4096]{2,1,0:T(8,128)(2,1)}), bf16[4,16,4096]{2,1,0:T(8,128)(2,1)}, u32[]{:S(2)}, u32[]{:S(2)}) async-start(bf16[4,16,4096]{2,1,0:T(8,128)(2,1)} %broadcast_in_dim.92), calls=%async_computation.3 | async-start | bytes 1048576 | tf_op jit(solution)/shard_map/all_to_all | solution.py:30
  87.2 8.3 %all-to-all-done.3 = bf16[4,16,4096]{2,1,0:T(8,128)(2,1)} async-done(((bf16[4,16,4096]{2,1,0:T(8,128)(2,1)}), bf16[4,16,4096]{2,1,0:T(8,128)(2,1)}, u32[]{:S(2)}, u32[]{:S(2)}) %all-to-all-start.3) | async-done | bytes 524320 | tf_op jit(solution)/shard_map/all_to_all | solution.py:30
  96.2 6.6 %all-to-all-start.2 = ((f32[64,2,512]{2,1,0:T(2,128)}), f32[64,2,512]{2,1,0:T(2,128)}, u32[]{:S(2)}, u32[]{:S(2)}) async-start(f32[64,2,512]{2,1,0:T(2,128)} %broadcast_in_dim.88), calls=%async_computation.2 | async-start | bytes 524288 | tf_op jit(solution)/shard_map/all_to_all | solution.py:30
  105.3 2.9 %fusion.6 = f32[64,7680]{1,0:T(8,128)S(1)} fusion(bf16[64,256]{1,0:T(8,128)(2,1)S(1)} %fusion.15, bf16[1,256,7680]{2,1,0:T(8,128)(2,1)} %param.29), kind=kOutput, calls=%fused_computation.13 | convolution fusion | flops 251658240 | bytes 5931008 | tf_op jit(solution)/shard_map/dot_general | solution.py:26
  110.7 2.0 collective-permute-start.14
  114.5 2.0 fusion.113
  119.0 6.1 %collective-permute-done.12 = f32[16,7680]{1,0:T(8,128)} collective-permute-done((f32[16,7680]{1,0:T(8,128)}, f32[16,7680]{1,0:T(8,128)}, u32[]{:S(2)}, u32[]{:S(2)}) %collective-permute-start.12) | collective-permute-done | bytes 491552 | tf_op jit(solution)/shard_map/ppermute | solution.py:22
  125.1 10.9 %collective-permute-done.13 = f32[16,7680]{1,0:T(8,128)} collective-permute-done((f32[16,7680]{1,0:T(8,128)}, f32[16,7680]{1,0:T(8,128)}, u32[]{:S(2)}, u32[]{:S(2)}) %collective-permute-start.13) | collective-permute-done | bytes 491552 | tf_op jit(solution)/shard_map/ppermute | solution.py:22
  136.0 1.7 fusion.108
  138.3 3.2 %collective-permute-start.16 = (bf16[16,7680]{1,0:T(8,128)(2,1)S(1)}, bf16[16,7680]{1,0:T(8,128)(2,1)S(1)}, u32[]{:S(2)}, u32[]{:S(2)}) collective-permute-start(bf16[16,7680]{1,0:T(8,128)(2,1)S(1)} %multiply_convert_fusion), channel_id=1, source_target_pairs={{0,128},{64,192},{128,0},{192,64},{1,129},{65,193},{129,1},{193,65... | collective-permute-start | bytes 737288 | tf_op jit(solution)/shard_map/ppermute | solution.py:22
  141.5 2.3 collective-permute-start.15
  144.7 2.4 %collective-permute-done.17 = bf16[16,7680]{1,0:T(8,128)(2,1)S(1)} collective-permute-done((bf16[16,7680]{1,0:T(8,128)(2,1)S(1)}, bf16[16,7680]{1,0:T(8,128)(2,1)S(1)}, u32[]{:S(2)}, u32[]{:S(2)}) %collective-permute-start.17) | collective-permute-done | bytes 245792 | tf_op jit(solution)/shard_map/ppermute | solution.py:22
  147.1 1.6 collective-permute-done.16
  148.7 3.2 %collective-permute-done.15 = bf16[16,7680]{1,0:T(8,128)(2,1)S(1)} collective-permute-done((bf16[16,7680]{1,0:T(8,128)(2,1)S(1)}, bf16[16,7680]{1,0:T(8,128)(2,1)S(1)}, u32[]{:S(2)}, u32[]{:S(2)}) %collective-permute-start.15) | collective-permute-done | bytes 245792 | tf_op jit(solution)/shard_map/ppermute | solution.py:22
  156.2 2.3 collective-permute-start.19
  160.7 3.2 %collective-permute-done.19 = bf16[16,4096]{1,0:T(8,128)(2,1)S(1)} collective-permute-done((bf16[16,4096]{1,0:T(8,128)(2,1)S(1)}, bf16[16,4096]{1,0:T(8,128)(2,1)S(1)}, u32[]{:S(2)}, u32[]{:S(2)}) %collective-permute-start.19) | collective-permute-done | bytes 131104 | tf_op jit(solution)/shard_map/ppermute | solution.py:22
  164.0 2.3 collective-permute-start.23
  166.3 2.9 %collective-permute-start.22 = (bf16[16,4096]{1,0:T(8,128)(2,1)S(1)}, bf16[16,4096]{1,0:T(8,128)(2,1)S(1)}, u32[]{:S(2)}, u32[]{:S(2)}) collective-permute-start(bf16[16,4096]{1,0:T(8,128)(2,1)S(1)} %fusion.31), channel_id=1, source_target_pairs={{0,32},{16,48},{32,0},{48,16},{1,33},{17,49},{33,1},{49,17},{2,34}... | collective-permute-start | bytes 393224 | tf_op jit(solution)/shard_map/ppermute | solution.py:22
  170.6 2.1 fusion.39
  175.4 2.8 %fusion.117 = (bf16[256,4096]{1,0:T(8,128)(2,1)S(1)}, f32[256,4096]{1,0:T(8,128)}) fusion(bf16[256,4096]{1,0:T(8,128)(2,1)S(1)} %collective-permute-done.8, bf16[4096,161]{0,1:T(8,128)(2,1)S(1)} %constant_dynamic-update-slice_fusion, bf16[512,161]{0,1:T(8,128)(2,1)S(1)} %multiply_convert_fusion.1), kind=kOutput, calls=%fused_computation.219 | convolution fusion | flops 340787200 | bytes 9850880 | tf_op jit(solution)/shard_map/dot_general | solution.py:26
  180.3 2.3 collective-permute-start.11
  184.2 1.8 reshape.383
  186.1 2.8 %copy.99 = bf16[161,4,1024]{2,0,1:T(8,128)(2,1)} copy(bf16[161,4,1024]{2,1,0:T(4,128)(2,1)} %reshape.383) | data formatting | bytes 2637824 | tf_op jit(solution)/shard_map/reshape | solution.py:173
  188.9 5.0 %all-to-all-start.5 = ((bf16[4,161,1024]{2,1,0:T(8,128)(2,1)}), bf16[4,161,1024]{2,1,0:T(8,128)(2,1)S(1)}, u32[]{:S(2)}, u32[]{:S(2)}) async-start(bf16[4,161,1024]{2,1,0:T(8,128)(2,1)} %bitcast.116), calls=%async_computation.5 | async-start | bytes 2752512 | tf_op jit(solution)/shard_map/all_to_all | solution.py:30
  195.3 10.5 %collective-permute-done.11 = bf16[64,4096]{1,0:T(8,128)(2,1)} collective-permute-done((bf16[64,4096]{1,0:T(8,128)(2,1)}, bf16[64,4096]{1,0:T(8,128)(2,1)}, u32[]{:S(2)}, u32[]{:S(2)}) %collective-permute-start.11) | collective-permute-done | bytes 524320 | tf_op jit(solution)/shard_map/ppermute | solution.py:22
  207.3 3.0 %fusion.25 = bf16[8,8,4096]{2,1,0:T(8,128)(2,1)} fusion(bf16[64,4096]{1,0:T(8,128)(2,1)} %collective-permute-done.24, f32[64,4096]{1,0:T(8,128)S(1)} %fusion.38, bf16[64,4096]{1,0:T(8,128)(2,1)} %collective-permute-done.11, bf16[64,4096]{1,0:T(8,128)(2,1)} %collective-permute-done.10, bf16[64,4096]{1,0:T(8,128)(2,1)} %collective-permute-done.9, ...), kind=kLoop, calls=%fused_computation.35 | loop fusion | flops 2621440 | bytes 4718592 | tf_op jit(solution)/shard_map/convert_element_type | solution.py:169
  211.1 7.1 %all-to-all-start.4 = ((bf16[8,8,4096]{2,1,0:T(8,128)(2,1)}), bf16[8,8,4096]{2,1,0:T(8,128)(2,1)}, u32[]{:S(2)}, u32[]{:S(2)}) async-start(bf16[8,8,4096]{2,1,0:T(8,128)(2,1)} %fusion.25), calls=%async_computation.4 | async-start | bytes 1048576 | tf_op jit(solution)/shard_map/all_to_all | solution.py:30
  218.3 3.2 %fusion.1 = bf16[1,4096,256]{2,1,0:T(8,128)(2,1)} fusion(bf16[64,4096]{1,0:T(8,128)(2,1)} %bitcast.118, bf16[64,256]{1,0:T(8,128)(2,1)S(1)} %fusion.12), kind=kOutput, calls=%fused_computation.5 | convolution fusion | flops 135266304 | bytes 2654208 | tf_op jit(solution)/shard_map/dot_general | solution.py:26
  221.5 3.1 %fusion = bf16[1,256,7680]{2,1,0:T(8,128)(2,1)} fusion(bf16[64,256]{1,0:T(8,128)(2,1)S(1)} %fusion.15, bf16[16,7680]{1,0:T(8,128)(2,1)S(1)} %copy-done.12, bf16[16,7680]{1,0:T(8,128)(2,1)S(1)} %copy-done.14, bf16[16,7680]{1,0:T(8,128)(2,1)S(1)} %copy-done.16, bf16[16,7680]{1,0:T(8,128)(2,1)S(1)} %copy-done.9), kind=kOutput, calls=%fused_computation.1 | convolution fusion | flops 257556480 | bytes 4947968 | tf_op jit(solution)/shard_map/dot_general | solution.py:26
  227.0 1.7 slice_bitcast_fusion
  228.7 6.5 %all-to-all-done.4 = bf16[8,8,4096]{2,1,0:T(8,128)(2,1)} async-done(((bf16[8,8,4096]{2,1,0:T(8,128)(2,1)}), bf16[8,8,4096]{2,1,0:T(8,128)(2,1)}, u32[]{:S(2)}, u32[]{:S(2)}) %all-to-all-start.4) | async-done | bytes 524320 | tf_op jit(solution)/shard_map/all_to_all | solution.py:30
  235.2 1.8 reduce_sum.87
  (167 shorter events, 58.6 us)
Async XLA Ops:
  0.6 104.2 %copy-start = (bf16[1,4096,256]{2,1,0:T(8,128)(2,1)S(1)}, bf16[1,4096,256]{2,1,0:T(8,128)(2,1)}, u32[]{:S(2)}) copy-start(bf16[1,4096,256]{2,1,0:T(8,128)(2,1)} %param.28) | copy-start | bytes 6291460
  1.5 21.2 %collective-permute-start.2 = (bf16[8,1408]{1,0:T(8,128)(2,1)S(1)}, bf16[8,1408]{1,0:T(8,128)(2,1)S(1)}, u32[]{:S(2)}, u32[]{:S(2)}) collective-permute-start(bf16[8,1408]{1,0:T(8,128)(2,1)S(1)} %slice.249), channel_id=1, source_target_pairs={{0,16},{16,32},{32,48},{48,0},{1,17},{17,33},{33,49},{49,1},{2,18}... | collective-permute-start | bytes 67592 | tf_op jit(solution)/shard_map/ppermute | solution.py:22
  3.0 19.8 %collective-permute-start.1 = (bf16[8,1408]{1,0:T(8,128)(2,1)S(1)}, bf16[8,1408]{1,0:T(8,128)(2,1)S(1)}, u32[]{:S(2)}, u32[]{:S(2)}) collective-permute-start(bf16[8,1408]{1,0:T(8,128)(2,1)S(1)} %slice.249), channel_id=1, source_target_pairs={{0,32},{16,48},{32,0},{48,16},{1,33},{17,49},{33,1},{49,17},{2,34}... | collective-permute-start | bytes 67592 | tf_op jit(solution)/shard_map/ppermute | solution.py:22
  5.8 17.0 %collective-permute-start = (bf16[8,1408]{1,0:T(8,128)(2,1)S(1)}, bf16[8,1408]{1,0:T(8,128)(2,1)}, u32[]{:S(2)}, u32[]{:S(2)}) collective-permute-start(bf16[8,1408]{1,0:T(8,128)(2,1)S(1)} %slice.249), channel_id=1, source_target_pairs={{0,48},{16,0},{32,16},{48,32},{1,49},{17,1},{33,17},{49,33},{2,50}... | collective-permute-start | bytes 67592 | tf_op jit(solution)/shard_map/ppermute | solution.py:22
  10.2 21.7 %all-to-all-start = ((bf16[8,8,2816]{2,1,0:T(8,128)(2,1)}), bf16[8,8,2816]{2,1,0:T(8,128)(2,1)}, u32[]{:S(2)}, u32[]{:S(2)}) async-start(bf16[8,8,2816]{2,1,0:T(8,128)(2,1)} %broadcast_in_dim.83), calls=%async_computation | async-start | bytes 720896 | tf_op jit(solution)/shard_map/all_to_all | solution.py:30
  18.7 3.3 %copy-start.20 = (bf16[4096,1]{0,1:T(2,128)(2,1)S(1)}, bf16[4096,1]{0,1:T(2,128)(2,1)}, u32[]{:S(2)}) copy-start(bf16[4096,1]{0,1:T(2,128)(2,1)} %param.27) | copy-start | bytes 24580
  31.9 19.5 %collective-permute-start.5 = (bf16[64,2816]{1,0:T(8,128)(2,1)}, bf16[64,2816]{1,0:T(8,128)(2,1)}, u32[]{:S(2)}, u32[]{:S(2)}) collective-permute-start(bf16[64,2816]{1,0:T(8,128)(2,1)} %bitcast.4), channel_id=1, source_target_pairs={{0,16},{16,32},{32,48},{48,0},{1,17},{17,33},{33,49},{49,1},{2,18}... | collective-permute-start | bytes 1081352 | tf_op jit(solution)/shard_map/ppermute | solution.py:22
  32.5 19.7 %collective-permute-start.4 = (bf16[64,2816]{1,0:T(8,128)(2,1)}, bf16[64,2816]{1,0:T(8,128)(2,1)}, u32[]{:S(2)}, u32[]{:S(2)}) collective-permute-start(bf16[64,2816]{1,0:T(8,128)(2,1)} %bitcast.4), channel_id=1, source_target_pairs={{0,32},{16,48},{32,0},{48,16},{1,33},{17,49},{33,1},{49,17},{2,34}... | collective-permute-start | bytes 1081352 | tf_op jit(solution)/shard_map/ppermute | solution.py:22
  33.6 19.4 %collective-permute-start.3 = (bf16[64,2816]{1,0:T(8,128)(2,1)}, bf16[64,2816]{1,0:T(8,128)(2,1)}, u32[]{:S(2)}, u32[]{:S(2)}) collective-permute-start(bf16[64,2816]{1,0:T(8,128)(2,1)} %bitcast.4), channel_id=1, source_target_pairs={{0,48},{16,0},{32,16},{48,32},{1,49},{17,1},{33,17},{49,33},{2,50}... | collective-permute-start | bytes 1081352 | tf_op jit(solution)/shard_map/ppermute | solution.py:22
  40.2 23.2 %all-to-all-start.1 = ((bf16[8,32,1408]{2,1,0:T(8,128)(2,1)}), bf16[8,32,1408]{2,1,0:T(8,128)(2,1)}, u32[]{:S(2)}, u32[]{:S(2)}) async-start(bf16[8,32,1408]{2,1,0:T(8,128)(2,1)} %broadcast_in_dim.85), calls=%async_computation.1 | async-start | bytes 1441792 | tf_op jit(solution)/shard_map/all_to_all | solution.py:30
  67.3 5.7 %collective-permute-start.7 = (bf16[256,4096]{1,0:T(8,128)(2,1)}, bf16[256,4096]{1,0:T(8,128)(2,1)}, u32[]{:S(2)}, u32[]{:S(2)}) collective-permute-start(bf16[256,4096]{1,0:T(8,128)(2,1)} %fusion.23), channel_id=1, source_target_pairs={{0,1},{1,0},{2,3},{3,2},{4,5},{5,4},{6,7},{7,6},{8,9},{9,8},{10,11... | collective-permute-start | bytes 6291464 | tf_op jit(solution)/shard_map/ppermute | solution.py:22
  67.3 4.5 %collective-permute-start.6 = (f32[2,4,64]{2,1,0:T(4,128)S(1)}, f32[2,4,64]{2,1,0:T(4,128)S(1)}, u32[]{:S(2)}, u32[]{:S(2)}) collective-permute-start(f32[2,4,64]{2,1,0:T(4,128)S(1)} %get-tuple-element.122), channel_id=1, source_target_pairs={{0,1},{1,0},{2,3},{3,2},{4,5},{5,4},{6,7},{7,6},{8,9},{9,8},{10,11... | collective-permute-start | bytes 6152 | tf_op jit(solution)/shard_map/ppermute | solution.py:22
  72.5 2.6 %copy-start.1 = (bf16[256,4096]{1,0:T(8,128)(2,1)S(1)}, bf16[256,4096]{1,0:T(8,128)(2,1)}, u32[]{:S(2)}) copy-start(bf16[256,4096]{1,0:T(8,128)(2,1)} %fusion.23) | copy-start | bytes 6291460
  77.0 2.6 %copy-start.6 = (f32[256,161]{0,1:T(8,128)}, f32[256,161]{0,1:T(8,128)S(1)}, u32[]{:S(2)}) copy-start(f32[256,161]{0,1:T(8,128)S(1)} %fusion.118) | copy-start | bytes 494596
  82.1 13.3 %all-to-all-start.3 = ((bf16[4,16,4096]{2,1,0:T(8,128)(2,1)}), bf16[4,16,4096]{2,1,0:T(8,128)(2,1)}, u32[]{:S(2)}, u32[]{:S(2)}) async-start(bf16[4,16,4096]{2,1,0:T(8,128)(2,1)} %broadcast_in_dim.92), calls=%async_computation.3 | async-start | bytes 1048576 | tf_op jit(solution)/shard_map/all_to_all | solution.py:30
  96.2 18.2 %all-to-all-start.2 = ((f32[64,2,512]{2,1,0:T(2,128)}), f32[64,2,512]{2,1,0:T(2,128)}, u32[]{:S(2)}, u32[]{:S(2)}) async-start(f32[64,2,512]{2,1,0:T(2,128)} %broadcast_in_dim.88), calls=%async_computation.2 | async-start | bytes 524288 | tf_op jit(solution)/shard_map/all_to_all | solution.py:30
  110.7 14.4 %collective-permute-start.12 = (f32[16,7680]{1,0:T(8,128)}, f32[16,7680]{1,0:T(8,128)}, u32[]{:S(2)}, u32[]{:S(2)}) collective-permute-start(f32[16,7680]{1,0:T(8,128)} %get-tuple-element.108), channel_id=1, source_target_pairs={{0,64},{64,128},{128,192},{192,0},{1,65},{65,129},{129,193},{193,1... | collective-permute-start | bytes 1474568 | tf_op jit(solution)/shard_map/ppermute | solution.py:22
  110.7 14.4 %collective-permute-start.14 = (f32[16,7680]{1,0:T(8,128)}, f32[16,7680]{1,0:T(8,128)}, u32[]{:S(2)}, u32[]{:S(2)}) collective-permute-start(f32[16,7680]{1,0:T(8,128)} %get-tuple-element.109), channel_id=1, source_target_pairs={{0,192},{64,0},{128,64},{192,128},{1,193},{65,1},{129,65},{193,129... | collective-permute-start | bytes 1474568 | tf_op jit(solution)/shard_map/ppermute | solution.py:22
  112.7 23.3 %collective-permute-start.13 = (f32[16,7680]{1,0:T(8,128)}, f32[16,7680]{1,0:T(8,128)}, u32[]{:S(2)}, u32[]{:S(2)}) collective-permute-start(f32[16,7680]{1,0:T(8,128)} %get-tuple-element.110), channel_id=1, source_target_pairs={{0,128},{64,192},{128,0},{192,64},{1,129},{65,193},{129,1},{193,65... | collective-permute-start | bytes 1474568 | tf_op jit(solution)/shard_map/ppermute | solution.py:22
  138.0 14.0 %copy-start.5 = (bf16[1,256,7680]{2,1,0:T(8,128)(2,1)S(1)}, bf16[1,256,7680]{2,1,0:T(8,128)(2,1)}, u32[]{:S(2)}) copy-start(bf16[1,256,7680]{2,1,0:T(8,128)(2,1)} %param.29) | copy-start | bytes 11796484
  138.2 15.1 %copy-start.8 = (bf16[16,7680]{1,0:T(8,128)(2,1)}, bf16[16,7680]{1,0:T(8,128)(2,1)S(1)}, u32[]{:S(2)}) copy-start(bf16[16,7680]{1,0:T(8,128)(2,1)S(1)} %multiply_convert_fusion) | copy-start | bytes 737284
  138.2 8.9 %collective-permute-start.17 = (bf16[16,7680]{1,0:T(8,128)(2,1)S(1)}, bf16[16,7680]{1,0:T(8,128)(2,1)S(1)}, u32[]{:S(2)}, u32[]{:S(2)}) collective-permute-start(bf16[16,7680]{1,0:T(8,128)(2,1)S(1)} %multiply_convert_fusion), channel_id=1, source_target_pairs={{0,64},{64,128},{128,192},{192,0},{1,65},{65,129},{129,193},{193,1... | collective-permute-start | bytes 737288 | tf_op jit(solution)/shard_map/ppermute | solution.py:22
  138.3 10.5 %collective-permute-start.16 = (bf16[16,7680]{1,0:T(8,128)(2,1)S(1)}, bf16[16,7680]{1,0:T(8,128)(2,1)S(1)}, u32[]{:S(2)}, u32[]{:S(2)}) collective-permute-start(bf16[16,7680]{1,0:T(8,128)(2,1)S(1)} %multiply_convert_fusion), channel_id=1, source_target_pairs={{0,128},{64,192},{128,0},{192,64},{1,129},{65,193},{129,1},{193,65... | collective-permute-start | bytes 737288 | tf_op jit(solution)/shard_map/ppermute | solution.py:22
  141.5 10.4 %collective-permute-start.15 = (bf16[16,7680]{1,0:T(8,128)(2,1)S(1)}, bf16[16,7680]{1,0:T(8,128)(2,1)S(1)}, u32[]{:S(2)}, u32[]{:S(2)}) collective-permute-start(bf16[16,7680]{1,0:T(8,128)(2,1)S(1)} %multiply_convert_fusion), channel_id=1, source_target_pairs={{0,192},{64,0},{128,64},{192,128},{1,193},{65,1},{129,65},{193,129... | collective-permute-start | bytes 737288 | tf_op jit(solution)/shard_map/ppermute | solution.py:22
  144.6 30.8 %collective-permute-start.8 = (bf16[256,4096]{1,0:T(8,128)(2,1)S(1)}, bf16[256,4096]{1,0:T(8,128)(2,1)S(1)}, u32[]{:S(2)}, u32[]{:S(2)}) collective-permute-start(bf16[256,4096]{1,0:T(8,128)(2,1)S(1)} %convolution_convert_fusion.2), channel_id=1, source_target_pairs={{0,1},{1,0},{2,3},{3,2},{4,5},{5,4},{6,7},{7,6},{8,9},{9,8},{10,11... | collective-permute-start | bytes 6291464 | tf_op jit(solution)/shard_map/ppermute | solution.py:22
  147.1 6.2 %copy-start.11 = (bf16[16,7680]{1,0:T(8,128)(2,1)}, bf16[16,7680]{1,0:T(8,128)(2,1)S(1)}, u32[]{:S(2)}) copy-start(bf16[16,7680]{1,0:T(8,128)(2,1)S(1)} %collective-permute-done.17) | copy-start | bytes 737284
  148.7 4.5 %copy-start.13 = (bf16[16,7680]{1,0:T(8,128)(2,1)}, bf16[16,7680]{1,0:T(8,128)(2,1)S(1)}, u32[]{:S(2)}) copy-start(bf16[16,7680]{1,0:T(8,128)(2,1)S(1)} %collective-permute-done.16) | copy-start | bytes 737284
  153.3 5.2 %copy-start.21 = (s32[64]{0:T(128)S(1)}, s32[64]{0:T(128)}, u32[]{:S(2)}) copy-start(s32[64]{0:T(128)} %add.293) | copy-start | bytes 772
  154.1 6.0 %collective-permute-start.18 = (bf16[16,4096]{1,0:T(8,128)(2,1)S(1)}, bf16[16,4096]{1,0:T(8,128)(2,1)S(1)}, u32[]{:S(2)}, u32[]{:S(2)}) collective-permute-start(bf16[16,4096]{1,0:T(8,128)(2,1)S(1)} %get-tuple-element.111), channel_id=1, source_target_pairs={{0,64},{64,128},{128,192},{192,0},{1,65},{65,129},{129,193},{193,1... | collective-permute-start | bytes 393224 | tf_op jit(solution)/shard_map/ppermute | solution.py:22
  154.8 5.9 %collective-permute-start.20 = (bf16[16,4096]{1,0:T(8,128)(2,1)S(1)}, bf16[16,4096]{1,0:T(8,128)(2,1)S(1)}, u32[]{:S(2)}, u32[]{:S(2)}) collective-permute-start(bf16[16,4096]{1,0:T(8,128)(2,1)S(1)} %get-tuple-element.112), channel_id=1, source_target_pairs={{0,192},{64,0},{128,64},{192,128},{1,193},{65,1},{129,65},{193,129... | collective-permute-start | bytes 393224 | tf_op jit(solution)/shard_map/ppermute | solution.py:22
  156.2 7.7 %collective-permute-start.19 = (bf16[16,4096]{1,0:T(8,128)(2,1)S(1)}, bf16[16,4096]{1,0:T(8,128)(2,1)S(1)}, u32[]{:S(2)}, u32[]{:S(2)}) collective-permute-start(bf16[16,4096]{1,0:T(8,128)(2,1)S(1)} %get-tuple-element.113), channel_id=1, source_target_pairs={{0,128},{64,192},{128,0},{192,64},{1,129},{65,193},{129,1},{193,65... | collective-permute-start | bytes 393224 | tf_op jit(solution)/shard_map/ppermute | solution.py:22
  164.0 10.2 %copy-start.10 = (bf16[16,4096]{1,0:T(8,128)(2,1)}, bf16[16,4096]{1,0:T(8,128)(2,1)S(1)}, u32[]{:S(2)}) copy-start(bf16[16,4096]{1,0:T(8,128)(2,1)S(1)} %fusion.31) | copy-start | bytes 393220
  164.0 8.7 %collective-permute-start.23 = (bf16[16,4096]{1,0:T(8,128)(2,1)S(1)}, bf16[16,4096]{1,0:T(8,128)(2,1)S(1)}, u32[]{:S(2)}, u32[]{:S(2)}) collective-permute-start(bf16[16,4096]{1,0:T(8,128)(2,1)S(1)} %fusion.31), channel_id=1, source_target_pairs={{0,16},{16,32},{32,48},{48,0},{1,17},{17,33},{33,49},{49,1},{2,18}... | collective-permute-start | bytes 393224 | tf_op jit(solution)/shard_map/ppermute | solution.py:22
  166.3 7.5 %collective-permute-start.22 = (bf16[16,4096]{1,0:T(8,128)(2,1)S(1)}, bf16[16,4096]{1,0:T(8,128)(2,1)S(1)}, u32[]{:S(2)}, u32[]{:S(2)}) collective-permute-start(bf16[16,4096]{1,0:T(8,128)(2,1)S(1)} %fusion.31), channel_id=1, source_target_pairs={{0,32},{16,48},{32,0},{48,16},{1,33},{17,49},{33,1},{49,17},{2,34}... | collective-permute-start | bytes 393224 | tf_op jit(solution)/shard_map/ppermute | solution.py:22
  169.2 5.0 %collective-permute-start.21 = (bf16[16,4096]{1,0:T(8,128)(2,1)S(1)}, bf16[16,4096]{1,0:T(8,128)(2,1)S(1)}, u32[]{:S(2)}, u32[]{:S(2)}) collective-permute-start(bf16[16,4096]{1,0:T(8,128)(2,1)S(1)} %fusion.31), channel_id=1, source_target_pairs={{0,48},{16,0},{32,16},{48,32},{1,49},{17,1},{33,17},{49,33},{2,50}... | collective-permute-start | bytes 393224 | tf_op jit(solution)/shard_map/ppermute | solution.py:22
  172.7 2.7 %copy-start.17 = (bf16[16,4096]{1,0:T(8,128)(2,1)}, bf16[16,4096]{1,0:T(8,128)(2,1)S(1)}, u32[]{:S(2)}) copy-start(bf16[16,4096]{1,0:T(8,128)(2,1)S(1)} %collective-permute-done.23) | copy-start | bytes 393220
  173.8 1.6 copy-start.18
  175.4 19.9 %collective-permute-start.24 = (bf16[64,4096]{1,0:T(8,128)(2,1)}, bf16[64,4096]{1,0:T(8,128)(2,1)}, u32[]{:S(2)}, u32[]{:S(2)}) collective-permute-start(bf16[64,4096]{1,0:T(8,128)(2,1)} %convolution_convert_fusion.3), channel_id=1, source_target_pairs={{0,1},{1,0},{2,3},{3,2},{4,5},{5,4},{6,7},{7,6},{8,9},{9,8},{10,11... | collective-permute-start | bytes 1572872 | tf_op jit(solution)/shard_map/ppermute | solution.py:22
  178.2 5.5 %copy-start.2 = (bf16[256,4096]{1,0:T(8,128)(2,1)S(1)}, bf16[256,4096]{1,0:T(8,128)(2,1)}, u32[]{:S(2)}) copy-start(bf16[256,4096]{1,0:T(8,128)(2,1)} %fusion.23) | copy-start | bytes 6291460
  179.4 15.9 %collective-permute-start.9 = (bf16[64,4096]{1,0:T(8,128)(2,1)}, bf16[64,4096]{1,0:T(8,128)(2,1)}, u32[]{:S(2)}, u32[]{:S(2)}) collective-permute-start(bf16[64,4096]{1,0:T(8,128)(2,1)} %get-tuple-element.105), channel_id=1, source_target_pairs={{0,16},{16,32},{32,48},{48,0},{1,17},{17,33},{33,49},{49,1},{2,18}... | collective-permute-start | bytes 1572872 | tf_op jit(solution)/shard_map/ppermute | solution.py:22
  180.3 25.5 %collective-permute-start.11 = (bf16[64,4096]{1,0:T(8,128)(2,1)}, bf16[64,4096]{1,0:T(8,128)(2,1)}, u32[]{:S(2)}, u32[]{:S(2)}) collective-permute-start(bf16[64,4096]{1,0:T(8,128)(2,1)} %get-tuple-element.106), channel_id=1, source_target_pairs={{0,48},{16,0},{32,16},{48,32},{1,49},{17,1},{33,17},{49,33},{2,50}... | collective-permute-start | bytes 1572872 | tf_op jit(solution)/shard_map/ppermute | solution.py:22
  182.6 24.6 %collective-permute-start.10 = (bf16[64,4096]{1,0:T(8,128)(2,1)}, bf16[64,4096]{1,0:T(8,128)(2,1)}, u32[]{:S(2)}, u32[]{:S(2)}) collective-permute-start(bf16[64,4096]{1,0:T(8,128)(2,1)} %get-tuple-element.107), channel_id=1, source_target_pairs={{0,32},{16,48},{32,0},{48,16},{1,33},{17,49},{33,1},{49,17},{2,34}... | collective-permute-start | bytes 1572872 | tf_op jit(solution)/shard_map/ppermute | solution.py:22
  188.9 22.3 %all-to-all-start.5 = ((bf16[4,161,1024]{2,1,0:T(8,128)(2,1)}), bf16[4,161,1024]{2,1,0:T(8,128)(2,1)S(1)}, u32[]{:S(2)}, u32[]{:S(2)}) async-start(bf16[4,161,1024]{2,1,0:T(8,128)(2,1)} %bitcast.116), calls=%async_computation.5 | async-start | bytes 2752512 | tf_op jit(solution)/shard_map/all_to_all | solution.py:30
  211.1 24.1 %all-to-all-start.4 = ((bf16[8,8,4096]{2,1,0:T(8,128)(2,1)}), bf16[8,8,4096]{2,1,0:T(8,128)(2,1)}, u32[]{:S(2)}, u32[]{:S(2)}) async-start(bf16[8,8,4096]{2,1,0:T(8,128)(2,1)} %fusion.25), calls=%async_computation.4 | async-start | bytes 1048576 | tf_op jit(solution)/shard_map/all_to_all | solution.py:30
  218.2 3.2 %copy-start.9 = (bf16[16,7680]{1,0:T(8,128)(2,1)S(1)}, bf16[16,7680]{1,0:T(8,128)(2,1)}, u32[]{:S(2)}) copy-start(bf16[16,7680]{1,0:T(8,128)(2,1)} %copy-done.8) | copy-start | bytes 737284
  218.2 3.2 %copy-start.12 = (bf16[16,7680]{1,0:T(8,128)(2,1)S(1)}, bf16[16,7680]{1,0:T(8,128)(2,1)}, u32[]{:S(2)}) copy-start(bf16[16,7680]{1,0:T(8,128)(2,1)} %copy-done.11) | copy-start | bytes 737284
  218.2 3.2 %copy-start.14 = (bf16[16,7680]{1,0:T(8,128)(2,1)S(1)}, bf16[16,7680]{1,0:T(8,128)(2,1)}, u32[]{:S(2)}) copy-start(bf16[16,7680]{1,0:T(8,128)(2,1)} %copy-done.13) | copy-start | bytes 737284
  218.3 3.2 %copy-start.16 = (bf16[16,7680]{1,0:T(8,128)(2,1)S(1)}, bf16[16,7680]{1,0:T(8,128)(2,1)}, u32[]{:S(2)}) copy-start(bf16[16,7680]{1,0:T(8,128)(2,1)} %copy-done.15) | copy-start | bytes 737284
  (5 other events, 5.3 us)

commit v2 on v1

--- a/solution.py
+++ b/solution.py
@@ -57,10 +57,8 @@
     target = digits[..., 0] * 65536.0 + digits[..., 1] * 256.0 + digits[..., 2]
     meta = jnp.stack([target, digits[..., 3]])
     meta = jnp.stack([meta, shift(meta, "core", 1)], axis=1)
-    own = jnp.zeros((NX * NZ * OWN, model), BF16)
-    for k in range(NX):
-        own = own.at[k * NZ * OWN : (k + 1) * NZ * OWN, CA:].set(b2[k][:, :rest])
-    own = own.at[:, :CA].set(jnp.swapaxes(a2, 0, 1).reshape(-1, CA))
+    a2 = jnp.swapaxes(a2, 0, 1).reshape(-1, CA)
+    own = jnp.concatenate([a2, jnp.concatenate(b2, axis=0)[:, :rest]], axis=1)
     other = shift(own, "core", 1)
     return own, other, meta.reshape(2, -1)
 
@@ -85,6 +83,7 @@
 def step(hidden, targets, loss_weight, head_weight, cluster_weight, tail_proj, tail_out):
     x_index, z_index, core_index = (lax.axis_index(a) for a in ("x", "z", "core"))
     vocab_index = lax.axis_index(("x", "z", "core"))
+    dp_index = lax.axis_index("dp")
     model, width = head_weight.shape
     weight = jnp.concatenate([head_weight, cluster_weight], axis=1)
     own, other, meta = gathered(hidden, targets, loss_weight)
@@ -108,28 +107,29 @@
     select = holds.astype(BF16)
     picked = (dot(select[:, :side], own) + dot(select[:, side:], other)).astype(BF16)
     rows = from_everyone(picked, "dp")
-    rows = lax.dynamic_slice_in_dim(jnp.concatenate([rows] * 2), lax.axis_index("dp"), NDP)
     rows = rows.reshape(NDP * CAP, -1)
     proj = tail_proj[0]
     out = tail_out[0]
     reduced = dot(rows, proj).astype(BF16)
     partial = dot(reduced, out)
-    share = partial[:CAP]
+
+    def block(value, k, size, dim):
+        return lax.dynamic_slice_in_dim(value, lax.rem(dp_index + k, NDP) * size, size, dim)
+
+    share = block(partial, 0, CAP, 0)
     for k in range(1, NDP):
-        share = share + shift(partial[k * CAP : (k + 1) * CAP], "dp", k)
+        share = share + shift(block(partial, k, CAP, 0), "dp", k)
     top = jnp.max(share, axis=1, keepdims=True)
     share_exp = jnp.exp(share - top)
     total = jnp.sum(share_exp, axis=1, keepdims=True)
     hot = (jnp.arange(CV, dtype=jnp.int32)[None, :] == words[:, None]).astype(F32)
     share_delta = (gain_tail[:, None] * (share_exp / total - hot)).astype(BF16)
-    word_delta = jnp.concatenate(
-        [share_delta] + [shift(share_delta, "dp", -k) for k in range(1, NDP)], axis=0
-    )
+    word_delta = from_everyone(share_delta, "dp").reshape(NDP * CAP, -1)
     reduced_grad = dot(word_delta, out, 1, 1).astype(BF16)
     tail_partial = dot(reduced_grad, proj, 1, 1)
-    tail_sum = tail_partial[:CAP]
+    tail_sum = block(tail_partial, 0, CAP, 0)
     for k in range(1, NDP):
-        piece = tail_partial[k * CAP : (k + 1) * CAP].astype(BF16)
+        piece = block(tail_partial, k, CAP, 0).astype(BF16)
         tail_sum = tail_sum + shift(piece, "dp", k).astype(F32)
     tail_sum = tail_sum.astype(BF16)
 
@@ -170,9 +170,11 @@
     hidden_grad = jnp.sum(last.astype(F32), axis=0).astype(BF16)
 
     grad_t = (dot(near, own, 0, 0) + dot(far, other, 0, 0)).astype(BF16)
-    grad_t = jnp.moveaxis(grad_t.reshape(width + 1, NDP, -1), 1, 0)
-    grad_t = swapped(grad_t, "dp")
-    head_sum = jnp.sum(grad_t.astype(F32), axis=0).astype(BF16)
+    pieces = [block(grad_t, k, model // NDP, 1) for k in range(NDP)]
+    head_sum = pieces[0].astype(F32)
+    for k in range(1, NDP):
+        head_sum = head_sum + shift(pieces[k], "dp", k).astype(F32)
+    head_sum = head_sum.astype(BF16)
     out_grad = dot(reduced, word_delta, 0, 0).astype(BF16)
     proj_grad = dot(rows, reduced_grad, 0, 0).astype(BF16)
     return (

time: 239 us -> 241 us (level)
  waiting for transfers between devices: 74.1 us -> 93 us
  local copies, waits for them, and re-layouts: 39.8 us -> 21 us
  matrix products: 27.1 us -> 35.3 us
  other arithmetic: 24.4 us -> 18 us
    scatter x4 -> x0, local copies, waits for them, and re-layouts: 10.6 us -> none  [gathered(): own = own.at[k * NZ * OWN:(k + 1) * NZ * OWN, CA:].set(b2[k][:, :rest])]
    ppermute x25, waiting for transfers between devices: 46.3 us -> 56.3 us  [shift(): return lax.ppermute(value, axis, [(j, (j + step) % n) for j in range(n)])]
    all_to_all x6, waiting for transfers between devices: 27.9 us -> 36.7 us  [swapped(): return lax.all_to_all(parts, axis, split_axis=0, concat_axis=0, tiled=True)]
    dot_general x16, matrix products: 27.1 us -> 35.3 us  [dot(): lax.dot_general(a, b, (((ca,), (cb,)), ((), ())), preferred_element_type=...]
    reshape x2 -> x0, local copies, waits for them, and re-layouts: 4.61 us -> none  [step(): grad_t = jnp.moveaxis(grad_t.reshape(width + 1, NDP, -1), 1, 0)]
    another operation x4 -> x0, other arithmetic: 4.34 us -> none
    ppermute x25, starting transfers between devices: 34.1 us -> 30 us  [shift(): return lax.ppermute(value, axis, [(j, (j + step) % n) for j in range(n)])]
    all_to_all x6, starting transfers between devices: 36.3 us -> 39.1 us  [swapped(): return lax.all_to_all(parts, axis, split_axis=0, concat_axis=0, tiled=True)]
  transfers between devices with their start and end apart: 31 -> 31, of which waited for: 19 -> 22; matrix products, arithmetic and copies ran while one was open for 30% -> 20% of each run, Pallas kernels for 0% -> 0%
where the time goes in v2:
time: 241 us; the launch traced here: 237 us
  waiting for transfers between devices  93 us (39%)
  starting transfers between devices  69.1 us (29%)
  matrix products  35.3 us (15%)
  local copies, waits for them, and re-layouts  21 us (9%)
  other arithmetic  18 us (7%)
    ppermute x25, waiting for transfers between devices, shift(): return lax.ppermute(value, axis, [(j, (j + step) % n) for j in range(n)])  56.3 us
    all_to_all x6, starting transfers between devices, swapped(): return lax.all_to_all(parts, axis, split_axis=0, concat_axis=0, tiled=True)  39.1 us
    all_to_all x6, waiting for transfers between devices, swapped(): return lax.all_to_all(parts, axis, split_axis=0, concat_axis=0, tiled=True)  36.7 us
    dot_general x16, matrix products, dot(): lax.dot_general(a, b, (((ca,), (cb,)), ((), ())), preferred_element_type=...  35.3 us
    ppermute x25, starting transfers between devices, shift(): return lax.ppermute(value, axis, [(j, (j + step) % n) for j in range(n)])  30 us
    broadcast_in_dim x5, local copies, waits for them, and re-layouts, from_everyone(): jnp.broadcast_to(value, (lax.axis_size(axis), *value.shape))  6.11 us
  transfers between devices with their start and end apart: 31, of which 22 were waited for; matrix products, arithmetic and copies ran while one was open for 20% of the time, Pallas kernels for 0%

profile of v2, /device:TPU:8, one launch (start us, length us, event | category | flops | bytes accessed | tf_op | source)
XLA Modules:
  0.0 237.4 jit_solution(1917109853210942901)
XLA Ops:
  1.5 2.8 %collective-permute-start = (bf16[8,1408]{1,0:T(8,128)(2,1)S(1)}, bf16[8,1408]{1,0:T(8,128)(2,1)S(1)}, u32[]{:S(2)}, u32[]{:S(2)}) collective-permute-start(bf16[8,1408]{1,0:T(8,128)(2,1)S(1)} %slice.99), channel_id=1, source_target_pairs={{0,48},{16,0},{32,16},{48,32},{1,49},{17,1},{33,17},{49,33},{2,50}... | collective-permute-start | bytes 67592 | tf_op jit(solution)/shard_map/ppermute | solution.py:22
  9.0 8.5 %all-to-all-start = ((bf16[8,8,2816]{2,1,0:T(8,128)(2,1)}), bf16[8,8,2816]{2,1,0:T(8,128)(2,1)}, u32[]{:S(2)}, u32[]{:S(2)}) async-start(bf16[8,8,2816]{2,1,0:T(8,128)(2,1)} %broadcast_in_dim.83), calls=%async_computation | async-start | bytes 720896 | tf_op jit(solution)/shard_map/all_to_all | solution.py:30
  20.3 10.3 %all-to-all-done = bf16[8,8,2816]{2,1,0:T(8,128)(2,1)} async-done(((bf16[8,8,2816]{2,1,0:T(8,128)(2,1)}), bf16[8,8,2816]{2,1,0:T(8,128)(2,1)}, u32[]{:S(2)}, u32[]{:S(2)}) %all-to-all-start) | async-done | bytes 360480 | tf_op jit(solution)/shard_map/all_to_all | solution.py:30
  30.7 1.8 broadcast_in_dim.84
  32.5 4.2 %all-to-all-start.1 = ((bf16[8,32,1408]{2,1,0:T(8,128)(2,1)}), bf16[8,32,1408]{2,1,0:T(8,128)(2,1)}, u32[]{:S(2)}, u32[]{:S(2)}) async-start(bf16[8,32,1408]{2,1,0:T(8,128)(2,1)} %broadcast_in_dim.84), calls=%async_computation.1 | async-start | bytes 1441792 | tf_op jit(solution)/shard_map/all_to_all | solution.py:30
  36.8 1.8 collective-permute-start.5
  41.8 7.2 %collective-permute-done.5 = bf16[64,2816]{1,0:T(8,128)(2,1)} collective-permute-done((bf16[64,2816]{1,0:T(8,128)(2,1)}, bf16[64,2816]{1,0:T(8,128)(2,1)}, u32[]{:S(2)}, u32[]{:S(2)}) %collective-permute-start.5) | collective-permute-done | bytes 360480 | tf_op jit(solution)/shard_map/ppermute | solution.py:22
  51.0 3.3 %collective-permute-done.4 = bf16[64,2816]{1,0:T(8,128)(2,1)} collective-permute-done((bf16[64,2816]{1,0:T(8,128)(2,1)}, bf16[64,2816]{1,0:T(8,128)(2,1)}, u32[]{:S(2)}, u32[]{:S(2)}) %collective-permute-start.4) | collective-permute-done | bytes 360480 | tf_op jit(solution)/shard_map/ppermute | solution.py:22
  57.4 3.3 %fusion.8 = bf16[256,4096]{1,0:T(8,128)(2,1)} fusion(bf16[64,2816]{1,0:T(8,128)(2,1)} %collective-permute-done.5, bf16[64,2816]{1,0:T(8,128)(2,1)} %collective-permute-done.4, bf16[64,2816]{1,0:T(8,128)(2,1)} %collective-permute-done.3, bf16[64,2816]{1,0:T(8,128)(2,1)} %bitcast.4, bf16[256,1408]{1,0:T(8,128)(2,1)S(1)} %bitcast.112), kind=kLoop, calls=%fused_computation.16 | loop fusion | flops 10485760 | bytes 4259840 | tf_op jit(solution)/shard_map/concatenate | solution.py:61
  61.4 3.8 %collective-permute-done.6 = f32[2,4,64]{2,1,0:T(4,128)S(1)} collective-permute-done((f32[2,4,64]{2,1,0:T(4,128)S(1)}, f32[2,4,64]{2,1,0:T(4,128)S(1)}, u32[]{:S(2)}, u32[]{:S(2)}) %collective-permute-start.6) | collective-permute-done | bytes 2080 | tf_op jit(solution)/shard_map/ppermute | solution.py:22
  66.4 2.0 fusion.44
  68.4 2.6 %fusion.3 = bf16[16,4096]{1,0:T(8,128)(2,1)} fusion(f32[16,4096]{1,0:T(8,128)S(1)} %fusion.44, bf16[256,4096]{1,0:T(8,128)(2,1)} %fusion.8, pred[16,512]{1,0:T(8,128)(4,1)S(1)} %broadcast_compare_fusion.1), kind=kOutput, calls=%fused_computation.9 | convolution fusion | flops 33685504 | bytes 2494464 | tf_op jit(solution)/shard_map/dot_general | solution.py:26
  71.0 2.4 %fusion.105 = f32[256,161]{0,1:T(8,128)S(1)} fusion(bf16[256,4096]{1,0:T(8,128)(2,1)} %fusion.8, bf16[4096,161]{0,1:T(8,128)(2,1)S(1)} %constant_dynamic-update-slice_fusion), kind=kOutput, calls=%fused_computation.209 | convolution fusion | flops 337641472 | bytes 3580928 | tf_op jit(solution)/shard_map/dot_general | solution.py:26
  73.5 2.5 %fusion.106 = f32[256,161]{0,1:T(8,128)S(1)} fusion(bf16[256,4096]{1,0:T(8,128)(2,1)} %collective-permute-done.7, bf16[4096,161]{0,1:T(8,128)(2,1)S(1)} %constant_dynamic-update-slice_fusion), kind=kOutput, calls=%fused_computation.210 | convolution fusion | flops 337641472 | bytes 3580928 | tf_op jit(solution)/shard_map/dot_general | solution.py:26
  76.9 1.7 broadcast_in_dim.91
  78.6 4.9 %all-to-all-start.3 = ((bf16[4,16,4096]{2,1,0:T(8,128)(2,1)}), bf16[4,16,4096]{2,1,0:T(8,128)(2,1)}, u32[]{:S(2)}, u32[]{:S(2)}) async-start(bf16[4,16,4096]{2,1,0:T(8,128)(2,1)} %broadcast_in_dim.91), calls=%async_computation.3 | async-start | bytes 1048576 | tf_op jit(solution)/shard_map/all_to_all | solution.py:30
  83.7 8.3 %all-to-all-done.3 = bf16[4,16,4096]{2,1,0:T(8,128)(2,1)} async-done(((bf16[4,16,4096]{2,1,0:T(8,128)(2,1)}), bf16[4,16,4096]{2,1,0:T(8,128)(2,1)}, u32[]{:S(2)}, u32[]{:S(2)}) %all-to-all-start.3) | async-done | bytes 524320 | tf_op jit(solution)/shard_map/all_to_all | solution.py:30
  92.8 8.8 %all-to-all-start.2 = ((f32[64,2,512]{2,1,0:T(2,128)}), f32[64,2,512]{2,1,0:T(2,128)}, u32[]{:S(2)}, u32[]{:S(2)}) async-start(f32[64,2,512]{2,1,0:T(2,128)} %broadcast_in_dim.87), calls=%async_computation.2 | async-start | bytes 524288 | tf_op jit(solution)/shard_map/all_to_all | solution.py:30
  101.6 1.5 fusion.16
  103.1 2.9 %fusion.6 = f32[64,7680]{1,0:T(8,128)S(1)} fusion(bf16[64,256]{1,0:T(8,128)(2,1)S(1)} %fusion.16, bf16[1,256,7680]{2,1,0:T(8,128)(2,1)} %param.19), kind=kOutput, calls=%fused_computation.13 | convolution fusion | flops 251658240 | bytes 5931008 | tf_op jit(solution)/shard_map/dot_general | solution.py:26
  108.5 3.5 %collective-permute-start.13 = (f32[16,7680]{1,0:T(8,128)}, f32[16,7680]{1,0:T(8,128)}, u32[]{:S(2)}, u32[]{:S(2)}) collective-permute-start(f32[16,7680]{1,0:T(8,128)} %get-tuple-element.50), channel_id=1, source_target_pairs={{0,128},{64,192},{128,0},{192,64},{1,129},{65,193},{129,1},{193,65... | collective-permute-start | bytes 1474568 | tf_op jit(solution)/shard_map/ppermute | solution.py:22
  113.4 2.0 fusion.102
  116.6 6.3 %collective-permute-done.12 = f32[16,7680]{1,0:T(8,128)} collective-permute-done((f32[16,7680]{1,0:T(8,128)}, f32[16,7680]{1,0:T(8,128)}, u32[]{:S(2)}, u32[]{:S(2)}) %collective-permute-start.12) | collective-permute-done | bytes 491552 | tf_op jit(solution)/shard_map/ppermute | solution.py:22
  122.9 1.6 collective-permute-done.13
  124.4 9.5 %collective-permute-done.14 = f32[16,7680]{1,0:T(8,128)} collective-permute-done((f32[16,7680]{1,0:T(8,128)}, f32[16,7680]{1,0:T(8,128)}, u32[]{:S(2)}, u32[]{:S(2)}) %collective-permute-start.14) | collective-permute-done | bytes 491552 | tf_op jit(solution)/shard_map/ppermute | solution.py:22
  133.9 1.7 fusion.100
  137.2 6.0 %all-to-all-start.4 = ((bf16[4,16,7680]{2,1,0:T(8,128)(2,1)}), bf16[4,16,7680]{2,1,0:T(8,128)(2,1)}, u32[]{:S(2)}, u32[]{:S(2)}) async-start(bf16[4,16,7680]{2,1,0:T(8,128)(2,1)} %broadcast_in_dim.94), calls=%async_computation.4 | async-start | bytes 1966080 | tf_op jit(solution)/shard_map/all_to_all | solution.py:30
  145.1 2.1 convolution_convert_fusion.2
  147.2 8.5 %all-to-all-done.4 = bf16[4,16,7680]{2,1,0:T(8,128)(2,1)} async-done(((bf16[4,16,7680]{2,1,0:T(8,128)(2,1)}), bf16[4,16,7680]{2,1,0:T(8,128)(2,1)}, u32[]{:S(2)}, u32[]{:S(2)}) %all-to-all-start.4) | async-done | bytes 983072 | tf_op jit(solution)/shard_map/all_to_all | solution.py:30
  155.7 3.7 %fusion.13 = bf16[64,256]{1,0:T(8,128)(2,1)S(1)} fusion(bf16[64,7680]{1,0:T(8,128)(2,1)} %bitcast.27, bf16[1,256,7680]{2,1,0:T(8,128)(2,1)} %param.19), kind=kOutput, calls=%fused_computation.23 | convolution fusion | flops 251674624 | bytes 4947968 | tf_op jit(solution)/shard_map/dot_general | solution.py:26
  160.4 3.3 %collective-permute-start.16 = (bf16[16,4096]{1,0:T(8,128)(2,1)S(1)}, bf16[16,4096]{1,0:T(8,128)(2,1)S(1)}, u32[]{:S(2)}, u32[]{:S(2)}) collective-permute-start(bf16[16,4096]{1,0:T(8,128)(2,1)S(1)} %get-tuple-element.56), channel_id=1, source_target_pairs={{0,128},{64,192},{128,0},{192,64},{1,129},{65,193},{129,1},{193,65... | collective-permute-start | bytes 393224 | tf_op jit(solution)/shard_map/ppermute | solution.py:22
  165.4 1.6 collective-permute-done.16
  167.0 1.6 collective-permute-done.17
  168.7 3.3 %collective-permute-start.18 = (bf16[16,4096]{1,0:T(8,128)(2,1)S(1)}, bf16[16,4096]{1,0:T(8,128)(2,1)S(1)}, u32[]{:S(2)}, u32[]{:S(2)}) collective-permute-start(bf16[16,4096]{1,0:T(8,128)(2,1)S(1)} %add_convert_fusion.1), channel_id=1, source_target_pairs={{0,48},{16,0},{32,16},{48,32},{1,49},{17,1},{33,17},{49,33},{2,50}... | collective-permute-start | bytes 393224 | tf_op jit(solution)/shard_map/ppermute | solution.py:22
  173.6 2.1 fusion.33
  175.9 2.6 %collective-permute-done.19 = bf16[16,4096]{1,0:T(8,128)(2,1)S(1)} collective-permute-done((bf16[16,4096]{1,0:T(8,128)(2,1)S(1)}, bf16[16,4096]{1,0:T(8,128)(2,1)S(1)}, u32[]{:S(2)}, u32[]{:S(2)}) %collective-permute-start.19) | collective-permute-done | bytes 131104 | tf_op jit(solution)/shard_map/ppermute | solution.py:22
  180.4 2.3 fusion.104
  185.6 2.2 fusion.2
  189.4 3.4 %collective-permute-start.23 = (bf16[161,1024]{1,0:T(8,128)(2,1)}, bf16[161,1024]{1,0:T(8,128)(2,1)}, u32[]{:S(2)}, u32[]{:S(2)}) collective-permute-start(bf16[161,1024]{1,0:T(8,128)(2,1)} %get-tuple-element.53), channel_id=1, source_target_pairs={{0,128},{64,192},{128,0},{192,64},{1,129},{65,193},{129,1},{193,65... | collective-permute-start | bytes 989192 | tf_op jit(solution)/shard_map/ppermute | solution.py:22
  192.7 6.5 %collective-permute-done.10 = bf16[64,4096]{1,0:T(8,128)(2,1)S(1)} collective-permute-done((bf16[64,4096]{1,0:T(8,128)(2,1)S(1)}, bf16[64,4096]{1,0:T(8,128)(2,1)S(1)}, u32[]{:S(2)}, u32[]{:S(2)}) %collective-permute-start.10) | collective-permute-done | bytes 524320 | tf_op jit(solution)/shard_map/ppermute | solution.py:22
  199.3 1.4 collective-permute-start.24
  200.7 7.2 %collective-permute-done.11 = bf16[64,4096]{1,0:T(8,128)(2,1)S(1)} collective-permute-done((bf16[64,4096]{1,0:T(8,128)(2,1)S(1)}, bf16[64,4096]{1,0:T(8,128)(2,1)S(1)}, u32[]{:S(2)}, u32[]{:S(2)}) %collective-permute-start.11) | collective-permute-done | bytes 524320 | tf_op jit(solution)/shard_map/ppermute | solution.py:22
  207.9 2.1 collective-permute-done.9
  211.2 6.7 %all-to-all-start.5 = ((bf16[8,8,4096]{2,1,0:T(8,128)(2,1)}), bf16[8,8,4096]{2,1,0:T(8,128)(2,1)}, u32[]{:S(2)}, u32[]{:S(2)}) async-start(bf16[8,8,4096]{2,1,0:T(8,128)(2,1)} %fusion.24), calls=%async_computation.5 | async-start | bytes 1048576 | tf_op jit(solution)/shard_map/all_to_all | solution.py:30
  220.7 3.1 %fusion.1 = bf16[1,4096,256]{2,1,0:T(8,128)(2,1)} fusion(bf16[64,4096]{1,0:T(8,128)(2,1)} %bitcast.24, bf16[64,256]{1,0:T(8,128)(2,1)S(1)} %fusion.13), kind=kOutput, calls=%fused_computation.5 | convolution fusion | flops 135266304 | bytes 2654208 | tf_op jit(solution)/shard_map/dot_general | solution.py:26
  223.8 4.3 %fusion = bf16[1,256,7680]{2,1,0:T(8,128)(2,1)} fusion(bf16[64,256]{1,0:T(8,128)(2,1)S(1)} %fusion.16, bf16[64,7680]{1,0:T(8,128)(2,1)} %bitcast.27), kind=kOutput, calls=%fused_computation.1 | convolution fusion | flops 253624320 | bytes 4947968 | tf_op jit(solution)/shard_map/dot_general | solution.py:26
  228.1 7.6 %all-to-all-done.5 = bf16[8,8,4096]{2,1,0:T(8,128)(2,1)} async-done(((bf16[8,8,4096]{2,1,0:T(8,128)(2,1)}), bf16[8,8,4096]{2,1,0:T(8,128)(2,1)}, u32[]{:S(2)}, u32[]{:S(2)}) %all-to-all-start.5) | async-done | bytes 524320 | tf_op jit(solution)/shard_map/all_to_all | solution.py:30
  235.6 1.8 reduce_sum.75
  (126 shorter events, 43.7 us)
Async XLA Ops:
  0.6 101.0 %copy-start = (bf16[1,4096,256]{2,1,0:T(8,128)(2,1)S(1)}, bf16[1,4096,256]{2,1,0:T(8,128)(2,1)}, u32[]{:S(2)}) copy-start(bf16[1,4096,256]{2,1,0:T(8,128)(2,1)} %param.18) | copy-start | bytes 6291460
  1.5 17.4 %collective-permute-start = (bf16[8,1408]{1,0:T(8,128)(2,1)S(1)}, bf16[8,1408]{1,0:T(8,128)(2,1)S(1)}, u32[]{:S(2)}, u32[]{:S(2)}) collective-permute-start(bf16[8,1408]{1,0:T(8,128)(2,1)S(1)} %slice.99), channel_id=1, source_target_pairs={{0,48},{16,0},{32,16},{48,32},{1,49},{17,1},{33,17},{49,33},{2,50}... | collective-permute-start | bytes 67592 | tf_op jit(solution)/shard_map/ppermute | solution.py:22
  4.3 14.7 %collective-permute-start.1 = (bf16[8,1408]{1,0:T(8,128)(2,1)S(1)}, bf16[8,1408]{1,0:T(8,128)(2,1)S(1)}, u32[]{:S(2)}, u32[]{:S(2)}) collective-permute-start(bf16[8,1408]{1,0:T(8,128)(2,1)S(1)} %slice.99), channel_id=1, source_target_pairs={{0,32},{16,48},{32,0},{48,16},{1,33},{17,49},{33,1},{49,17},{2,34}... | collective-permute-start | bytes 67592 | tf_op jit(solution)/shard_map/ppermute | solution.py:22
  5.1 13.9 %collective-permute-start.2 = (bf16[8,1408]{1,0:T(8,128)(2,1)S(1)}, bf16[8,1408]{1,0:T(8,128)(2,1)}, u32[]{:S(2)}, u32[]{:S(2)}) collective-permute-start(bf16[8,1408]{1,0:T(8,128)(2,1)S(1)} %slice.99), channel_id=1, source_target_pairs={{0,16},{16,32},{32,48},{48,0},{1,17},{17,33},{33,49},{49,1},{2,18}... | collective-permute-start | bytes 67592 | tf_op jit(solution)/shard_map/ppermute | solution.py:22
  9.0 21.7 %all-to-all-start = ((bf16[8,8,2816]{2,1,0:T(8,128)(2,1)}), bf16[8,8,2816]{2,1,0:T(8,128)(2,1)}, u32[]{:S(2)}, u32[]{:S(2)}) async-start(bf16[8,8,2816]{2,1,0:T(8,128)(2,1)} %broadcast_in_dim.83), calls=%async_computation | async-start | bytes 720896 | tf_op jit(solution)/shard_map/all_to_all | solution.py:30
  17.4 1.5 copy-start.6
  32.5 23.8 %all-to-all-start.1 = ((bf16[8,32,1408]{2,1,0:T(8,128)(2,1)}), bf16[8,32,1408]{2,1,0:T(8,128)(2,1)}, u32[]{:S(2)}, u32[]{:S(2)}) async-start(bf16[8,32,1408]{2,1,0:T(8,128)(2,1)} %broadcast_in_dim.84), calls=%async_computation.1 | async-start | bytes 1441792 | tf_op jit(solution)/shard_map/all_to_all | solution.py:30
  36.8 12.2 %collective-permute-start.5 = (bf16[64,2816]{1,0:T(8,128)(2,1)}, bf16[64,2816]{1,0:T(8,128)(2,1)}, u32[]{:S(2)}, u32[]{:S(2)}) collective-permute-start(bf16[64,2816]{1,0:T(8,128)(2,1)} %bitcast.4), channel_id=1, source_target_pairs={{0,16},{16,32},{32,48},{48,0},{1,17},{17,33},{33,49},{49,1},{2,18}... | collective-permute-start | bytes 1081352 | tf_op jit(solution)/shard_map/ppermute | solution.py:22
  38.6 11.6 %collective-permute-start.3 = (bf16[64,2816]{1,0:T(8,128)(2,1)}, bf16[64,2816]{1,0:T(8,128)(2,1)}, u32[]{:S(2)}, u32[]{:S(2)}) collective-permute-start(bf16[64,2816]{1,0:T(8,128)(2,1)} %bitcast.4), channel_id=1, source_target_pairs={{0,48},{16,0},{32,16},{48,32},{1,49},{17,1},{33,17},{49,33},{2,50}... | collective-permute-start | bytes 1081352 | tf_op jit(solution)/shard_map/ppermute | solution.py:22
  40.1 14.2 %collective-permute-start.4 = (bf16[64,2816]{1,0:T(8,128)(2,1)}, bf16[64,2816]{1,0:T(8,128)(2,1)}, u32[]{:S(2)}, u32[]{:S(2)}) collective-permute-start(bf16[64,2816]{1,0:T(8,128)(2,1)} %bitcast.4), channel_id=1, source_target_pairs={{0,32},{16,48},{32,0},{48,16},{1,33},{17,49},{33,1},{49,17},{2,34}... | collective-permute-start | bytes 1081352 | tf_op jit(solution)/shard_map/ppermute | solution.py:22
  60.7 5.7 %collective-permute-start.7 = (bf16[256,4096]{1,0:T(8,128)(2,1)}, bf16[256,4096]{1,0:T(8,128)(2,1)}, u32[]{:S(2)}, u32[]{:S(2)}) collective-permute-start(bf16[256,4096]{1,0:T(8,128)(2,1)} %fusion.8), channel_id=1, source_target_pairs={{0,1},{1,0},{2,3},{3,2},{4,5},{5,4},{6,7},{7,6},{8,9},{9,8},{10,11... | collective-permute-start | bytes 6291464 | tf_op jit(solution)/shard_map/ppermute | solution.py:22
  60.8 4.5 %collective-permute-start.6 = (f32[2,4,64]{2,1,0:T(4,128)S(1)}, f32[2,4,64]{2,1,0:T(4,128)S(1)}, u32[]{:S(2)}, u32[]{:S(2)}) collective-permute-start(f32[2,4,64]{2,1,0:T(4,128)S(1)} %get-tuple-element.65), channel_id=1, source_target_pairs={{0,1},{1,0},{2,3},{3,2},{4,5},{5,4},{6,7},{7,6},{8,9},{9,8},{10,11... | collective-permute-start | bytes 6152 | tf_op jit(solution)/shard_map/ppermute | solution.py:22
  73.5 2.6 %copy-start.2 = (f32[256,161]{0,1:T(8,128)}, f32[256,161]{0,1:T(8,128)S(1)}, u32[]{:S(2)}) copy-start(f32[256,161]{0,1:T(8,128)S(1)} %fusion.105) | copy-start | bytes 494596
  76.0 0.7 copy-start.3
  78.6 13.3 %all-to-all-start.3 = ((bf16[4,16,4096]{2,1,0:T(8,128)(2,1)}), bf16[4,16,4096]{2,1,0:T(8,128)(2,1)}, u32[]{:S(2)}, u32[]{:S(2)}) async-start(bf16[4,16,4096]{2,1,0:T(8,128)(2,1)} %broadcast_in_dim.91), calls=%async_computation.3 | async-start | bytes 1048576 | tf_op jit(solution)/shard_map/all_to_all | solution.py:30
  92.8 20.7 %all-to-all-start.2 = ((f32[64,2,512]{2,1,0:T(2,128)}), f32[64,2,512]{2,1,0:T(2,128)}, u32[]{:S(2)}, u32[]{:S(2)}) async-start(f32[64,2,512]{2,1,0:T(2,128)} %broadcast_in_dim.87), calls=%async_computation.2 | async-start | bytes 524288 | tf_op jit(solution)/shard_map/all_to_all | solution.py:30
  106.0 1.3 copy-start.1
  108.5 14.4 %collective-permute-start.12 = (f32[16,7680]{1,0:T(8,128)}, f32[16,7680]{1,0:T(8,128)}, u32[]{:S(2)}, u32[]{:S(2)}) collective-permute-start(f32[16,7680]{1,0:T(8,128)} %get-tuple-element.48), channel_id=1, source_target_pairs={{0,64},{64,128},{128,192},{192,0},{1,65},{65,129},{129,193},{193,1... | collective-permute-start | bytes 1474568 | tf_op jit(solution)/shard_map/ppermute | solution.py:22
  108.5 16.0 %collective-permute-start.13 = (f32[16,7680]{1,0:T(8,128)}, f32[16,7680]{1,0:T(8,128)}, u32[]{:S(2)}, u32[]{:S(2)}) collective-permute-start(f32[16,7680]{1,0:T(8,128)} %get-tuple-element.50), channel_id=1, source_target_pairs={{0,128},{64,192},{128,0},{192,64},{1,129},{65,193},{129,1},{193,65... | collective-permute-start | bytes 1474568 | tf_op jit(solution)/shard_map/ppermute | solution.py:22
  112.0 21.9 %collective-permute-start.14 = (f32[16,7680]{1,0:T(8,128)}, f32[16,7680]{1,0:T(8,128)}, u32[]{:S(2)}, u32[]{:S(2)}) collective-permute-start(f32[16,7680]{1,0:T(8,128)} %get-tuple-element.49), channel_id=1, source_target_pairs={{0,192},{64,0},{128,64},{192,128},{1,193},{65,1},{129,65},{193,129... | collective-permute-start | bytes 1474568 | tf_op jit(solution)/shard_map/ppermute | solution.py:22
  137.2 18.6 %all-to-all-start.4 = ((bf16[4,16,7680]{2,1,0:T(8,128)(2,1)}), bf16[4,16,7680]{2,1,0:T(8,128)(2,1)}, u32[]{:S(2)}, u32[]{:S(2)}) async-start(bf16[4,16,7680]{2,1,0:T(8,128)(2,1)} %broadcast_in_dim.94), calls=%async_computation.4 | async-start | bytes 1966080 | tf_op jit(solution)/shard_map/all_to_all | solution.py:30
  144.4 0.7 copy-start.4
  147.2 33.2 %collective-permute-start.8 = (bf16[256,4096]{1,0:T(8,128)(2,1)}, bf16[256,4096]{1,0:T(8,128)(2,1)}, u32[]{:S(2)}, u32[]{:S(2)}) collective-permute-start(bf16[256,4096]{1,0:T(8,128)(2,1)} %convolution_convert_fusion.2), channel_id=1, source_target_pairs={{0,1},{1,0},{2,3},{3,2},{4,5},{5,4},{6,7},{7,6},{8,9},{9,8},{10,11... | collective-permute-start | bytes 6291464 | tf_op jit(solution)/shard_map/ppermute | solution.py:22
  159.4 14.1 %copy-start.5 = (bf16[512,161]{0,1:T(8,128)(2,1)S(1)}, bf16[512,161]{0,1:T(8,128)(2,1)}, u32[]{:S(2)}) copy-start(bf16[512,161]{0,1:T(8,128)(2,1)} %copy-done.4) | copy-start | bytes 494596
  160.3 5.2 %collective-permute-start.15 = (bf16[16,4096]{1,0:T(8,128)(2,1)S(1)}, bf16[16,4096]{1,0:T(8,128)(2,1)S(1)}, u32[]{:S(2)}, u32[]{:S(2)}) collective-permute-start(bf16[16,4096]{1,0:T(8,128)(2,1)S(1)} %get-tuple-element.54), channel_id=1, source_target_pairs={{0,64},{64,128},{128,192},{192,0},{1,65},{65,129},{129,193},{193,1... | collective-permute-start | bytes 393224 | tf_op jit(solution)/shard_map/ppermute | solution.py:22
  160.4 6.6 %collective-permute-start.16 = (bf16[16,4096]{1,0:T(8,128)(2,1)S(1)}, bf16[16,4096]{1,0:T(8,128)(2,1)S(1)}, u32[]{:S(2)}, u32[]{:S(2)}) collective-permute-start(bf16[16,4096]{1,0:T(8,128)(2,1)S(1)} %get-tuple-element.56), channel_id=1, source_target_pairs={{0,128},{64,192},{128,0},{192,64},{1,129},{65,193},{129,1},{193,65... | collective-permute-start | bytes 393224 | tf_op jit(solution)/shard_map/ppermute | solution.py:22
  163.7 5.0 %collective-permute-start.17 = (bf16[16,4096]{1,0:T(8,128)(2,1)S(1)}, bf16[16,4096]{1,0:T(8,128)(2,1)S(1)}, u32[]{:S(2)}, u32[]{:S(2)}) collective-permute-start(bf16[16,4096]{1,0:T(8,128)(2,1)S(1)} %get-tuple-element.55), channel_id=1, source_target_pairs={{0,192},{64,0},{128,64},{192,128},{1,193},{65,1},{129,65},{193,129... | collective-permute-start | bytes 393224 | tf_op jit(solution)/shard_map/ppermute | solution.py:22
  168.7 7.2 %collective-permute-start.18 = (bf16[16,4096]{1,0:T(8,128)(2,1)S(1)}, bf16[16,4096]{1,0:T(8,128)(2,1)S(1)}, u32[]{:S(2)}, u32[]{:S(2)}) collective-permute-start(bf16[16,4096]{1,0:T(8,128)(2,1)S(1)} %add_convert_fusion.1), channel_id=1, source_target_pairs={{0,48},{16,0},{32,16},{48,32},{1,49},{17,1},{33,17},{49,33},{2,50}... | collective-permute-start | bytes 393224 | tf_op jit(solution)/shard_map/ppermute | solution.py:22
  172.0 6.6 %collective-permute-start.19 = (bf16[16,4096]{1,0:T(8,128)(2,1)S(1)}, bf16[16,4096]{1,0:T(8,128)(2,1)S(1)}, u32[]{:S(2)}, u32[]{:S(2)}) collective-permute-start(bf16[16,4096]{1,0:T(8,128)(2,1)S(1)} %add_convert_fusion.1), channel_id=1, source_target_pairs={{0,32},{16,48},{32,0},{48,16},{1,33},{17,49},{33,1},{49,17},{2,34}... | collective-permute-start | bytes 393224 | tf_op jit(solution)/shard_map/ppermute | solution.py:22
  172.6 7.2 %collective-permute-start.20 = (bf16[16,4096]{1,0:T(8,128)(2,1)S(1)}, bf16[16,4096]{1,0:T(8,128)(2,1)S(1)}, u32[]{:S(2)}, u32[]{:S(2)}) collective-permute-start(bf16[16,4096]{1,0:T(8,128)(2,1)S(1)} %add_convert_fusion.1), channel_id=1, source_target_pairs={{0,16},{16,32},{32,48},{48,0},{1,17},{17,33},{33,49},{49,1},{2,18}... | collective-permute-start | bytes 393224 | tf_op jit(solution)/shard_map/ppermute | solution.py:22
  180.3 9.1 %collective-permute-start.21 = (bf16[64,4096]{1,0:T(8,128)(2,1)S(1)}, bf16[64,4096]{1,0:T(8,128)(2,1)S(1)}, u32[]{:S(2)}, u32[]{:S(2)}) collective-permute-start(bf16[64,4096]{1,0:T(8,128)(2,1)S(1)} %convolution_convert_fusion.3), channel_id=1, source_target_pairs={{0,1},{1,0},{2,3},{3,2},{4,5},{5,4},{6,7},{7,6},{8,9},{9,8},{10,11... | collective-permute-start | bytes 1572872 | tf_op jit(solution)/shard_map/ppermute | solution.py:22
  182.8 16.4 %collective-permute-start.10 = (bf16[64,4096]{1,0:T(8,128)(2,1)S(1)}, bf16[64,4096]{1,0:T(8,128)(2,1)S(1)}, u32[]{:S(2)}, u32[]{:S(2)}) collective-permute-start(bf16[64,4096]{1,0:T(8,128)(2,1)S(1)} %get-tuple-element.47), channel_id=1, source_target_pairs={{0,32},{16,48},{32,0},{48,16},{1,33},{17,49},{33,1},{49,17},{2,34}... | collective-permute-start | bytes 1572872 | tf_op jit(solution)/shard_map/ppermute | solution.py:22
  183.6 24.3 %collective-permute-start.11 = (bf16[64,4096]{1,0:T(8,128)(2,1)S(1)}, bf16[64,4096]{1,0:T(8,128)(2,1)S(1)}, u32[]{:S(2)}, u32[]{:S(2)}) collective-permute-start(bf16[64,4096]{1,0:T(8,128)(2,1)S(1)} %get-tuple-element.46), channel_id=1, source_target_pairs={{0,48},{16,0},{32,16},{48,32},{1,49},{17,1},{33,17},{49,33},{2,50}... | collective-permute-start | bytes 1572872 | tf_op jit(solution)/shard_map/ppermute | solution.py:22
  184.7 25.2 %collective-permute-start.9 = (bf16[64,4096]{1,0:T(8,128)(2,1)S(1)}, bf16[64,4096]{1,0:T(8,128)(2,1)S(1)}, u32[]{:S(2)}, u32[]{:S(2)}) collective-permute-start(bf16[64,4096]{1,0:T(8,128)(2,1)S(1)} %get-tuple-element.45), channel_id=1, source_target_pairs={{0,16},{16,32},{32,48},{48,0},{1,17},{17,33},{33,49},{49,1},{2,18}... | collective-permute-start | bytes 1572872 | tf_op jit(solution)/shard_map/ppermute | solution.py:22
  188.8 29.1 %collective-permute-start.22 = (bf16[161,1024]{1,0:T(8,128)(2,1)}, bf16[161,1024]{1,0:T(8,128)(2,1)}, u32[]{:S(2)}, u32[]{:S(2)}) collective-permute-start(bf16[161,1024]{1,0:T(8,128)(2,1)} %get-tuple-element.51), channel_id=1, source_target_pairs={{0,64},{64,128},{128,192},{192,0},{1,65},{65,129},{129,193},{193,1... | collective-permute-start | bytes 989192 | tf_op jit(solution)/shard_map/ppermute | solution.py:22
  189.4 28.5 %collective-permute-start.23 = (bf16[161,1024]{1,0:T(8,128)(2,1)}, bf16[161,1024]{1,0:T(8,128)(2,1)}, u32[]{:S(2)}, u32[]{:S(2)}) collective-permute-start(bf16[161,1024]{1,0:T(8,128)(2,1)} %get-tuple-element.53), channel_id=1, source_target_pairs={{0,128},{64,192},{128,0},{192,64},{1,129},{65,193},{129,1},{193,65... | collective-permute-start | bytes 989192 | tf_op jit(solution)/shard_map/ppermute | solution.py:22
  199.3 18.6 %collective-permute-start.24 = (bf16[161,1024]{1,0:T(8,128)(2,1)}, bf16[161,1024]{1,0:T(8,128)(2,1)}, u32[]{:S(2)}, u32[]{:S(2)}) collective-permute-start(bf16[161,1024]{1,0:T(8,128)(2,1)} %get-tuple-element.52), channel_id=1, source_target_pairs={{0,192},{64,0},{128,64},{192,128},{1,193},{65,1},{129,65},{193,129... | collective-permute-start | bytes 989192 | tf_op jit(solution)/shard_map/ppermute | solution.py:22
  211.2 24.5 %all-to-all-start.5 = ((bf16[8,8,4096]{2,1,0:T(8,128)(2,1)}), bf16[8,8,4096]{2,1,0:T(8,128)(2,1)}, u32[]{:S(2)}, u32[]{:S(2)}) async-start(bf16[8,8,4096]{2,1,0:T(8,128)(2,1)} %fusion.24), calls=%async_computation.5 | async-start | bytes 1048576 | tf_op jit(solution)/shard_map/all_to_all | solution.py:30

commit v3 on v2

--- a/solution.py
+++ b/solution.py
@@ -53,14 +53,27 @@
     a1, b1 = lax.optimization_barrier((a1, b1))
     a2 = from_everyone(a1, "z").reshape(NZ, NX, OWN, CA)
     b2 = [b1] + [shift(b1, "x", -k) for k in range(1, NX)]
-    digits = jnp.stack([b[:, rest : rest + 4] for b in b2]).astype(F32)
-    target = digits[..., 0] * 65536.0 + digits[..., 1] * 256.0 + digits[..., 2]
-    meta = jnp.stack([target, digits[..., 3]])
+    own = jnp.zeros((NX * NZ * OWN, model + META), BF16)
+    for k in range(NX):
+        own = lax.dynamic_update_slice(own, b2[k], (k * NZ * OWN, 0))
+    digits = own[:, rest : rest + META].astype(F32)
+    target = digits[:, 0] * 65536.0 + digits[:, 1] * 256.0 + digits[:, 2]
+    meta = jnp.stack([target, digits[:, 3]])
     meta = jnp.stack([meta, shift(meta, "core", 1)], axis=1)
     a2 = jnp.swapaxes(a2, 0, 1).reshape(-1, CA)
-    own = jnp.concatenate([a2, jnp.concatenate(b2, axis=0)[:, :rest]], axis=1)
+    own = lax.dynamic_update_slice(own, a2, (0, rest + META))
     other = shift(own, "core", 1)
     return own, other, meta.reshape(2, -1)
+
+
+def mixed(weight):
+    gap = jnp.zeros((META, weight.shape[1]), weight.dtype)
+    return jnp.concatenate([weight[CA:], gap, weight[:CA]], axis=0)
+
+
+def plain(value):
+    split = value.shape[1] - CA
+    return jnp.concatenate([value[:, split:], value[:, : split - META]], axis=1)
 
 
 def joined_stats(top, total):
@@ -86,6 +99,7 @@
     dp_index = lax.axis_index("dp")
     model, width = head_weight.shape
     weight = jnp.concatenate([head_weight, cluster_weight], axis=1)
+    weight_mixed = mixed(weight)
     own, other, meta = gathered(hidden, targets, loss_weight)
     side = own.shape[0]
 
@@ -105,7 +119,7 @@
     gain_tail = jnp.sum(jnp.where(holds, gain[None, :], 0.0), axis=1)
 
     select = holds.astype(BF16)
-    picked = (dot(select[:, :side], own) + dot(select[:, side:], other)).astype(BF16)
+    picked = plain((dot(select[:, :side], own) + dot(select[:, side:], other)).astype(BF16))
     rows = from_everyone(picked, "dp")
     rows = rows.reshape(NDP * CAP, -1)
     proj = tail_proj[0]
@@ -124,17 +138,19 @@
     total = jnp.sum(share_exp, axis=1, keepdims=True)
     hot = (jnp.arange(CV, dtype=jnp.int32)[None, :] == words[:, None]).astype(F32)
     share_delta = (gain_tail[:, None] * (share_exp / total - hot)).astype(BF16)
-    word_delta = from_everyone(share_delta, "dp").reshape(NDP * CAP, -1)
+    word_delta = jnp.concatenate(
+        [share_delta] + [shift(share_delta, "dp", -k) for k in range(1, NDP)], axis=0
+    )
     reduced_grad = dot(word_delta, out, 1, 1).astype(BF16)
     tail_partial = dot(reduced_grad, proj, 1, 1)
-    tail_sum = block(tail_partial, 0, CAP, 0)
+    tail_sum = tail_partial[:CAP]
     for k in range(1, NDP):
-        piece = block(tail_partial, k, CAP, 0).astype(BF16)
+        piece = tail_partial[k * CAP : (k + 1) * CAP].astype(BF16)
         tail_sum = tail_sum + shift(piece, "dp", k).astype(F32)
     tail_sum = tail_sum.astype(BF16)
 
     (own, other), _ = lax.optimization_barrier(((own, other), picked))
-    logits = jnp.concatenate([dot(own, weight), dot(other, weight)], axis=0)
+    logits = jnp.concatenate([dot(own, weight_mixed), dot(other, weight_mixed)], axis=0)
     lane = jnp.arange(width + 1, dtype=jnp.int32)
     columns = jnp.where(lane < width, vocab_index * width + lane, HEAD + vocab_index)
     target_column = jnp.where(offset >= 0, HEAD + offset // CV, target)
@@ -170,13 +186,20 @@
     hidden_grad = jnp.sum(last.astype(F32), axis=0).astype(BF16)
 
     grad_t = (dot(near, own, 0, 0) + dot(far, other, 0, 0)).astype(BF16)
+    grad_t = plain(grad_t)
     pieces = [block(grad_t, k, model // NDP, 1) for k in range(NDP)]
     head_sum = pieces[0].astype(F32)
     for k in range(1, NDP):
         head_sum = head_sum + shift(pieces[k], "dp", k).astype(F32)
     head_sum = head_sum.astype(BF16)
-    out_grad = dot(reduced, word_delta, 0, 0).astype(BF16)
-    proj_grad = dot(rows, reduced_grad, 0, 0).astype(BF16)
+
+    def turned(value):
+        return lax.dynamic_slice_in_dim(
+            jnp.concatenate([value] * 2), dp_index * CAP, NDP * CAP
+        )
+
+    out_grad = dot(turned(reduced), word_delta, 0, 0).astype(BF16)
+    proj_grad = dot(turned(rows), reduced_grad, 0, 0).astype(BF16)
     return (
         hidden_grad,
         head_sum[:width].T,

time: 241 us -> 227 us (0.942)
  matrix products: 35.3 us -> 23.9 us
  waiting for transfers between devices: 93 us -> 88.5 us
  local copies, waits for them, and re-layouts: 21 us -> 24.5 us
    dot_general x16, matrix products: 35.3 us -> 23.9 us  [dot(): lax.dot_general(a, b, (((ca,), (cb,)), ((), ())), preferred_element_type=...]
    all_to_all x6 -> x5, starting transfers between devices: 39.1 us -> 30.1 us  [swapped(): return lax.all_to_all(parts, axis, split_axis=0, concat_axis=0, tiled=True)]
    ppermute x25 -> x28, starting transfers between devices: 30 us -> 38.2 us  [shift(): return lax.ppermute(value, axis, [(j, (j + step) % n) for j in range(n)])]
    dynamic_update_slice x0 -> x5, local copies, waits for them, and re-layouts: none -> 5.07 us  [the longest x4 4.15 us: gathered(): own = lax.dynamic_update_slice(own, b2[k], (k * NZ * OWN, 0))]
    ppermute x25 -> x28, waiting for transfers between devices: 56.3 us -> 53.7 us  [shift(): return lax.ppermute(value, axis, [(j, (j + step) % n) for j in range(n)])]
    another operation x6 -> x0, local copies, waits for them, and re-layouts: 2.45 us -> none  [gathered(): digits = jnp.stack([b[:, rest:rest + 4] for b in b2]).astype(F32)]
    all_to_all x6 -> x5, waiting for transfers between devices: 36.7 us -> 34.8 us  [swapped(): return lax.all_to_all(parts, axis, split_axis=0, concat_axis=0, tiled=True)]
    unnamed x18 -> x48, local copies, waits for them, and re-layouts: 4.11 us -> 5.74 us
  transfers between devices with their start and end apart: 31 -> 33, of which waited for: 22 -> 22; matrix products, arithmetic and copies ran while one was open for 20% -> 20% of each run, Pallas kernels for 0% -> 0%
where the time goes in v3:
time: 227 us; the launch traced here: 224 us
  waiting for transfers between devices  88.5 us (39%)
  starting transfers between devices  68.3 us (30%)
  local copies, waits for them, and re-layouts  24.5 us (11%)
  matrix products  23.9 us (11%)
  other arithmetic  17.6 us (8%)
    ppermute x28, waiting for transfers between devices, shift(): return lax.ppermute(value, axis, [(j, (j + step) % n) for j in range(n)])  53.7 us
    ppermute x28, starting transfers between devices, shift(): return lax.ppermute(value, axis, [(j, (j + step) % n) for j in range(n)])  38.2 us
    all_to_all x5, waiting for transfers between devices, swapped(): return lax.all_to_all(parts, axis, split_axis=0, concat_axis=0, tiled=True)  34.8 us
    all_to_all x5, starting transfers between devices, swapped(): return lax.all_to_all(parts, axis, split_axis=0, concat_axis=0, tiled=True)  30.1 us
    dot_general x16, matrix products, dot(): lax.dot_general(a, b, (((ca,), (cb,)), ((), ())), preferred_element_type=...  23.9 us
    unnamed x48, local copies, waits for them, and re-layouts  5.74 us
    broadcast_in_dim x4, local copies, waits for them, and re-layouts, from_everyone(): jnp.broadcast_to(value, (lax.axis_size(axis), *value.shape))  5.06 us
  transfers between devices with their start and end apart: 33, of which 22 were waited for; matrix products, arithmetic and copies ran while one was open for 20% of the time, Pallas kernels for 0%

profile of v3, /device:TPU:8, one launch (start us, length us, event | category | flops | bytes accessed | tf_op | source)
XLA Modules:
  0.0 224.0 jit_solution(1287508012492468707)
XLA Ops:
  1.5 1.5 collective-permute-start.2
  3.0 2.7 %collective-permute-start.1 = (bf16[8,1408]{1,0:T(8,128)(2,1)S(1)}, bf16[8,1408]{1,0:T(8,128)(2,1)S(1)}, u32[]{:S(2)}, u32[]{:S(2)}) collective-permute-start(bf16[8,1408]{1,0:T(8,128)(2,1)S(1)} %slice.120), channel_id=1, source_target_pairs={{0,32},{16,48},{32,0},{48,16},{1,33},{17,49},{33,1},{49,17},{2,34}... | collective-permute-start | bytes 67592 | tf_op jit(solution)/shard_map/ppermute | solution.py:22
  5.8 1.4 collective-permute-start
  10.2 8.5 %all-to-all-start = ((bf16[8,8,2816]{2,1,0:T(8,128)(2,1)}), bf16[8,8,2816]{2,1,0:T(8,128)(2,1)}, u32[]{:S(2)}, u32[]{:S(2)}) async-start(bf16[8,8,2816]{2,1,0:T(8,128)(2,1)} %broadcast_in_dim.84), calls=%async_computation | async-start | bytes 720896 | tf_op jit(solution)/shard_map/all_to_all | solution.py:30
  21.5 10.4 %all-to-all-done = bf16[8,8,2816]{2,1,0:T(8,128)(2,1)} async-done(((bf16[8,8,2816]{2,1,0:T(8,128)(2,1)}), bf16[8,8,2816]{2,1,0:T(8,128)(2,1)}, u32[]{:S(2)}, u32[]{:S(2)}) %all-to-all-start) | async-done | bytes 360480 | tf_op jit(solution)/shard_map/all_to_all | solution.py:30
  32.3 2.4 %collective-permute-start.4 = (bf16[64,2816]{1,0:T(8,128)(2,1)}, bf16[64,2816]{1,0:T(8,128)(2,1)}, u32[]{:S(2)}, u32[]{:S(2)}) collective-permute-start(bf16[64,2816]{1,0:T(8,128)(2,1)} %bitcast.4), channel_id=1, source_target_pairs={{0,32},{16,48},{32,0},{48,16},{1,33},{17,49},{33,1},{49,17},{2,34}... | collective-permute-start | bytes 1081352 | tf_op jit(solution)/shard_map/ppermute | solution.py:22
  34.7 1.8 broadcast_in_dim.85
  36.5 4.2 %all-to-all-start.1 = ((bf16[8,32,1408]{2,1,0:T(8,128)(2,1)}), bf16[8,32,1408]{2,1,0:T(8,128)(2,1)}, u32[]{:S(2)}, u32[]{:S(2)}) async-start(bf16[8,32,1408]{2,1,0:T(8,128)(2,1)} %broadcast_in_dim.85), calls=%async_computation.1 | async-start | bytes 1441792 | tf_op jit(solution)/shard_map/all_to_all | solution.py:30
  41.8 1.7 collective-permute-done.3
  46.4 2.9 %collective-permute-done.5 = bf16[64,2816]{1,0:T(8,128)(2,1)} collective-permute-done((bf16[64,2816]{1,0:T(8,128)(2,1)}, bf16[64,2816]{1,0:T(8,128)(2,1)}, u32[]{:S(2)}, u32[]{:S(2)}) %collective-permute-start.5) | collective-permute-done | bytes 360480 | tf_op jit(solution)/shard_map/ppermute | solution.py:22
  52.4 7.3 %all-to-all-done.1 = bf16[8,32,1408]{2,1,0:T(8,128)(2,1)} async-done(((bf16[8,32,1408]{2,1,0:T(8,128)(2,1)}), bf16[8,32,1408]{2,1,0:T(8,128)(2,1)}, u32[]{:S(2)}, u32[]{:S(2)}) %all-to-all-start.1) | async-done | bytes 720928 | tf_op jit(solution)/shard_map/all_to_all | solution.py:30
  64.6 1.7 collective-permute-done.6
  67.7 2.2 fusion.60
  72.1 2.6 %fusion.23 = f32[256,161]{0,1:T(8,128)S(1)} fusion(bf16[256,4224]{1,0:T(8,128)(2,1)} %collective-permute-done.7, bf16[1408,161]{0,1:T(8,128)(2,1)S(1)} %copy-done.13, bf16[2688,161]{0,1:T(8,128)(2,1)S(1)} %copy-done.12, bf16[4224]{0:T(1024)(128)(2,1)S(1)} %pad.27.clone), kind=kOutput, calls=%fused_computation.40 | convolution fusion | flops 352273152 | bytes 3654912 | tf_op jit(solution)/shard_map/dot_general | solution.py:26
  75.6 1.7 broadcast_in_dim.93
  77.3 4.9 %all-to-all-start.3 = ((bf16[4,16,4096]{2,1,0:T(8,128)(2,1)}), bf16[4,16,4096]{2,1,0:T(8,128)(2,1)}, u32[]{:S(2)}, u32[]{:S(2)}) async-start(bf16[4,16,4096]{2,1,0:T(8,128)(2,1)} %broadcast_in_dim.93), calls=%async_computation.3 | async-start | bytes 1048576 | tf_op jit(solution)/shard_map/all_to_all | solution.py:30
  82.4 8.3 %all-to-all-done.3 = bf16[4,16,4096]{2,1,0:T(8,128)(2,1)} async-done(((bf16[4,16,4096]{2,1,0:T(8,128)(2,1)}), bf16[4,16,4096]{2,1,0:T(8,128)(2,1)}, u32[]{:S(2)}, u32[]{:S(2)}) %all-to-all-start.3) | async-done | bytes 524320 | tf_op jit(solution)/shard_map/all_to_all | solution.py:30
  91.4 5.8 %all-to-all-start.2 = ((f32[64,2,512]{2,1,0:T(2,128)}), f32[64,2,512]{2,1,0:T(2,128)}, u32[]{:S(2)}, u32[]{:S(2)}) async-start(f32[64,2,512]{2,1,0:T(2,128)} %broadcast_in_dim.89), calls=%async_computation.2 | async-start | bytes 524288 | tf_op jit(solution)/shard_map/all_to_all | solution.py:30
  97.2 1.5 fusion.15
  98.7 2.9 %fusion.6 = f32[64,7680]{1,0:T(8,128)S(1)} fusion(bf16[64,256]{1,0:T(8,128)(2,1)S(1)} %fusion.15, bf16[1,256,7680]{2,1,0:T(8,128)(2,1)} %param.19), kind=kOutput, calls=%fused_computation.13 | convolution fusion | flops 251658240 | bytes 5931008 | tf_op jit(solution)/shard_map/dot_general | solution.py:26
  104.1 2.0 collective-permute-start.14
  106.1 1.5 collective-permute-start.13
  109.0 2.0 fusion.119
  113.5 5.0 %collective-permute-done.12 = f32[16,7680]{1,0:T(8,128)} collective-permute-done((f32[16,7680]{1,0:T(8,128)}, f32[16,7680]{1,0:T(8,128)}, u32[]{:S(2)}, u32[]{:S(2)}) %collective-permute-start.12) | collective-permute-done | bytes 491552 | tf_op jit(solution)/shard_map/ppermute | solution.py:22
  118.5 11.0 %collective-permute-done.13 = f32[16,7680]{1,0:T(8,128)} collective-permute-done((f32[16,7680]{1,0:T(8,128)}, f32[16,7680]{1,0:T(8,128)}, u32[]{:S(2)}, u32[]{:S(2)}) %collective-permute-start.13) | collective-permute-done | bytes 491552 | tf_op jit(solution)/shard_map/ppermute | solution.py:22
  129.6 1.7 fusion.116
  131.8 3.2 %collective-permute-start.16 = (bf16[16,7680]{1,0:T(8,128)(2,1)S(1)}, bf16[16,7680]{1,0:T(8,128)(2,1)S(1)}, u32[]{:S(2)}, u32[]{:S(2)}) collective-permute-start(bf16[16,7680]{1,0:T(8,128)(2,1)S(1)} %multiply_convert_fusion), channel_id=1, source_target_pairs={{0,128},{64,192},{128,0},{192,64},{1,129},{65,193},{129,1},{193,65... | collective-permute-start | bytes 737288 | tf_op jit(solution)/shard_map/ppermute | solution.py:22
  135.1 2.3 %collective-permute-start.15 = (bf16[16,7680]{1,0:T(8,128)(2,1)S(1)}, bf16[16,7680]{1,0:T(8,128)(2,1)S(1)}, u32[]{:S(2)}, u32[]{:S(2)}) collective-permute-start(bf16[16,7680]{1,0:T(8,128)(2,1)S(1)} %multiply_convert_fusion), channel_id=1, source_target_pairs={{0,192},{64,0},{128,64},{192,128},{1,193},{65,1},{129,65},{193,129... | collective-permute-start | bytes 737288 | tf_op jit(solution)/shard_map/ppermute | solution.py:22
  138.3 2.4 %collective-permute-done.17 = bf16[16,7680]{1,0:T(8,128)(2,1)S(1)} collective-permute-done((bf16[16,7680]{1,0:T(8,128)(2,1)S(1)}, bf16[16,7680]{1,0:T(8,128)(2,1)S(1)}, u32[]{:S(2)}, u32[]{:S(2)}) %collective-permute-start.17) | collective-permute-done | bytes 245792 | tf_op jit(solution)/shard_map/ppermute | solution.py:22
  140.7 1.6 collective-permute-done.16
  142.3 3.4 %collective-permute-done.15 = bf16[16,7680]{1,0:T(8,128)(2,1)S(1)} collective-permute-done((bf16[16,7680]{1,0:T(8,128)(2,1)S(1)}, bf16[16,7680]{1,0:T(8,128)(2,1)S(1)}, u32[]{:S(2)}, u32[]{:S(2)}) %collective-permute-start.15) | collective-permute-done | bytes 245792 | tf_op jit(solution)/shard_map/ppermute | solution.py:22
  149.9 2.3 %collective-permute-start.19 = (bf16[16,4096]{1,0:T(8,128)(2,1)S(1)}, bf16[16,4096]{1,0:T(8,128)(2,1)S(1)}, u32[]{:S(2)}, u32[]{:S(2)}) collective-permute-start(bf16[16,4096]{1,0:T(8,128)(2,1)S(1)} %get-tuple-element.59), channel_id=1, source_target_pairs={{0,128},{64,192},{128,0},{192,64},{1,129},{65,193},{129,1},{193,65... | collective-permute-start | bytes 393224 | tf_op jit(solution)/shard_map/ppermute | solution.py:22
  152.3 1.6 collective-permute-done.18
  154.2 3.5 %collective-permute-done.19 = bf16[16,4096]{1,0:T(8,128)(2,1)S(1)} collective-permute-done((bf16[16,4096]{1,0:T(8,128)(2,1)S(1)}, bf16[16,4096]{1,0:T(8,128)(2,1)S(1)}, u32[]{:S(2)}, u32[]{:S(2)}) %collective-permute-start.19) | collective-permute-done | bytes 131104 | tf_op jit(solution)/shard_map/ppermute | solution.py:22
  157.8 2.0 collective-permute-start.23
  159.8 2.9 %collective-permute-start.22 = (bf16[16,4096]{1,0:T(8,128)(2,1)S(1)}, bf16[16,4096]{1,0:T(8,128)(2,1)S(1)}, u32[]{:S(2)}, u32[]{:S(2)}) collective-permute-start(bf16[16,4096]{1,0:T(8,128)(2,1)S(1)} %fusion.37), channel_id=1, source_target_pairs={{0,32},{16,48},{32,0},{48,16},{1,33},{17,49},{33,1},{49,17},{2,34}... | collective-permute-start | bytes 393224 | tf_op jit(solution)/shard_map/ppermute | solution.py:22
  164.0 2.2 fusion.47
  170.3 2.3 %collective-permute-start.11 = (bf16[64,4096]{1,0:T(8,128)(2,1)S(1)}, bf16[64,4096]{1,0:T(8,128)(2,1)S(1)}, u32[]{:S(2)}, u32[]{:S(2)}) collective-permute-start(bf16[64,4096]{1,0:T(8,128)(2,1)S(1)} %get-tuple-element.49), channel_id=1, source_target_pairs={{0,48},{16,0},{32,16},{48,32},{1,49},{17,1},{33,17},{49,33},{2,50}... | collective-permute-start | bytes 1572872 | tf_op jit(solution)/shard_map/ppermute | solution.py:22
  176.4 3.2 %collective-permute-start.26 = (bf16[161,1024]{1,0:T(8,128)(2,1)}, bf16[161,1024]{1,0:T(8,128)(2,1)}, u32[]{:S(2)}, u32[]{:S(2)}) collective-permute-start(bf16[161,1024]{1,0:T(8,128)(2,1)} %get-tuple-element.55), channel_id=1, source_target_pairs={{0,128},{64,192},{128,0},{192,64},{1,129},{65,193},{129,1},{193,65... | collective-permute-start | bytes 989192 | tf_op jit(solution)/shard_map/ppermute | solution.py:22
  179.7 5.3 %collective-permute-done.9 = bf16[64,4096]{1,0:T(8,128)(2,1)S(1)} collective-permute-done((bf16[64,4096]{1,0:T(8,128)(2,1)S(1)}, bf16[64,4096]{1,0:T(8,128)(2,1)S(1)}, u32[]{:S(2)}, u32[]{:S(2)}) %collective-permute-start.9) | collective-permute-done | bytes 524320 | tf_op jit(solution)/shard_map/ppermute | solution.py:22
  186.1 9.4 %collective-permute-done.11 = bf16[64,4096]{1,0:T(8,128)(2,1)S(1)} collective-permute-done((bf16[64,4096]{1,0:T(8,128)(2,1)S(1)}, bf16[64,4096]{1,0:T(8,128)(2,1)S(1)}, u32[]{:S(2)}, u32[]{:S(2)}) %collective-permute-start.11) | collective-permute-done | bytes 524320 | tf_op jit(solution)/shard_map/ppermute | solution.py:22
  195.4 1.5 collective-permute-done.10
  198.1 6.7 %all-to-all-start.4 = ((bf16[8,8,4096]{2,1,0:T(8,128)(2,1)}), bf16[8,8,4096]{2,1,0:T(8,128)(2,1)}, u32[]{:S(2)}, u32[]{:S(2)}) async-start(bf16[8,8,4096]{2,1,0:T(8,128)(2,1)} %fusion.29), calls=%async_computation.4 | async-start | bytes 1048576 | tf_op jit(solution)/shard_map/all_to_all | solution.py:30
  205.6 1.5 add_convert_fusion
  208.5 3.2 %fusion = bf16[1,256,7680]{2,1,0:T(8,128)(2,1)} fusion(bf16[16,7680]{1,0:T(8,128)(2,1)S(1)} %copy-done.16, bf16[16,7680]{1,0:T(8,128)(2,1)S(1)} %copy-done.18, bf16[16,7680]{1,0:T(8,128)(2,1)S(1)} %copy-done.20, bf16[16,7680]{1,0:T(8,128)(2,1)S(1)} %copy-done.11, s32[]{:T(128)S(6)} %select_n.212, bf16[64,256]{1,0:T(8,128)(2,1)S(1)} %fusion.15), kind=kOutput, calls=%fused_computation.1 | convolution fusion | flops 257622016 | bytes 4947972 | tf_op jit(solution)/shard_map/dot_general | solution.py:26
  211.7 3.1 %fusion.3 = bf16[1,4096,256]{2,1,0:T(8,128)(2,1)} fusion(bf16[64,256]{1,0:T(8,128)(2,1)S(1)} %fusion.12, s32[]{:T(128)S(6)} %select_n.212, bf16[64,4096]{1,0:T(8,128)(2,1)} %bitcast.13), kind=kOutput, calls=%fused_computation.8 | convolution fusion | flops 136314880 | bytes 2654212 | tf_op jit(solution)/shard_map/dot_general | solution.py:26
  214.8 7.5 %all-to-all-done.4 = bf16[8,8,4096]{2,1,0:T(8,128)(2,1)} async-done(((bf16[8,8,4096]{2,1,0:T(8,128)(2,1)}), bf16[8,8,4096]{2,1,0:T(8,128)(2,1)}, u32[]{:S(2)}, u32[]{:S(2)}) %all-to-all-start.4) | async-done | bytes 524320 | tf_op jit(solution)/shard_map/all_to_all | solution.py:30
  222.2 1.8 reduce_sum.75
  (164 shorter events, 50.3 us)
Async XLA Ops:
  0.6 96.6 %copy-start = (bf16[1,4096,256]{2,1,0:T(8,128)(2,1)S(1)}, bf16[1,4096,256]{2,1,0:T(8,128)(2,1)}, u32[]{:S(2)}) copy-start(bf16[1,4096,256]{2,1,0:T(8,128)(2,1)} %param.18) | copy-start | bytes 6291460
  1.5 18.6 %collective-permute-start.2 = (bf16[8,1408]{1,0:T(8,128)(2,1)S(1)}, bf16[8,1408]{1,0:T(8,128)(2,1)S(1)}, u32[]{:S(2)}, u32[]{:S(2)}) collective-permute-start(bf16[8,1408]{1,0:T(8,128)(2,1)S(1)} %slice.120), channel_id=1, source_target_pairs={{0,16},{16,32},{32,48},{48,0},{1,17},{17,33},{33,49},{49,1},{2,18}... | collective-permute-start | bytes 67592 | tf_op jit(solution)/shard_map/ppermute | solution.py:22
  3.0 17.1 %collective-permute-start.1 = (bf16[8,1408]{1,0:T(8,128)(2,1)S(1)}, bf16[8,1408]{1,0:T(8,128)(2,1)S(1)}, u32[]{:S(2)}, u32[]{:S(2)}) collective-permute-start(bf16[8,1408]{1,0:T(8,128)(2,1)S(1)} %slice.120), channel_id=1, source_target_pairs={{0,32},{16,48},{32,0},{48,16},{1,33},{17,49},{33,1},{49,17},{2,34}... | collective-permute-start | bytes 67592 | tf_op jit(solution)/shard_map/ppermute | solution.py:22
  5.8 14.4 %collective-permute-start = (bf16[8,1408]{1,0:T(8,128)(2,1)S(1)}, bf16[8,1408]{1,0:T(8,128)(2,1)}, u32[]{:S(2)}, u32[]{:S(2)}) collective-permute-start(bf16[8,1408]{1,0:T(8,128)(2,1)S(1)} %slice.120), channel_id=1, source_target_pairs={{0,48},{16,0},{32,16},{48,32},{1,49},{17,1},{33,17},{49,33},{2,50}... | collective-permute-start | bytes 67592 | tf_op jit(solution)/shard_map/ppermute | solution.py:22
  10.2 21.7 %all-to-all-start = ((bf16[8,8,2816]{2,1,0:T(8,128)(2,1)}), bf16[8,8,2816]{2,1,0:T(8,128)(2,1)}, u32[]{:S(2)}, u32[]{:S(2)}) async-start(bf16[8,8,2816]{2,1,0:T(8,128)(2,1)} %broadcast_in_dim.84), calls=%async_computation | async-start | bytes 720896 | tf_op jit(solution)/shard_map/all_to_all | solution.py:30
  31.9 11.6 %collective-permute-start.3 = (bf16[64,2816]{1,0:T(8,128)(2,1)}, bf16[64,2816]{1,0:T(8,128)(2,1)}, u32[]{:S(2)}, u32[]{:S(2)}) collective-permute-start(bf16[64,2816]{1,0:T(8,128)(2,1)} %bitcast.4), channel_id=1, source_target_pairs={{0,48},{16,0},{32,16},{48,32},{1,49},{17,1},{33,17},{49,33},{2,50}... | collective-permute-start | bytes 1081352 | tf_op jit(solution)/shard_map/ppermute | solution.py:22
  32.3 13.1 %collective-permute-start.4 = (bf16[64,2816]{1,0:T(8,128)(2,1)}, bf16[64,2816]{1,0:T(8,128)(2,1)}, u32[]{:S(2)}, u32[]{:S(2)}) collective-permute-start(bf16[64,2816]{1,0:T(8,128)(2,1)} %bitcast.4), channel_id=1, source_target_pairs={{0,32},{16,48},{32,0},{48,16},{1,33},{17,49},{33,1},{49,17},{2,34}... | collective-permute-start | bytes 1081352 | tf_op jit(solution)/shard_map/ppermute | solution.py:22
  34.7 14.7 %collective-permute-start.5 = (bf16[64,2816]{1,0:T(8,128)(2,1)}, bf16[64,2816]{1,0:T(8,128)(2,1)}, u32[]{:S(2)}, u32[]{:S(2)}) collective-permute-start(bf16[64,2816]{1,0:T(8,128)(2,1)} %bitcast.4), channel_id=1, source_target_pairs={{0,16},{16,32},{32,48},{48,0},{1,17},{17,33},{33,49},{49,1},{2,18}... | collective-permute-start | bytes 1081352 | tf_op jit(solution)/shard_map/ppermute | solution.py:22
  36.5 23.2 %all-to-all-start.1 = ((bf16[8,32,1408]{2,1,0:T(8,128)(2,1)}), bf16[8,32,1408]{2,1,0:T(8,128)(2,1)}, u32[]{:S(2)}, u32[]{:S(2)}) async-start(bf16[8,32,1408]{2,1,0:T(8,128)(2,1)} %broadcast_in_dim.85), calls=%async_computation.1 | async-start | bytes 1441792 | tf_op jit(solution)/shard_map/all_to_all | solution.py:30
  44.5 17.3 %copy-start.21 = (bf16[4096,1]{0,1:T(2,128)(2,1)S(1)}, bf16[4096,1]{0,1:T(2,128)(2,1)}, u32[]{:S(2)}) copy-start(bf16[4096,1]{0,1:T(2,128)(2,1)} %param.17) | copy-start | bytes 24580
  59.6 2.2 copy-start.7
  61.8 5.9 %collective-permute-start.7 = (bf16[256,4224]{1,0:T(8,128)(2,1)}, bf16[256,4224]{1,0:T(8,128)(2,1)}, u32[]{:S(2)}, u32[]{:S(2)}) collective-permute-start(bf16[256,4224]{1,0:T(8,128)(2,1)} %constant_dynamic-update-slice_fusion.6), channel_id=1, source_target_pairs={{0,1},{1,0},{2,3},{3,2},{4,5},{5,4},{6,7},{7,6},{8,9},{9,8},{10,11... | collective-permute-start | bytes 6488072 | tf_op jit(solution)/shard_map/ppermute | solution.py:22
  62.1 4.2 %collective-permute-start.6 = (f32[2,256]{1,0:T(2,128)S(1)}, f32[2,256]{1,0:T(2,128)S(1)}, u32[]{:S(2)}, u32[]{:S(2)}) collective-permute-start(f32[2,256]{1,0:T(2,128)S(1)} %get-tuple-element.69), channel_id=1, source_target_pairs={{0,1},{1,0},{2,3},{3,2},{4,5},{5,4},{6,7},{7,6},{8,9},{9,8},{10,11... | collective-permute-start | bytes 6152 | tf_op jit(solution)/shard_map/ppermute | solution.py:22
  67.2 2.7 %copy-start.2 = (bf16[256,4224]{1,0:T(8,128)(2,1)S(1)}, bf16[256,4224]{1,0:T(8,128)(2,1)}, u32[]{:S(2)}) copy-start(bf16[256,4224]{1,0:T(8,128)(2,1)} %constant_dynamic-update-slice_fusion.6) | copy-start | bytes 6488068
  72.1 2.7 %copy-start.8 = (f32[256,161]{0,1:T(8,128)}, f32[256,161]{0,1:T(8,128)S(1)}, u32[]{:S(2)}) copy-start(f32[256,161]{0,1:T(8,128)S(1)} %fusion.24) | copy-start | bytes 494596
  77.3 13.3 %all-to-all-start.3 = ((bf16[4,16,4096]{2,1,0:T(8,128)(2,1)}), bf16[4,16,4096]{2,1,0:T(8,128)(2,1)}, u32[]{:S(2)}, u32[]{:S(2)}) async-start(bf16[4,16,4096]{2,1,0:T(8,128)(2,1)} %broadcast_in_dim.93), calls=%async_computation.3 | async-start | bytes 1048576 | tf_op jit(solution)/shard_map/all_to_all | solution.py:30
  91.4 17.6 %all-to-all-start.2 = ((f32[64,2,512]{2,1,0:T(2,128)}), f32[64,2,512]{2,1,0:T(2,128)}, u32[]{:S(2)}, u32[]{:S(2)}) async-start(f32[64,2,512]{2,1,0:T(2,128)} %broadcast_in_dim.89), calls=%async_computation.2 | async-start | bytes 524288 | tf_op jit(solution)/shard_map/all_to_all | solution.py:30
  104.1 14.4 %collective-permute-start.12 = (f32[16,7680]{1,0:T(8,128)}, f32[16,7680]{1,0:T(8,128)}, u32[]{:S(2)}, u32[]{:S(2)}) collective-permute-start(f32[16,7680]{1,0:T(8,128)} %get-tuple-element.51), channel_id=1, source_target_pairs={{0,64},{64,128},{128,192},{192,0},{1,65},{65,129},{129,193},{193,1... | collective-permute-start | bytes 1474568 | tf_op jit(solution)/shard_map/ppermute | solution.py:22
  104.1 14.4 %collective-permute-start.14 = (f32[16,7680]{1,0:T(8,128)}, f32[16,7680]{1,0:T(8,128)}, u32[]{:S(2)}, u32[]{:S(2)}) collective-permute-start(f32[16,7680]{1,0:T(8,128)} %get-tuple-element.52), channel_id=1, source_target_pairs={{0,192},{64,0},{128,64},{192,128},{1,193},{65,1},{129,65},{193,129... | collective-permute-start | bytes 1474568 | tf_op jit(solution)/shard_map/ppermute | solution.py:22
  106.1 23.4 %collective-permute-start.13 = (f32[16,7680]{1,0:T(8,128)}, f32[16,7680]{1,0:T(8,128)}, u32[]{:S(2)}, u32[]{:S(2)}) collective-permute-start(f32[16,7680]{1,0:T(8,128)} %get-tuple-element.53), channel_id=1, source_target_pairs={{0,128},{64,192},{128,0},{192,64},{1,129},{65,193},{129,1},{193,65... | collective-permute-start | bytes 1474568 | tf_op jit(solution)/shard_map/ppermute | solution.py:22
  131.5 14.2 %copy-start.6 = (bf16[1,256,7680]{2,1,0:T(8,128)(2,1)S(1)}, bf16[1,256,7680]{2,1,0:T(8,128)(2,1)}, u32[]{:S(2)}) copy-start(bf16[1,256,7680]{2,1,0:T(8,128)(2,1)} %param.19) | copy-start | bytes 11796484
  131.7 15.2 %copy-start.10 = (bf16[16,7680]{1,0:T(8,128)(2,1)}, bf16[16,7680]{1,0:T(8,128)(2,1)S(1)}, u32[]{:S(2)}) copy-start(bf16[16,7680]{1,0:T(8,128)(2,1)S(1)} %multiply_convert_fusion) | copy-start | bytes 737284
  131.7 8.9 %collective-permute-start.17 = (bf16[16,7680]{1,0:T(8,128)(2,1)S(1)}, bf16[16,7680]{1,0:T(8,128)(2,1)S(1)}, u32[]{:S(2)}, u32[]{:S(2)}) collective-permute-start(bf16[16,7680]{1,0:T(8,128)(2,1)S(1)} %multiply_convert_fusion), channel_id=1, source_target_pairs={{0,64},{64,128},{128,192},{192,0},{1,65},{65,129},{129,193},{193,1... | collective-permute-start | bytes 737288 | tf_op jit(solution)/shard_map/ppermute | solution.py:22
  131.8 10.5 %collective-permute-start.16 = (bf16[16,7680]{1,0:T(8,128)(2,1)S(1)}, bf16[16,7680]{1,0:T(8,128)(2,1)S(1)}, u32[]{:S(2)}, u32[]{:S(2)}) collective-permute-start(bf16[16,7680]{1,0:T(8,128)(2,1)S(1)} %multiply_convert_fusion), channel_id=1, source_target_pairs={{0,128},{64,192},{128,0},{192,64},{1,129},{65,193},{129,1},{193,65... | collective-permute-start | bytes 737288 | tf_op jit(solution)/shard_map/ppermute | solution.py:22
  135.1 10.6 %collective-permute-start.15 = (bf16[16,7680]{1,0:T(8,128)(2,1)S(1)}, bf16[16,7680]{1,0:T(8,128)(2,1)S(1)}, u32[]{:S(2)}, u32[]{:S(2)}) collective-permute-start(bf16[16,7680]{1,0:T(8,128)(2,1)S(1)} %multiply_convert_fusion), channel_id=1, source_target_pairs={{0,192},{64,0},{128,64},{192,128},{1,193},{65,1},{129,65},{193,129... | collective-permute-start | bytes 737288 | tf_op jit(solution)/shard_map/ppermute | solution.py:22
  138.2 30.2 %collective-permute-start.8 = (bf16[256,4096]{1,0:T(8,128)(2,1)S(1)}, bf16[256,4096]{1,0:T(8,128)(2,1)S(1)}, u32[]{:S(2)}, u32[]{:S(2)}) collective-permute-start(bf16[256,4096]{1,0:T(8,128)(2,1)S(1)} %convolution_convert_fusion.2), channel_id=1, source_target_pairs={{0,1},{1,0},{2,3},{3,2},{4,5},{5,4},{6,7},{7,6},{8,9},{9,8},{10,11... | collective-permute-start | bytes 6291464 | tf_op jit(solution)/shard_map/ppermute | solution.py:22
  140.7 6.3 %copy-start.15 = (bf16[16,7680]{1,0:T(8,128)(2,1)}, bf16[16,7680]{1,0:T(8,128)(2,1)S(1)}, u32[]{:S(2)}) copy-start(bf16[16,7680]{1,0:T(8,128)(2,1)S(1)} %collective-permute-done.17) | copy-start | bytes 737284
  142.3 4.7 %copy-start.17 = (bf16[16,7680]{1,0:T(8,128)(2,1)}, bf16[16,7680]{1,0:T(8,128)(2,1)S(1)}, u32[]{:S(2)}) copy-start(bf16[16,7680]{1,0:T(8,128)(2,1)S(1)} %collective-permute-done.16) | copy-start | bytes 737284
  147.8 6.1 %collective-permute-start.18 = (bf16[16,4096]{1,0:T(8,128)(2,1)S(1)}, bf16[16,4096]{1,0:T(8,128)(2,1)S(1)}, u32[]{:S(2)}, u32[]{:S(2)}) collective-permute-start(bf16[16,4096]{1,0:T(8,128)(2,1)S(1)} %get-tuple-element.57), channel_id=1, source_target_pairs={{0,64},{64,128},{128,192},{192,0},{1,65},{65,129},{129,193},{193,1... | collective-permute-start | bytes 393224 | tf_op jit(solution)/shard_map/ppermute | solution.py:22
  148.5 5.7 %collective-permute-start.20 = (bf16[16,4096]{1,0:T(8,128)(2,1)S(1)}, bf16[16,4096]{1,0:T(8,128)(2,1)S(1)}, u32[]{:S(2)}, u32[]{:S(2)}) collective-permute-start(bf16[16,4096]{1,0:T(8,128)(2,1)S(1)} %get-tuple-element.58), channel_id=1, source_target_pairs={{0,192},{64,0},{128,64},{192,128},{1,193},{65,1},{129,65},{193,129... | collective-permute-start | bytes 393224 | tf_op jit(solution)/shard_map/ppermute | solution.py:22
  149.9 7.8 %collective-permute-start.19 = (bf16[16,4096]{1,0:T(8,128)(2,1)S(1)}, bf16[16,4096]{1,0:T(8,128)(2,1)S(1)}, u32[]{:S(2)}, u32[]{:S(2)}) collective-permute-start(bf16[16,4096]{1,0:T(8,128)(2,1)S(1)} %get-tuple-element.59), channel_id=1, source_target_pairs={{0,128},{64,192},{128,0},{192,64},{1,129},{65,193},{129,1},{193,65... | collective-permute-start | bytes 393224 | tf_op jit(solution)/shard_map/ppermute | solution.py:22
  157.8 8.4 %collective-permute-start.23 = (bf16[16,4096]{1,0:T(8,128)(2,1)S(1)}, bf16[16,4096]{1,0:T(8,128)(2,1)S(1)}, u32[]{:S(2)}, u32[]{:S(2)}) collective-permute-start(bf16[16,4096]{1,0:T(8,128)(2,1)S(1)} %fusion.37), channel_id=1, source_target_pairs={{0,16},{16,32},{32,48},{48,0},{1,17},{17,33},{33,49},{49,1},{2,18}... | collective-permute-start | bytes 393224 | tf_op jit(solution)/shard_map/ppermute | solution.py:22
  159.8 7.4 %collective-permute-start.22 = (bf16[16,4096]{1,0:T(8,128)(2,1)S(1)}, bf16[16,4096]{1,0:T(8,128)(2,1)S(1)}, u32[]{:S(2)}, u32[]{:S(2)}) collective-permute-start(bf16[16,4096]{1,0:T(8,128)(2,1)S(1)} %fusion.37), channel_id=1, source_target_pairs={{0,32},{16,48},{32,0},{48,16},{1,33},{17,49},{33,1},{49,17},{2,34}... | collective-permute-start | bytes 393224 | tf_op jit(solution)/shard_map/ppermute | solution.py:22
  162.7 5.0 %collective-permute-start.21 = (bf16[16,4096]{1,0:T(8,128)(2,1)S(1)}, bf16[16,4096]{1,0:T(8,128)(2,1)S(1)}, u32[]{:S(2)}, u32[]{:S(2)}) collective-permute-start(bf16[16,4096]{1,0:T(8,128)(2,1)S(1)} %fusion.37), channel_id=1, source_target_pairs={{0,48},{16,0},{32,16},{48,32},{1,49},{17,1},{33,17},{49,33},{2,50}... | collective-permute-start | bytes 393224 | tf_op jit(solution)/shard_map/ppermute | solution.py:22
  168.1 8.3 %collective-permute-start.24 = (bf16[64,4096]{1,0:T(8,128)(2,1)S(1)}, bf16[64,4096]{1,0:T(8,128)(2,1)S(1)}, u32[]{:S(2)}, u32[]{:S(2)}) collective-permute-start(bf16[64,4096]{1,0:T(8,128)(2,1)S(1)} %convolution_convert_fusion.3), channel_id=1, source_target_pairs={{0,1},{1,0},{2,3},{3,2},{4,5},{5,4},{6,7},{7,6},{8,9},{9,8},{10,11... | collective-permute-start | bytes 1572872 | tf_op jit(solution)/shard_map/ppermute | solution.py:22
  169.2 4.5 %copy-start.3 = (bf16[256,4224]{1,0:T(8,128)(2,1)S(1)}, bf16[256,4224]{1,0:T(8,128)(2,1)}, u32[]{:S(2)}) copy-start(bf16[256,4224]{1,0:T(8,128)(2,1)} %constant_dynamic-update-slice_fusion.6) | copy-start | bytes 6488068
  169.3 15.6 %collective-permute-start.9 = (bf16[64,4096]{1,0:T(8,128)(2,1)S(1)}, bf16[64,4096]{1,0:T(8,128)(2,1)S(1)}, u32[]{:S(2)}, u32[]{:S(2)}) collective-permute-start(bf16[64,4096]{1,0:T(8,128)(2,1)S(1)} %get-tuple-element.48), channel_id=1, source_target_pairs={{0,16},{16,32},{32,48},{48,0},{1,17},{17,33},{33,49},{49,1},{2,18}... | collective-permute-start | bytes 1572872 | tf_op jit(solution)/shard_map/ppermute | solution.py:22
  170.3 25.2 %collective-permute-start.11 = (bf16[64,4096]{1,0:T(8,128)(2,1)S(1)}, bf16[64,4096]{1,0:T(8,128)(2,1)S(1)}, u32[]{:S(2)}, u32[]{:S(2)}) collective-permute-start(bf16[64,4096]{1,0:T(8,128)(2,1)S(1)} %get-tuple-element.49), channel_id=1, source_target_pairs={{0,48},{16,0},{32,16},{48,32},{1,49},{17,1},{33,17},{49,33},{2,50}... | collective-permute-start | bytes 1572872 | tf_op jit(solution)/shard_map/ppermute | solution.py:22
  172.6 24.3 %collective-permute-start.10 = (bf16[64,4096]{1,0:T(8,128)(2,1)S(1)}, bf16[64,4096]{1,0:T(8,128)(2,1)S(1)}, u32[]{:S(2)}, u32[]{:S(2)}) collective-permute-start(bf16[64,4096]{1,0:T(8,128)(2,1)S(1)} %get-tuple-element.50), channel_id=1, source_target_pairs={{0,32},{16,48},{32,0},{48,16},{1,33},{17,49},{33,1},{49,17},{2,34}... | collective-permute-start | bytes 1572872 | tf_op jit(solution)/shard_map/ppermute | solution.py:22
  174.3 1.4 copy-start.5
  175.7 29.2 %collective-permute-start.25 = (bf16[161,1024]{1,0:T(8,128)(2,1)}, bf16[161,1024]{1,0:T(8,128)(2,1)S(1)}, u32[]{:S(2)}, u32[]{:S(2)}) collective-permute-start(bf16[161,1024]{1,0:T(8,128)(2,1)} %get-tuple-element.54), channel_id=1, source_target_pairs={{0,64},{64,128},{128,192},{192,0},{1,65},{65,129},{129,193},{193,1... | collective-permute-start | bytes 989192 | tf_op jit(solution)/shard_map/ppermute | solution.py:22
  176.4 28.5 %collective-permute-start.26 = (bf16[161,1024]{1,0:T(8,128)(2,1)}, bf16[161,1024]{1,0:T(8,128)(2,1)}, u32[]{:S(2)}, u32[]{:S(2)}) collective-permute-start(bf16[161,1024]{1,0:T(8,128)(2,1)} %get-tuple-element.55), channel_id=1, source_target_pairs={{0,128},{64,192},{128,0},{192,64},{1,129},{65,193},{129,1},{193,65... | collective-permute-start | bytes 989192 | tf_op jit(solution)/shard_map/ppermute | solution.py:22
  184.9 20.7 %collective-permute-start.27 = (bf16[161,1024]{1,0:T(8,128)(2,1)}, bf16[161,1024]{1,0:T(8,128)(2,1)}, u32[]{:S(2)}, u32[]{:S(2)}) collective-permute-start(bf16[161,1024]{1,0:T(8,128)(2,1)} %get-tuple-element.56), channel_id=1, source_target_pairs={{0,192},{64,0},{128,64},{192,128},{1,193},{65,1},{129,65},{193,129... | collective-permute-start | bytes 989192 | tf_op jit(solution)/shard_map/ppermute | solution.py:22
  198.1 24.1 %all-to-all-start.4 = ((bf16[8,8,4096]{2,1,0:T(8,128)(2,1)}), bf16[8,8,4096]{2,1,0:T(8,128)(2,1)}, u32[]{:S(2)}, u32[]{:S(2)}) async-start(bf16[8,8,4096]{2,1,0:T(8,128)(2,1)} %fusion.29), calls=%async_computation.4 | async-start | bytes 1048576 | tf_op jit(solution)/shard_map/all_to_all | solution.py:30
  204.8 3.6 %copy-start.11 = (bf16[16,7680]{1,0:T(8,128)(2,1)S(1)}, bf16[16,7680]{1,0:T(8,128)(2,1)}, u32[]{:S(2)}) copy-start(bf16[16,7680]{1,0:T(8,128)(2,1)} %copy-done.10) | copy-start | bytes 737284
  204.8 3.6 %copy-start.16 = (bf16[16,7680]{1,0:T(8,128)(2,1)S(1)}, bf16[16,7680]{1,0:T(8,128)(2,1)}, u32[]{:S(2)}) copy-start(bf16[16,7680]{1,0:T(8,128)(2,1)} %copy-done.15) | copy-start | bytes 737284
  204.8 3.6 %copy-start.18 = (bf16[16,7680]{1,0:T(8,128)(2,1)S(1)}, bf16[16,7680]{1,0:T(8,128)(2,1)}, u32[]{:S(2)}) copy-start(bf16[16,7680]{1,0:T(8,128)(2,1)} %copy-done.17) | copy-start | bytes 737284
  204.9 3.6 %copy-start.20 = (bf16[16,7680]{1,0:T(8,128)(2,1)S(1)}, bf16[16,7680]{1,0:T(8,128)(2,1)}, u32[]{:S(2)}) copy-start(bf16[16,7680]{1,0:T(8,128)(2,1)} %copy-done.19) | copy-start | bytes 737284
  (7 other events, 7.9 us)

commit v4 on v3

--- a/solution.py
+++ b/solution.py
@@ -11,7 +11,7 @@
 OWN = 8
 NX, NZ, NDP = 4, 8, 4
 META = 128
-CA = 1408
+CA = 1536
 
 
 F32, BF16 = jnp.float32, jnp.bfloat16
@@ -20,6 +20,11 @@
 def shift(value, axis, step):
     n = lax.axis_size(axis)
     return lax.ppermute(value, axis, [(j, (j + step) % n) for j in range(n)])
+
+
+def swap(value, axis, bits):
+    n = lax.axis_size(axis)
+    return lax.ppermute(value, axis, [(j, j ^ bits) for j in range(n)])
 
 
 def dot(a, b, ca=1, cb=0):
@@ -48,11 +53,12 @@
     rest = model - CA
     a1 = hidden[:, :CA]
     pay = jnp.concatenate([hidden[:, CA:], jnp.pad(digits, ((0, 0), (0, META - 4)))], axis=1)
-    a1 = jnp.concatenate([a1] + [shift(a1, "x", -k) for k in range(1, NX)], axis=0)
+    a1 = jnp.concatenate([a1, swap(a1, "x", 1)], axis=0)
+    a1 = jnp.concatenate([a1, swap(a1, "x", 2)], axis=0)
     b1 = from_everyone(pay, "z").reshape(NZ * OWN, -1)
     a1, b1 = lax.optimization_barrier((a1, b1))
     a2 = from_everyone(a1, "z").reshape(NZ, NX, OWN, CA)
-    b2 = [b1] + [shift(b1, "x", -k) for k in range(1, NX)]
+    b2 = [b1] + [swap(b1, "x", k) for k in range(1, NX)]
     own = jnp.zeros((NX * NZ * OWN, model + META), BF16)
     for k in range(NX):
         own = lax.dynamic_update_slice(own, b2[k], (k * NZ * OWN, 0))
@@ -77,19 +83,19 @@
 
 
 def joined_stats(top, total):
-    first = lax.axis_index("core") == 0
-    place = lax.axis_index("x")
-
-    def turned(stats, start):
-        stats = jnp.where(first, stats, stats[:, ::-1])
-        return lax.dynamic_slice_in_dim(jnp.concatenate([stats] * 2, axis=2), start, NX, 2)
-
-    shape = (2, 2, NX, NZ * OWN)
-    stats = turned(jnp.stack([top, total]).reshape(shape), lax.rem(NX - place, NX))
+    core, place = lax.axis_index("core"), lax.axis_index("x")
+
+    def turned(stats):
+        stats = stats.reshape(2, 2, 2, 2, NZ * OWN)
+        stats = jnp.where(core == 0, stats, stats[:, ::-1])
+        stats = jnp.where(place < 2, stats, stats[:, :, ::-1])
+        return jnp.where(place % 2 == 0, stats, stats[:, :, :, ::-1])
+
+    stats = turned(jnp.stack([top, total]))
     every = from_everyone(stats.reshape(2, -1), ("x", "z", "core"))
     top = jnp.max(every[:, 0], axis=0)
     total = jnp.sum(every[:, 1] * jnp.exp(every[:, 0] - top), axis=0)
-    stats = turned(jnp.stack([top, total]).reshape(shape), place).reshape(2, -1)
+    stats = turned(jnp.stack([top, total])).reshape(2, -1)
     return stats[0], stats[1]
 
 
@@ -108,7 +114,7 @@
     offset = target - HEAD
     cluster = jnp.where(offset >= 0, offset // CV, -1)
     core_at, x_at, z_at, row_at = jnp.unravel_index(jnp.arange(2 * side), (2, NX, NZ, OWN))
-    x_at = lax.rem(x_at + x_index, NX)
+    x_at = lax.bitwise_xor(x_at, x_index)
     token = ((x_at * NZ + z_at) * 2 + lax.bitwise_xor(core_at, core_index)) * OWN + row_at
     earlier = (cluster[:, None] == cluster[None, :]) & (token[:, None] < token[None, :])
     rank = jnp.sum(earlier.astype(jnp.int32), axis=0)
@@ -120,19 +126,15 @@
 
     select = holds.astype(BF16)
     picked = plain((dot(select[:, :side], own) + dot(select[:, side:], other)).astype(BF16))
-    rows = from_everyone(picked, "dp")
-    rows = rows.reshape(NDP * CAP, -1)
+    rows = jnp.concatenate([picked] + [shift(picked, "dp", -k) for k in range(1, NDP)], axis=0)
     proj = tail_proj[0]
     out = tail_out[0]
     reduced = dot(rows, proj).astype(BF16)
     partial = dot(reduced, out)
 
-    def block(value, k, size, dim):
-        return lax.dynamic_slice_in_dim(value, lax.rem(dp_index + k, NDP) * size, size, dim)
-
-    share = block(partial, 0, CAP, 0)
+    share = partial[:CAP]
     for k in range(1, NDP):
-        share = share + shift(block(partial, k, CAP, 0), "dp", k)
+        share = share + shift(partial[k * CAP : (k + 1) * CAP], "dp", k)
     top = jnp.max(share, axis=1, keepdims=True)
     share_exp = jnp.exp(share - top)
     total = jnp.sum(share_exp, axis=1, keepdims=True)
@@ -166,14 +168,14 @@
     from_core = shift(far_part, "core", 1)
     pair = (dot(near, weight, 1, 1) + from_core.astype(F32)).reshape(NX, NZ * OWN, model)
     pair_16 = pair.astype(BF16)
-    from_x = [shift(pair_16[k], "x", k) for k in range(1, NX)]
+    from_x = [swap(pair_16[k], "x", k) for k in range(1, NX)]
     chip = pair[0]
     for piece in from_x:
         chip = chip + piece.astype(F32)
 
-    tail_all = [tail_sum] + [shift(tail_sum, "x", -k) for k in range(1, NX)]
+    tail_all = [tail_sum] + [swap(tail_sum, "x", k) for k in range(1, NX)]
     near_slot = slot.reshape(2, NX, NZ * OWN)[:, 0].reshape(-1)
-    source_x = lax.rem(x_index + jnp.arange(NX, dtype=jnp.int32), NX)
+    source_x = lax.bitwise_xor(x_index, jnp.arange(NX, dtype=jnp.int32))
     source = (source_x * NZ + z_index) * 2 + core_index
     source_slot = (source[:, None] * CAP + caps[None, :]).reshape(-1)
     place = (source_slot[:, None] == near_slot[None, :]).astype(BF16)
@@ -181,25 +183,26 @@
     rest = NZ * OWN
     far_tail = dot(place[:, rest:], tail_all, 0, 0).astype(BF16)
     tail_from_core = shift(far_tail, "core", 1)
-    chip = chip + dot(place[:, :rest], tail_all, 0, 0) + tail_from_core.astype(F32)
+    chip = lax.optimization_barrier(chip + dot(place[:, :rest], tail_all, 0, 0))
+    chip = chip + tail_from_core.astype(F32)
     last = swapped(chip.reshape(NZ, OWN, model).astype(BF16), "z")
     hidden_grad = jnp.sum(last.astype(F32), axis=0).astype(BF16)
 
     grad_t = (dot(near, own, 0, 0) + dot(far, other, 0, 0)).astype(BF16)
     grad_t = plain(grad_t)
-    pieces = [block(grad_t, k, model // NDP, 1) for k in range(NDP)]
-    head_sum = pieces[0].astype(F32)
-    for k in range(1, NDP):
-        head_sum = head_sum + shift(pieces[k], "dp", k).astype(F32)
-    head_sum = head_sum.astype(BF16)
-
-    def turned(value):
-        return lax.dynamic_slice_in_dim(
-            jnp.concatenate([value] * 2), dp_index * CAP, NDP * CAP
-        )
-
-    out_grad = dot(turned(reduced), word_delta, 0, 0).astype(BF16)
-    proj_grad = dot(turned(rows), reduced_grad, 0, 0).astype(BF16)
+    block = model // NDP
+    pieces = [
+        lax.dynamic_slice_in_dim(grad_t, lax.bitwise_xor(dp_index, k) * block, block, 1)
+        for k in range(NDP)
+    ]
+    pair = jnp.stack([pieces[1], pieces[3]])
+    pair = swap(pair, "dp", 1).astype(F32)
+    near_sum = pieces[0].astype(F32) + pair[0]
+    far_sum = (pieces[2].astype(F32) + pair[1]).astype(BF16)
+    far_sum = swap(far_sum, "dp", 2).astype(F32)
+    head_sum = (near_sum + far_sum).astype(BF16)
+    out_grad = dot(reduced, word_delta, 0, 0).astype(BF16)
+    proj_grad = dot(rows, reduced_grad, 0, 0).astype(BF16)
     return (
         hidden_grad,
         head_sum[:width].T,

time: 227 us -> 229 us (level)
  waiting for transfers between devices: 88.5 us -> 71.8 us
  local copies, waits for them, and re-layouts: 24.5 us -> 38.5 us
  other arithmetic: 17.6 us -> 24.4 us
  starting transfers between devices: 68.3 us -> 65.3 us
    ppermute x28 -> x16, waiting for transfers between devices: 53.7 us -> 15.2 us  [shift(): return lax.ppermute(value, axis, [(j, (j + step) % n) for j in range(n)])]
    ppermute x0 -> x13, waiting for transfers between devices: none -> 35.4 us  [swap(): return lax.ppermute(value, axis, [(j, j ^ bits) for j in range(n)])]
    ppermute x0 -> x13, starting transfers between devices: none -> 18.4 us  [swap(): return lax.ppermute(value, axis, [(j, j ^ bits) for j in range(n)])]
    ppermute x28 -> x16, starting transfers between devices: 38.2 us -> 19.9 us  [shift(): return lax.ppermute(value, axis, [(j, (j + step) % n) for j in range(n)])]
    all_to_all x5 -> x4, waiting for transfers between devices: 34.8 us -> 21.2 us  [swapped(): return lax.all_to_all(parts, axis, split_axis=0, concat_axis=0, tiled=True)]
    another operation x6 -> x7, local copies, waits for them, and re-layouts: 0.35 us -> 7.44 us  [the longest x3 3.4 us: joined_stats(): stats = turned(jnp.stack([top, total]))]
    select_n x3 -> x7, other arithmetic: 0.05 us -> 3.94 us  [the longest x2 2.16 us: turned(): return jnp.where(place % 2 == 0, stats, stats[:, :, :, ::-1])]
    all_to_all x5 -> x4, starting transfers between devices: 30.1 us -> 27.1 us  [swapped(): return lax.all_to_all(parts, axis, split_axis=0, concat_axis=0, tiled=True)]
  transfers between devices with their start and end apart: 33 -> 33, of which waited for: 22 -> 19; matrix products, arithmetic and copies ran while one was open for 20% -> 32% of each run, Pallas kernels for 0% -> 0%
where the time goes in v4:
time: 229 us; the launch traced here: 227 us
  waiting for transfers between devices  71.8 us (31%)
  starting transfers between devices  65.3 us (29%)
  local copies, waits for them, and re-layouts  38.5 us (17%)
  matrix products  25.5 us (11%)
  other arithmetic  24.4 us (11%)
    ppermute x13, waiting for transfers between devices, swap(): return lax.ppermute(value, axis, [(j, j ^ bits) for j in range(n)])  35.4 us
    all_to_all x4, starting transfers between devices, swapped(): return lax.all_to_all(parts, axis, split_axis=0, concat_axis=0, tiled=True)  27.1 us
    dot_general x16, matrix products, dot(): lax.dot_general(a, b, (((ca,), (cb,)), ((), ())), preferred_element_type=...  25.5 us
    all_to_all x4, waiting for transfers between devices, swapped(): return lax.all_to_all(parts, axis, split_axis=0, concat_axis=0, tiled=True)  21.2 us
    ppermute x16, starting transfers between devices, shift(): return lax.ppermute(value, axis, [(j, (j + step) % n) for j in range(n)])  19.9 us
    ppermute x13, starting transfers between devices, swap(): return lax.ppermute(value, axis, [(j, j ^ bits) for j in range(n)])  18.4 us
    ppermute x16, waiting for transfers between devices, shift(): return lax.ppermute(value, axis, [(j, (j + step) % n) for j in range(n)])  15.2 us
    unnamed x72, local copies, waits for them, and re-layouts  8 us
  transfers between devices with their start and end apart: 33, of which 19 were waited for; matrix products, arithmetic and copies ran while one was open for 32% of the time, Pallas kernels for 0%

profile of v4, /device:TPU:8, one launch (start us, length us, event | category | flops | bytes accessed | tf_op | source)
XLA Modules:
  0.0 226.9 jit_solution(15216427603142944682)
XLA Ops:
  1.5 1.5 collective-permute-start
  6.0 8.5 %all-to-all-start = ((bf16[8,8,2688]{2,1,0:T(8,128)(2,1)}), bf16[8,8,2688]{2,1,0:T(8,128)(2,1)}, u32[]{:S(2)}, u32[]{:S(2)}) async-start(bf16[8,8,2688]{2,1,0:T(8,128)(2,1)} %broadcast_in_dim.81), calls=%async_computation | async-start | bytes 688128 | tf_op jit(solution)/shard_map/all_to_all | solution.py:35
  14.5 2.8 %collective-permute-start.1 = (bf16[16,1536]{1,0:T(8,128)(2,1)S(1)}, bf16[16,1536]{1,0:T(8,128)(2,1)S(1)}, u32[]{:S(2)}, u32[]{:S(2)}) collective-permute-start(bf16[16,1536]{1,0:T(8,128)(2,1)S(1)} %pad_maximum_fusion.16), channel_id=1, source_target_pairs={{0,32},{16,48},{32,0},{48,16},{1,33},{17,49},{33,1},{49,17},{2,34}... | collective-permute-start | bytes 147464 | tf_op jit(solution)/shard_map/ppermute | solution.py:27
  17.3 1.4 constant_dynamic-update-slice_fusion.1
  18.7 1.4 collective-permute-done.1
  20.8 7.1 %all-to-all-done = bf16[8,8,2688]{2,1,0:T(8,128)(2,1)} async-done(((bf16[8,8,2688]{2,1,0:T(8,128)(2,1)}), bf16[8,8,2688]{2,1,0:T(8,128)(2,1)}, u32[]{:S(2)}, u32[]{:S(2)}) %all-to-all-start) | async-done | bytes 344096 | tf_op jit(solution)/shard_map/all_to_all | solution.py:35
  29.1 1.8 broadcast_in_dim.82
  30.9 4.2 %all-to-all-start.1 = ((bf16[8,32,1536]{2,1,0:T(8,128)(2,1)}), bf16[8,32,1536]{2,1,0:T(8,128)(2,1)}, u32[]{:S(2)}, u32[]{:S(2)}) async-start(bf16[8,32,1536]{2,1,0:T(8,128)(2,1)} %broadcast_in_dim.82), calls=%async_computation.1 | async-start | bytes 1572864 | tf_op jit(solution)/shard_map/all_to_all | solution.py:35
  35.2 2.8 %collective-permute-start.4 = (bf16[64,2688]{1,0:T(8,128)(2,1)}, bf16[64,2688]{1,0:T(8,128)(2,1)S(1)}, u32[]{:S(2)}, u32[]{:S(2)}) collective-permute-start(bf16[64,2688]{1,0:T(8,128)(2,1)} %bitcast.4), channel_id=1, source_target_pairs={{0,48},{16,32},{32,16},{48,0},{1,49},{17,33},{33,17},{49,1},{2,50}... | collective-permute-start | bytes 1032200 | tf_op jit(solution)/shard_map/ppermute | solution.py:27
  41.0 6.1 %collective-permute-done.3 = bf16[64,2688]{1,0:T(8,128)(2,1)S(1)} collective-permute-done((bf16[64,2688]{1,0:T(8,128)(2,1)}, bf16[64,2688]{1,0:T(8,128)(2,1)S(1)}, u32[]{:S(2)}, u32[]{:S(2)}) %collective-permute-start.3) | collective-permute-done | bytes 344096 | tf_op jit(solution)/shard_map/ppermute | solution.py:27
  47.2 4.5 %collective-permute-done.4 = bf16[64,2688]{1,0:T(8,128)(2,1)S(1)} collective-permute-done((bf16[64,2688]{1,0:T(8,128)(2,1)}, bf16[64,2688]{1,0:T(8,128)(2,1)S(1)}, u32[]{:S(2)}, u32[]{:S(2)}) %collective-permute-start.4) | collective-permute-done | bytes 344096 | tf_op jit(solution)/shard_map/ppermute | solution.py:27
  53.7 2.7 %all-to-all-done.1 = bf16[8,32,1536]{2,1,0:T(8,128)(2,1)} async-done(((bf16[8,32,1536]{2,1,0:T(8,128)(2,1)}), bf16[8,32,1536]{2,1,0:T(8,128)(2,1)}, u32[]{:S(2)}, u32[]{:S(2)}) %all-to-all-start.1) | async-done | bytes 786464 | tf_op jit(solution)/shard_map/all_to_all | solution.py:35
  66.7 2.0 fusion.63
  69.8 1.6 collective-permute-start.13
  72.3 2.4 %collective-permute-start.11 = (bf16[16,4096]{1,0:T(8,128)(2,1)}, bf16[16,4096]{1,0:T(8,128)(2,1)}, u32[]{:S(2)}, u32[]{:S(2)}) collective-permute-start(bf16[16,4096]{1,0:T(8,128)(2,1)} %pad_maximum_fusion.10), channel_id=1, source_target_pairs={{0,192},{64,0},{128,64},{192,128},{1,193},{65,1},{129,65},{193,129... | collective-permute-start | bytes 393224 | tf_op jit(solution)/shard_map/ppermute | solution.py:22
  75.7 2.6 %fusion.21 = f32[256,161]{0,1:T(8,128)S(1)} fusion(bf16[256,4224]{1,0:T(8,128)(2,1)} %collective-permute-done.6, bf16[1536,161]{0,1:T(8,128)(2,1)S(1)} %copy-done.17, bf16[2560,161]{0,1:T(8,128)(2,1)S(1)} %copy-done.16, bf16[4224]{0:T(1024)(128)(2,1)S(1)} %copy-done.31), kind=kOutput, calls=%fused_computation.37 | convolution fusion | flops 352273152 | bytes 3654912 | tf_op jit(solution)/shard_map/dot_general | solution.py:31
  86.8 1.4 broadcast_select_fusion.1
  89.6 1.5 broadcast_in_dim.86
  91.0 7.7 %all-to-all-start.2 = ((f32[64,2,512]{2,1,0:T(2,128)}), f32[64,2,512]{2,1,0:T(2,128)}, u32[]{:S(2)}, u32[]{:S(2)}) async-start(f32[64,2,512]{2,1,0:T(2,128)} %broadcast_in_dim.86), calls=%async_computation.2 | async-start | bytes 524288 | tf_op jit(solution)/shard_map/all_to_all | solution.py:35
  98.8 1.5 fusion.15
  100.3 2.9 %fusion.6 = f32[64,7680]{1,0:T(8,128)S(1)} fusion(bf16[64,256]{1,0:T(8,128)(2,1)S(1)} %fusion.15, bf16[1,256,7680]{2,1,0:T(8,128)(2,1)} %param.19), kind=kOutput, calls=%fused_computation.13 | convolution fusion | flops 251658240 | bytes 5931008 | tf_op jit(solution)/shard_map/dot_general | solution.py:31
  105.7 2.0 collective-permute-start.16
  107.7 1.4 collective-permute-start.15
  110.4 2.6 %fusion.113 = (f32[64,1,512]{2,1,0:T(1,128)}, f32[512]{0:T(512)}, f32[64,1,512]{2,1,0:T(1,128)}) fusion(f32[64,2,512]{2,1,0:T(2,128)} %all-to-all-done.2), kind=kLoop, calls=%fused_computation.220 | loop fusion | flops 32256 | bytes 526336 | tf_op jit(solution)/shard_map/slice | solution.py:97
  114.3 1.6 fusion.49
  126.3 2.3 %fusion.52 = f32[161,4224]{1,0:T(8,128)S(1)} fusion(bf16[256,4224]{1,0:T(8,128)(2,1)} %collective-permute-done.6, bf16[512,161]{0,1:T(8,128)(2,1)S(1)} %multiply_convert_fusion.1), kind=kOutput, calls=%fused_computation.91 | convolution fusion | flops 348192768 | bytes 4968960 | tf_op jit(solution)/shard_map/dot_general | solution.py:31
  129.4 1.4 collective-permute-done.15
  130.8 1.7 fusion.108
  133.4 2.9 %collective-permute-start.18 = (bf16[16,7680]{1,0:T(8,128)(2,1)S(1)}, bf16[16,7680]{1,0:T(8,128)(2,1)S(1)}, u32[]{:S(2)}, u32[]{:S(2)}) collective-permute-start(bf16[16,7680]{1,0:T(8,128)(2,1)S(1)} %multiply_convert_fusion), channel_id=1, source_target_pairs={{0,128},{64,192},{128,0},{192,64},{1,129},{65,193},{129,1},{193,65... | collective-permute-start | bytes 737288 | tf_op jit(solution)/shard_map/ppermute | solution.py:22
  136.4 2.3 %collective-permute-start.17 = (bf16[16,7680]{1,0:T(8,128)(2,1)S(1)}, bf16[16,7680]{1,0:T(8,128)(2,1)S(1)}, u32[]{:S(2)}, u32[]{:S(2)}) collective-permute-start(bf16[16,7680]{1,0:T(8,128)(2,1)S(1)} %multiply_convert_fusion), channel_id=1, source_target_pairs={{0,192},{64,0},{128,64},{192,128},{1,193},{65,1},{129,65},{193,129... | collective-permute-start | bytes 737288 | tf_op jit(solution)/shard_map/ppermute | solution.py:22
  139.6 2.4 %collective-permute-done.19 = bf16[16,7680]{1,0:T(8,128)(2,1)S(1)} collective-permute-done((bf16[16,7680]{1,0:T(8,128)(2,1)S(1)}, bf16[16,7680]{1,0:T(8,128)(2,1)S(1)}, u32[]{:S(2)}, u32[]{:S(2)}) %collective-permute-start.19) | collective-permute-done | bytes 245792 | tf_op jit(solution)/shard_map/ppermute | solution.py:22
  142.0 1.8 collective-permute-done.18
  143.8 3.0 %collective-permute-done.17 = bf16[16,7680]{1,0:T(8,128)(2,1)S(1)} collective-permute-done((bf16[16,7680]{1,0:T(8,128)(2,1)S(1)}, bf16[16,7680]{1,0:T(8,128)(2,1)S(1)}, u32[]{:S(2)}, u32[]{:S(2)}) %collective-permute-start.17) | collective-permute-done | bytes 245792 | tf_op jit(solution)/shard_map/ppermute | solution.py:22
  149.6 1.4 collective-permute-start.22
  151.1 3.0 %collective-permute-start.21 = (bf16[16,4096]{1,0:T(8,128)(2,1)S(1)}, bf16[16,4096]{1,0:T(8,128)(2,1)S(1)}, u32[]{:S(2)}, u32[]{:S(2)}) collective-permute-start(bf16[16,4096]{1,0:T(8,128)(2,1)S(1)} %get-tuple-element.58), channel_id=1, source_target_pairs={{0,128},{64,192},{128,0},{192,64},{1,129},{65,193},{129,1},{193,65... | collective-permute-start | bytes 393224 | tf_op jit(solution)/shard_map/ppermute | solution.py:22
  156.0 5.2 %collective-permute-done.21 = bf16[16,4096]{1,0:T(8,128)(2,1)S(1)} collective-permute-done((bf16[16,4096]{1,0:T(8,128)(2,1)S(1)}, bf16[16,4096]{1,0:T(8,128)(2,1)S(1)}, u32[]{:S(2)}, u32[]{:S(2)}) %collective-permute-start.21) | collective-permute-done | bytes 131104 | tf_op jit(solution)/shard_map/ppermute | solution.py:22
  161.3 3.3 %collective-permute-start.25 = (bf16[16,4096]{1,0:T(8,128)(2,1)S(1)}, bf16[16,4096]{1,0:T(8,128)(2,1)S(1)}, u32[]{:S(2)}, u32[]{:S(2)}) collective-permute-start(bf16[16,4096]{1,0:T(8,128)(2,1)S(1)} %fusion.42), channel_id=1, source_target_pairs={{0,48},{16,32},{32,16},{48,0},{1,49},{17,33},{33,17},{49,1},{2,50}... | collective-permute-start | bytes 393224 | tf_op jit(solution)/shard_map/ppermute | solution.py:27
  165.6 3.1 %fusion.3 = bf16[1,4096,256]{2,1,0:T(8,128)(2,1)} fusion(bf16[64,256]{1,0:T(8,128)(2,1)S(1)} %fusion.12, bf16[16,4096]{1,0:T(8,128)(2,1)} %collective-permute-done.13, bf16[16,4096]{1,0:T(8,128)(2,1)} %collective-permute-done.12, bf16[16,4096]{1,0:T(8,128)(2,1)} %collective-permute-done.11, bf16[16,2560]{1,0:T(8,128)(2,1)S(1)} %slice.190, ...), kind=kOutput, calls=%fused_computation.8 | convolution fusion | flops 137887744 | bytes 2654208 | tf_op jit(solution)/shard_map/dot_general | solution.py:31
  168.9 2.2 collective-permute-done.24
  173.2 2.2 collective-permute-start.10
  175.4 1.4 collective-permute-start.9
  178.8 8.7 %collective-permute-done.8 = bf16[64,4096]{1,0:T(8,128)(2,1)S(1)} collective-permute-done((bf16[64,4096]{1,0:T(8,128)(2,1)S(1)}, bf16[64,4096]{1,0:T(8,128)(2,1)S(1)}, u32[]{:S(2)}, u32[]{:S(2)}) %collective-permute-start.8) | collective-permute-done | bytes 524320 | tf_op jit(solution)/shard_map/ppermute | solution.py:27
  187.5 10.7 %collective-permute-done.10 = bf16[64,4096]{1,0:T(8,128)(2,1)S(1)} collective-permute-done((bf16[64,4096]{1,0:T(8,128)(2,1)S(1)}, bf16[64,4096]{1,0:T(8,128)(2,1)S(1)}, u32[]{:S(2)}, u32[]{:S(2)}) %collective-permute-start.10) | collective-permute-done | bytes 524320 | tf_op jit(solution)/shard_map/ppermute | solution.py:27
  198.2 1.5 collective-permute-done.9
  201.1 6.7 %all-to-all-start.3 = ((bf16[8,8,4096]{2,1,0:T(8,128)(2,1)}), bf16[8,8,4096]{2,1,0:T(8,128)(2,1)}, u32[]{:S(2)}, u32[]{:S(2)}) async-start(bf16[8,8,4096]{2,1,0:T(8,128)(2,1)} %fusion.30), calls=%async_computation.3 | async-start | bytes 1048576 | tf_op jit(solution)/shard_map/all_to_all | solution.py:35
  207.8 4.6 %fusion = bf16[1,256,7680]{2,1,0:T(8,128)(2,1)} fusion(bf16[64,256]{1,0:T(8,128)(2,1)S(1)} %copy-done.24, bf16[16,7680]{1,0:T(8,128)(2,1)} %copy-done.18, bf16[16,7680]{1,0:T(8,128)(2,1)} %copy-done.19, bf16[16,7680]{1,0:T(8,128)(2,1)} %copy-done.20, bf16[16,7680]{1,0:T(8,128)(2,1)} %copy-done.15), kind=kOutput, calls=%fused_computation.1 | convolution fusion | flops 257556480 | bytes 4947968 | tf_op jit(solution)/shard_map/dot_general | solution.py:31
  215.0 10.2 %all-to-all-done.3 = bf16[8,8,4096]{2,1,0:T(8,128)(2,1)} async-done(((bf16[8,8,4096]{2,1,0:T(8,128)(2,1)}), bf16[8,8,4096]{2,1,0:T(8,128)(2,1)}, u32[]{:S(2)}, u32[]{:S(2)}) %all-to-all-start.3) | async-done | bytes 524320 | tf_op jit(solution)/shard_map/all_to_all | solution.py:35
  225.1 1.8 reduce_sum.75
  (196 shorter events, 65.8 us)
Async XLA Ops:
  0.6 98.1 %copy-start = (bf16[1,4096,256]{2,1,0:T(8,128)(2,1)S(1)}, bf16[1,4096,256]{2,1,0:T(8,128)(2,1)}, u32[]{:S(2)}) copy-start(bf16[1,4096,256]{2,1,0:T(8,128)(2,1)} %param.18) | copy-start | bytes 6291460
  1.5 26.9 %copy-start.30 = (bf16[4096,1]{0,1:T(2,128)(2,1)S(1)}, bf16[4096,1]{0,1:T(2,128)(2,1)}, u32[]{:S(2)}) copy-start(bf16[4096,1]{0,1:T(2,128)(2,1)} %param.17) | copy-start | bytes 24580
  1.5 12.9 %collective-permute-start = (bf16[8,1536]{1,0:T(8,128)(2,1)S(1)}, bf16[8,1536]{1,0:T(8,128)(2,1)S(1)}, u32[]{:S(2)}, u32[]{:S(2)}) collective-permute-start(bf16[8,1536]{1,0:T(8,128)(2,1)S(1)} %slice.138), channel_id=1, source_target_pairs={{0,16},{16,0},{32,48},{48,32},{1,17},{17,1},{33,49},{49,33},{2,18}... | collective-permute-start | bytes 73736 | tf_op jit(solution)/shard_map/ppermute | solution.py:27
  6.0 21.9 %all-to-all-start = ((bf16[8,8,2688]{2,1,0:T(8,128)(2,1)}), bf16[8,8,2688]{2,1,0:T(8,128)(2,1)}, u32[]{:S(2)}, u32[]{:S(2)}) async-start(bf16[8,8,2688]{2,1,0:T(8,128)(2,1)} %broadcast_in_dim.81), calls=%async_computation | async-start | bytes 688128 | tf_op jit(solution)/shard_map/all_to_all | solution.py:35
  14.5 5.7 %collective-permute-start.1 = (bf16[16,1536]{1,0:T(8,128)(2,1)S(1)}, bf16[16,1536]{1,0:T(8,128)(2,1)S(1)}, u32[]{:S(2)}, u32[]{:S(2)}) collective-permute-start(bf16[16,1536]{1,0:T(8,128)(2,1)S(1)} %pad_maximum_fusion.16), channel_id=1, source_target_pairs={{0,32},{16,48},{32,0},{48,16},{1,33},{17,49},{33,1},{49,17},{2,34}... | collective-permute-start | bytes 147464 | tf_op jit(solution)/shard_map/ppermute | solution.py:27
  27.9 12.1 %collective-permute-start.2 = (bf16[64,2688]{1,0:T(8,128)(2,1)}, bf16[64,2688]{1,0:T(8,128)(2,1)}, u32[]{:S(2)}, u32[]{:S(2)}) collective-permute-start(bf16[64,2688]{1,0:T(8,128)(2,1)} %bitcast.4), channel_id=1, source_target_pairs={{0,16},{16,0},{32,48},{48,32},{1,17},{17,1},{33,49},{49,33},{2,18}... | collective-permute-start | bytes 1032200 | tf_op jit(solution)/shard_map/ppermute | solution.py:27
  30.9 25.5 %all-to-all-start.1 = ((bf16[8,32,1536]{2,1,0:T(8,128)(2,1)}), bf16[8,32,1536]{2,1,0:T(8,128)(2,1)}, u32[]{:S(2)}, u32[]{:S(2)}) async-start(bf16[8,32,1536]{2,1,0:T(8,128)(2,1)} %broadcast_in_dim.82), calls=%async_computation.1 | async-start | bytes 1572864 | tf_op jit(solution)/shard_map/all_to_all | solution.py:35
  35.2 16.5 %collective-permute-start.4 = (bf16[64,2688]{1,0:T(8,128)(2,1)}, bf16[64,2688]{1,0:T(8,128)(2,1)S(1)}, u32[]{:S(2)}, u32[]{:S(2)}) collective-permute-start(bf16[64,2688]{1,0:T(8,128)(2,1)} %bitcast.4), channel_id=1, source_target_pairs={{0,48},{16,32},{32,16},{48,0},{1,49},{17,33},{33,17},{49,1},{2,50}... | collective-permute-start | bytes 1032200 | tf_op jit(solution)/shard_map/ppermute | solution.py:27
  38.0 9.1 %collective-permute-start.3 = (bf16[64,2688]{1,0:T(8,128)(2,1)}, bf16[64,2688]{1,0:T(8,128)(2,1)S(1)}, u32[]{:S(2)}, u32[]{:S(2)}) collective-permute-start(bf16[64,2688]{1,0:T(8,128)(2,1)} %bitcast.4), channel_id=1, source_target_pairs={{0,32},{16,48},{32,0},{48,16},{1,33},{17,49},{33,1},{49,17},{2,34}... | collective-permute-start | bytes 1032200 | tf_op jit(solution)/shard_map/ppermute | solution.py:27
  58.6 8.1 %collective-permute-start.6 = (bf16[256,4224]{1,0:T(8,128)(2,1)}, bf16[256,4224]{1,0:T(8,128)(2,1)}, u32[]{:S(2)}, u32[]{:S(2)}) collective-permute-start(bf16[256,4224]{1,0:T(8,128)(2,1)} %constant_dynamic-update-slice_fusion.6), channel_id=1, source_target_pairs={{0,1},{1,0},{2,3},{3,2},{4,5},{5,4},{6,7},{7,6},{8,9},{9,8},{10,11... | collective-permute-start | bytes 6488072 | tf_op jit(solution)/shard_map/ppermute | solution.py:22
  58.9 4.2 %collective-permute-start.5 = (f32[2,256]{1,0:T(2,128)S(1)}, f32[2,256]{1,0:T(2,128)S(1)}, u32[]{:S(2)}, u32[]{:S(2)}) collective-permute-start(f32[2,256]{1,0:T(2,128)S(1)} %get-tuple-element.68), channel_id=1, source_target_pairs={{0,1},{1,0},{2,3},{3,2},{4,5},{5,4},{6,7},{7,6},{8,9},{9,8},{10,11... | collective-permute-start | bytes 6152 | tf_op jit(solution)/shard_map/ppermute | solution.py:22
  68.7 6.1 %copy-start.16 = (bf16[2560,161]{0,1:T(8,128)(2,1)S(1)}, bf16[2560,161]{0,1:T(8,128)(2,1)}, u32[]{:S(2)}) copy-start(bf16[2560,161]{0,1:T(8,128)(2,1)} %slice.191) | copy-start | bytes 2472964
  68.7 6.1 %copy-start.17 = (bf16[1536,161]{0,1:T(8,128)(2,1)S(1)}, bf16[1536,161]{0,1:T(8,128)(2,1)}, u32[]{:S(2)}) copy-start(bf16[1536,161]{0,1:T(8,128)(2,1)} %slice.192) | copy-start | bytes 1483780
  68.7 6.0 %copy-start.31 = (bf16[4224]{0:T(1024)(128)(2,1)S(1)}, bf16[4224]{0:T(1024)(128)(2,1)}, u32[]{:S(2)}) copy-start(bf16[4224]{0:T(1024)(128)(2,1)} %pad.26.clone) | copy-start | bytes 25348
  69.8 28.9 %collective-permute-start.13 = (bf16[16,4096]{1,0:T(8,128)(2,1)}, bf16[16,4096]{1,0:T(8,128)(2,1)}, u32[]{:S(2)}, u32[]{:S(2)}) collective-permute-start(bf16[16,4096]{1,0:T(8,128)(2,1)} %pad_maximum_fusion.10), channel_id=1, source_target_pairs={{0,64},{64,128},{128,192},{192,0},{1,65},{65,129},{129,193},{193,1... | collective-permute-start | bytes 393224 | tf_op jit(solution)/shard_map/ppermute | solution.py:22
  71.4 27.3 %collective-permute-start.12 = (bf16[16,4096]{1,0:T(8,128)(2,1)}, bf16[16,4096]{1,0:T(8,128)(2,1)}, u32[]{:S(2)}, u32[]{:S(2)}) collective-permute-start(bf16[16,4096]{1,0:T(8,128)(2,1)} %pad_maximum_fusion.10), channel_id=1, source_target_pairs={{0,128},{64,192},{128,0},{192,64},{1,129},{65,193},{129,1},{193,65... | collective-permute-start | bytes 393224 | tf_op jit(solution)/shard_map/ppermute | solution.py:22
  72.3 26.4 %collective-permute-start.11 = (bf16[16,4096]{1,0:T(8,128)(2,1)}, bf16[16,4096]{1,0:T(8,128)(2,1)}, u32[]{:S(2)}, u32[]{:S(2)}) collective-permute-start(bf16[16,4096]{1,0:T(8,128)(2,1)} %pad_maximum_fusion.10), channel_id=1, source_target_pairs={{0,192},{64,0},{128,64},{192,128},{1,193},{65,1},{129,65},{193,129... | collective-permute-start | bytes 393224 | tf_op jit(solution)/shard_map/ppermute | solution.py:22
  91.0 19.3 %all-to-all-start.2 = ((f32[64,2,512]{2,1,0:T(2,128)}), f32[64,2,512]{2,1,0:T(2,128)}, u32[]{:S(2)}, u32[]{:S(2)}) async-start(f32[64,2,512]{2,1,0:T(2,128)} %broadcast_in_dim.86), calls=%async_computation.2 | async-start | bytes 524288 | tf_op jit(solution)/shard_map/all_to_all | solution.py:35
  105.7 23.7 %collective-permute-start.14 = (f32[16,7680]{1,0:T(8,128)}, f32[16,7680]{1,0:T(8,128)}, u32[]{:S(2)}, u32[]{:S(2)}) collective-permute-start(f32[16,7680]{1,0:T(8,128)} %get-tuple-element.51), channel_id=1, source_target_pairs={{0,64},{64,128},{128,192},{192,0},{1,65},{65,129},{129,193},{193,1... | collective-permute-start | bytes 1474568 | tf_op jit(solution)/shard_map/ppermute | solution.py:22
  105.7 23.7 %collective-permute-start.16 = (f32[16,7680]{1,0:T(8,128)}, f32[16,7680]{1,0:T(8,128)}, u32[]{:S(2)}, u32[]{:S(2)}) collective-permute-start(f32[16,7680]{1,0:T(8,128)} %get-tuple-element.52), channel_id=1, source_target_pairs={{0,192},{64,0},{128,64},{192,128},{1,193},{65,1},{129,65},{193,129... | collective-permute-start | bytes 1474568 | tf_op jit(solution)/shard_map/ppermute | solution.py:22
  107.7 23.2 %collective-permute-start.15 = (f32[16,7680]{1,0:T(8,128)}, f32[16,7680]{1,0:T(8,128)}, u32[]{:S(2)}, u32[]{:S(2)}) collective-permute-start(f32[16,7680]{1,0:T(8,128)} %get-tuple-element.53), channel_id=1, source_target_pairs={{0,128},{64,192},{128,0},{192,64},{1,129},{65,193},{129,1},{193,65... | collective-permute-start | bytes 1474568 | tf_op jit(solution)/shard_map/ppermute | solution.py:22
  129.3 47.7 %copy-start.6 = (bf16[161,1536]{1,0:T(8,128)(2,1)}, bf16[161,1536]{1,0:T(8,128)(2,1)S(1)}, u32[]{:S(2)}) copy-start(bf16[161,1536]{1,0:T(8,128)(2,1)S(1)} %slice.217) | copy-start | bytes 1483780
  129.4 47.6 %copy-start.4 = (bf16[161,2560]{1,0:T(8,128)(2,1)}, bf16[161,2560]{1,0:T(8,128)(2,1)S(1)}, u32[]{:S(2)}) copy-start(bf16[161,2560]{1,0:T(8,128)(2,1)S(1)} %slice.218) | copy-start | bytes 2472964
  132.8 14.0 %copy-start.11 = (bf16[1,256,7680]{2,1,0:T(8,128)(2,1)S(1)}, bf16[1,256,7680]{2,1,0:T(8,128)(2,1)}, u32[]{:S(2)}) copy-start(bf16[1,256,7680]{2,1,0:T(8,128)(2,1)} %param.19) | copy-start | bytes 11796484
  133.1 15.1 %copy-start.15 = (bf16[16,7680]{1,0:T(8,128)(2,1)}, bf16[16,7680]{1,0:T(8,128)(2,1)S(1)}, u32[]{:S(2)}) copy-start(bf16[16,7680]{1,0:T(8,128)(2,1)S(1)} %multiply_convert_fusion) | copy-start | bytes 737284
  133.1 8.9 %collective-permute-start.19 = (bf16[16,7680]{1,0:T(8,128)(2,1)S(1)}, bf16[16,7680]{1,0:T(8,128)(2,1)S(1)}, u32[]{:S(2)}, u32[]{:S(2)}) collective-permute-start(bf16[16,7680]{1,0:T(8,128)(2,1)S(1)} %multiply_convert_fusion), channel_id=1, source_target_pairs={{0,64},{64,128},{128,192},{192,0},{1,65},{65,129},{129,193},{193,1... | collective-permute-start | bytes 737288 | tf_op jit(solution)/shard_map/ppermute | solution.py:22
  133.4 10.4 %collective-permute-start.18 = (bf16[16,7680]{1,0:T(8,128)(2,1)S(1)}, bf16[16,7680]{1,0:T(8,128)(2,1)S(1)}, u32[]{:S(2)}, u32[]{:S(2)}) collective-permute-start(bf16[16,7680]{1,0:T(8,128)(2,1)S(1)} %multiply_convert_fusion), channel_id=1, source_target_pairs={{0,128},{64,192},{128,0},{192,64},{1,129},{65,193},{129,1},{193,65... | collective-permute-start | bytes 737288 | tf_op jit(solution)/shard_map/ppermute | solution.py:22
  136.4 10.5 %collective-permute-start.17 = (bf16[16,7680]{1,0:T(8,128)(2,1)S(1)}, bf16[16,7680]{1,0:T(8,128)(2,1)S(1)}, u32[]{:S(2)}, u32[]{:S(2)}) collective-permute-start(bf16[16,7680]{1,0:T(8,128)(2,1)S(1)} %multiply_convert_fusion), channel_id=1, source_target_pairs={{0,192},{64,0},{128,64},{192,128},{1,193},{65,1},{129,65},{193,129... | collective-permute-start | bytes 737288 | tf_op jit(solution)/shard_map/ppermute | solution.py:22
  139.5 32.1 %collective-permute-start.7 = (bf16[256,4096]{1,0:T(8,128)(2,1)S(1)}, bf16[256,4096]{1,0:T(8,128)(2,1)S(1)}, u32[]{:S(2)}, u32[]{:S(2)}) collective-permute-start(bf16[256,4096]{1,0:T(8,128)(2,1)S(1)} %convolution_convert_fusion.2), channel_id=1, source_target_pairs={{0,1},{1,0},{2,3},{3,2},{4,5},{5,4},{6,7},{7,6},{8,9},{9,8},{10,11... | collective-permute-start | bytes 6291464 | tf_op jit(solution)/shard_map/ppermute | solution.py:22
  142.0 6.2 %copy-start.18 = (bf16[16,7680]{1,0:T(8,128)(2,1)}, bf16[16,7680]{1,0:T(8,128)(2,1)S(1)}, u32[]{:S(2)}) copy-start(bf16[16,7680]{1,0:T(8,128)(2,1)S(1)} %collective-permute-done.19) | copy-start | bytes 737284
  149.0 6.8 %collective-permute-start.20 = (bf16[16,4096]{1,0:T(8,128)(2,1)S(1)}, bf16[16,4096]{1,0:T(8,128)(2,1)S(1)}, u32[]{:S(2)}, u32[]{:S(2)}) collective-permute-start(bf16[16,4096]{1,0:T(8,128)(2,1)S(1)} %get-tuple-element.56), channel_id=1, source_target_pairs={{0,64},{64,128},{128,192},{192,0},{1,65},{65,129},{129,193},{193,1... | collective-permute-start | bytes 393224 | tf_op jit(solution)/shard_map/ppermute | solution.py:22
  149.6 6.4 %collective-permute-start.22 = (bf16[16,4096]{1,0:T(8,128)(2,1)S(1)}, bf16[16,4096]{1,0:T(8,128)(2,1)S(1)}, u32[]{:S(2)}, u32[]{:S(2)}) collective-permute-start(bf16[16,4096]{1,0:T(8,128)(2,1)S(1)} %get-tuple-element.57), channel_id=1, source_target_pairs={{0,192},{64,0},{128,64},{192,128},{1,193},{65,1},{129,65},{193,129... | collective-permute-start | bytes 393224 | tf_op jit(solution)/shard_map/ppermute | solution.py:22
  151.1 10.1 %collective-permute-start.21 = (bf16[16,4096]{1,0:T(8,128)(2,1)S(1)}, bf16[16,4096]{1,0:T(8,128)(2,1)S(1)}, u32[]{:S(2)}, u32[]{:S(2)}) collective-permute-start(bf16[16,4096]{1,0:T(8,128)(2,1)S(1)} %get-tuple-element.58), channel_id=1, source_target_pairs={{0,128},{64,192},{128,0},{192,64},{1,129},{65,193},{129,1},{193,65... | collective-permute-start | bytes 393224 | tf_op jit(solution)/shard_map/ppermute | solution.py:22
  154.3 11.3 %copy-start.22 = (bf16[16,1536]{1,0:T(8,128)(2,1)S(1)}, bf16[16,1536]{1,0:T(8,128)(2,1)}, u32[]{:S(2)}) copy-start(bf16[16,1536]{1,0:T(8,128)(2,1)} %copy-done.21) | copy-start | bytes 147460
  155.1 16.0 %copy-start.27 = (pred[64,128]{1,0:T(32,128)(4,1)S(1)}, pred[64,128]{1,0:T(32,128)(4,1)}, u32[]{:S(2)}) copy-start(pred[64,128]{1,0:T(32,128)(4,1)} %broadcast_compare_fusion) | copy-start | bytes 24580
  155.1 21.7 %collective-permute-start.27 = (bf16[2,161,1024]{2,0,1:T(2,128)(2,1)S(1)}, bf16[2,161,1024]{2,0,1:T(2,128)(2,1)S(1)}, u32[]{:S(2)}, u32[]{:S(2)}) collective-permute-start(bf16[2,161,1024]{2,0,1:T(2,128)(2,1)S(1)} %copy.36), channel_id=1, source_target_pairs={{0,64},{64,0},{128,192},{192,128},{1,65},{65,1},{129,193},{193,129... | collective-permute-start | bytes 1978376 | tf_op jit(solution)/shard_map/ppermute | solution.py:27
  161.3 7.6 %collective-permute-start.25 = (bf16[16,4096]{1,0:T(8,128)(2,1)S(1)}, bf16[16,4096]{1,0:T(8,128)(2,1)S(1)}, u32[]{:S(2)}, u32[]{:S(2)}) collective-permute-start(bf16[16,4096]{1,0:T(8,128)(2,1)S(1)} %fusion.42), channel_id=1, source_target_pairs={{0,48},{16,32},{32,16},{48,0},{1,49},{17,33},{33,17},{49,1},{2,50}... | collective-permute-start | bytes 393224 | tf_op jit(solution)/shard_map/ppermute | solution.py:27
  164.6 6.5 %collective-permute-start.24 = (bf16[16,4096]{1,0:T(8,128)(2,1)S(1)}, bf16[16,4096]{1,0:T(8,128)(2,1)S(1)}, u32[]{:S(2)}, u32[]{:S(2)}) collective-permute-start(bf16[16,4096]{1,0:T(8,128)(2,1)S(1)} %fusion.42), channel_id=1, source_target_pairs={{0,32},{16,48},{32,0},{48,16},{1,33},{17,49},{33,1},{49,17},{2,34}... | collective-permute-start | bytes 393224 | tf_op jit(solution)/shard_map/ppermute | solution.py:27
  165.2 5.8 %collective-permute-start.23 = (bf16[16,4096]{1,0:T(8,128)(2,1)S(1)}, bf16[16,4096]{1,0:T(8,128)(2,1)S(1)}, u32[]{:S(2)}, u32[]{:S(2)}) collective-permute-start(bf16[16,4096]{1,0:T(8,128)(2,1)S(1)} %fusion.42), channel_id=1, source_target_pairs={{0,16},{16,0},{32,48},{48,32},{1,17},{17,1},{33,49},{49,33},{2,18}... | collective-permute-start | bytes 393224 | tf_op jit(solution)/shard_map/ppermute | solution.py:27
  171.5 28.6 %collective-permute-start.26 = (bf16[64,4096]{1,0:T(8,128)(2,1)S(1)}, bf16[64,4096]{1,0:T(8,128)(2,1)S(1)}, u32[]{:S(2)}, u32[]{:S(2)}) collective-permute-start(bf16[64,4096]{1,0:T(8,128)(2,1)S(1)} %convolution_convert_fusion.3), channel_id=1, source_target_pairs={{0,1},{1,0},{2,3},{3,2},{4,5},{5,4},{6,7},{7,6},{8,9},{9,8},{10,11... | collective-permute-start | bytes 1572872 | tf_op jit(solution)/shard_map/ppermute | solution.py:22
  172.6 14.9 %collective-permute-start.8 = (bf16[64,4096]{1,0:T(8,128)(2,1)S(1)}, bf16[64,4096]{1,0:T(8,128)(2,1)S(1)}, u32[]{:S(2)}, u32[]{:S(2)}) collective-permute-start(bf16[64,4096]{1,0:T(8,128)(2,1)S(1)} %get-tuple-element.48), channel_id=1, source_target_pairs={{0,16},{16,0},{32,48},{48,32},{1,17},{17,1},{33,49},{49,33},{2,18}... | collective-permute-start | bytes 1572872 | tf_op jit(solution)/shard_map/ppermute | solution.py:27
  173.2 25.0 %collective-permute-start.10 = (bf16[64,4096]{1,0:T(8,128)(2,1)S(1)}, bf16[64,4096]{1,0:T(8,128)(2,1)S(1)}, u32[]{:S(2)}, u32[]{:S(2)}) collective-permute-start(bf16[64,4096]{1,0:T(8,128)(2,1)S(1)} %get-tuple-element.49), channel_id=1, source_target_pairs={{0,48},{16,32},{32,16},{48,0},{1,49},{17,33},{33,17},{49,1},{2,50}... | collective-permute-start | bytes 1572872 | tf_op jit(solution)/shard_map/ppermute | solution.py:27
  175.4 24.3 %collective-permute-start.9 = (bf16[64,4096]{1,0:T(8,128)(2,1)S(1)}, bf16[64,4096]{1,0:T(8,128)(2,1)S(1)}, u32[]{:S(2)}, u32[]{:S(2)}) collective-permute-start(bf16[64,4096]{1,0:T(8,128)(2,1)S(1)} %get-tuple-element.50), channel_id=1, source_target_pairs={{0,32},{16,48},{32,0},{48,16},{1,33},{17,49},{33,1},{49,17},{2,34}... | collective-permute-start | bytes 1572872 | tf_op jit(solution)/shard_map/ppermute | solution.py:27
  177.0 23.2 %copy-start.9 = (f32[2,161,1024]{2,1,0:T(8,128)}, f32[2,161,1024]{2,1,0:T(8,128)S(1)}, u32[]{:S(2)}) copy-start(f32[2,161,1024]{2,1,0:T(8,128)S(1)} %copy_convert_fusion) | copy-start | bytes 3956740
  178.1 34.4 %collective-permute-start.28 = (bf16[161,1024]{1,0:T(8,128)(2,1)}, bf16[161,1024]{1,0:T(8,128)(2,1)}, u32[]{:S(2)}, u32[]{:S(2)}) collective-permute-start(bf16[161,1024]{1,0:T(8,128)(2,1)} %fusion.26), channel_id=1, source_target_pairs={{0,128},{64,192},{128,0},{192,64},{1,129},{65,193},{129,1},{193,65... | collective-permute-start | bytes 989192 | tf_op jit(solution)/shard_map/ppermute | solution.py:27
  200.1 7.7 %copy-start.24 = (bf16[64,256]{1,0:T(8,128)(2,1)S(1)}, bf16[64,256]{1,0:T(8,128)(2,1)}, u32[]{:S(2)}) copy-start(bf16[64,256]{1,0:T(8,128)(2,1)} %copy-done.23) | copy-start | bytes 98308
  201.1 24.0 %all-to-all-start.3 = ((bf16[8,8,4096]{2,1,0:T(8,128)(2,1)}), bf16[8,8,4096]{2,1,0:T(8,128)(2,1)}, u32[]{:S(2)}, u32[]{:S(2)}) async-start(bf16[8,8,4096]{2,1,0:T(8,128)(2,1)} %fusion.30), calls=%async_computation.3 | async-start | bytes 1048576 | tf_op jit(solution)/shard_map/all_to_all | solution.py:35
  207.8 4.6 %copy-start.5 = (bf16[161,2560]{1,0:T(8,128)(2,1)S(1)}, bf16[161,2560]{1,0:T(8,128)(2,1)}, u32[]{:S(2)}) copy-start(bf16[161,2560]{1,0:T(8,128)(2,1)} %copy-done.4) | copy-start | bytes 2472964
  (19 other events, 46.8 us)

commit v5 on v3

--- a/solution.py
+++ b/solution.py
@@ -11,7 +11,7 @@
 OWN = 8
 NX, NZ, NDP = 4, 8, 4
 META = 128
-CA = 1408
+CA = 1536
 
 
 F32, BF16 = jnp.float32, jnp.bfloat16
@@ -35,19 +35,13 @@
 
 
 def gathered(hidden, targets, loss_weight):
-    digits = jnp.stack(
-        [
-            (targets >> 16).astype(BF16),
-            ((targets >> 8) & 255).astype(BF16),
-            (targets & 255).astype(BF16),
-            loss_weight,
-        ],
-        axis=1,
-    )
+    lane = jnp.arange(META, dtype=jnp.int32)
+    digit = (targets[:, None] >> jnp.maximum(16 - 8 * lane, 0)[None, :]) & 255
+    digits = jnp.where(lane[None, :] == 3, loss_weight[:, None], digit.astype(BF16))
     model = hidden.shape[1]
     rest = model - CA
     a1 = hidden[:, :CA]
-    pay = jnp.concatenate([hidden[:, CA:], jnp.pad(digits, ((0, 0), (0, META - 4)))], axis=1)
+    pay = jnp.concatenate([hidden[:, CA:], digits], axis=1)
     a1 = jnp.concatenate([a1] + [shift(a1, "x", -k) for k in range(1, NX)], axis=0)
     b1 = from_everyone(pay, "z").reshape(NZ * OWN, -1)
     a1, b1 = lax.optimization_barrier((a1, b1))
@@ -181,7 +175,8 @@
     rest = NZ * OWN
     far_tail = dot(place[:, rest:], tail_all, 0, 0).astype(BF16)
     tail_from_core = shift(far_tail, "core", 1)
-    chip = chip + dot(place[:, :rest], tail_all, 0, 0) + tail_from_core.astype(F32)
+    chip = lax.optimization_barrier(chip + dot(place[:, :rest], tail_all, 0, 0))
+    chip = chip + tail_from_core.astype(F32)
     last = swapped(chip.reshape(NZ, OWN, model).astype(BF16), "z")
     hidden_grad = jnp.sum(last.astype(F32), axis=0).astype(BF16)
 

time: 227 us -> 225 us (level)
  waiting for transfers between devices: 88.5 us -> 91.7 us
  local copies, waits for them, and re-layouts: 24.5 us -> 21.8 us
    ppermute x28, waiting for transfers between devices: 53.7 us -> 61.2 us  [shift(): return lax.ppermute(value, axis, [(j, (j + step) % n) for j in range(n)])]
    all_to_all x5, waiting for transfers between devices: 34.8 us -> 30.6 us  [swapped(): return lax.all_to_all(parts, axis, split_axis=0, concat_axis=0, tiled=True)]
    unnamed x48 -> x43, local copies, waits for them, and re-layouts: 5.74 us -> 4.92 us
  transfers between devices with their start and end apart: 33 -> 33, of which waited for: 22 -> 21; matrix products, arithmetic and copies ran while one was open for 20% -> 19% of each run, Pallas kernels for 0% -> 0%
where the time goes in v5:
time: 225 us; the launch traced here: 224 us
  waiting for transfers between devices  91.7 us (41%)
  starting transfers between devices  68.2 us (30%)
  matrix products  24 us (11%)
  local copies, waits for them, and re-layouts  21.8 us (10%)
  other arithmetic  16.8 us (7%)
    ppermute x28, waiting for transfers between devices, shift(): return lax.ppermute(value, axis, [(j, (j + step) % n) for j in range(n)])  61.2 us
    ppermute x28, starting transfers between devices, shift(): return lax.ppermute(value, axis, [(j, (j + step) % n) for j in range(n)])  37.1 us
    all_to_all x5, starting transfers between devices, swapped(): return lax.all_to_all(parts, axis, split_axis=0, concat_axis=0, tiled=True)  31.1 us
    all_to_all x5, waiting for transfers between devices, swapped(): return lax.all_to_all(parts, axis, split_axis=0, concat_axis=0, tiled=True)  30.6 us
    dot_general x16, matrix products, dot(): lax.dot_general(a, b, (((ca,), (cb,)), ((), ())), preferred_element_type=...  24 us
    broadcast_in_dim x4, local copies, waits for them, and re-layouts, from_everyone(): jnp.broadcast_to(value, (lax.axis_size(axis), *value.shape))  5.09 us
    unnamed x43, local copies, waits for them, and re-layouts  4.92 us
  transfers between devices with their start and end apart: 33, of which 21 were waited for; matrix products, arithmetic and copies ran while one was open for 19% of the time, Pallas kernels for 0%

profile of v5, /device:TPU:8, one launch (start us, length us, event | category | flops | bytes accessed | tf_op | source)
XLA Modules:
  0.0 223.7 jit_solution(6794062348985081213)
XLA Ops:
  1.5 1.5 collective-permute-start.2
  3.0 2.7 %collective-permute-start.1 = (bf16[8,1536]{1,0:T(8,128)(2,1)S(1)}, bf16[8,1536]{1,0:T(8,128)(2,1)S(1)}, u32[]{:S(2)}, u32[]{:S(2)}) collective-permute-start(bf16[8,1536]{1,0:T(8,128)(2,1)S(1)} %slice.120), channel_id=1, source_target_pairs={{0,32},{16,48},{32,0},{48,16},{1,33},{17,49},{33,1},{49,17},{2,34}... | collective-permute-start | bytes 73736 | tf_op jit(solution)/shard_map/ppermute | solution.py:22
  5.8 1.4 collective-permute-start
  9.5 8.5 %all-to-all-start = ((bf16[8,8,2688]{2,1,0:T(8,128)(2,1)}), bf16[8,8,2688]{2,1,0:T(8,128)(2,1)}, u32[]{:S(2)}, u32[]{:S(2)}) async-start(bf16[8,8,2688]{2,1,0:T(8,128)(2,1)} %broadcast_in_dim.106), calls=%async_computation | async-start | bytes 688128 | tf_op jit(solution)/shard_map/all_to_all | solution.py:30
  18.0 1.4 constant_dynamic-update-slice_fusion.1
  20.8 10.0 %all-to-all-done = bf16[8,8,2688]{2,1,0:T(8,128)(2,1)} async-done(((bf16[8,8,2688]{2,1,0:T(8,128)(2,1)}), bf16[8,8,2688]{2,1,0:T(8,128)(2,1)}, u32[]{:S(2)}, u32[]{:S(2)}) %all-to-all-start) | async-done | bytes 344096 | tf_op jit(solution)/shard_map/all_to_all | solution.py:30
  31.3 1.8 broadcast_in_dim.107
  33.1 4.2 %all-to-all-start.1 = ((bf16[8,32,1536]{2,1,0:T(8,128)(2,1)}), bf16[8,32,1536]{2,1,0:T(8,128)(2,1)}, u32[]{:S(2)}, u32[]{:S(2)}) async-start(bf16[8,32,1536]{2,1,0:T(8,128)(2,1)} %broadcast_in_dim.107), calls=%async_computation.1 | async-start | bytes 1572864 | tf_op jit(solution)/shard_map/all_to_all | solution.py:30
  37.3 1.8 collective-permute-start.5
  42.1 10.8 %collective-permute-done.4 = bf16[64,2688]{1,0:T(8,128)(2,1)S(1)} collective-permute-done((bf16[64,2688]{1,0:T(8,128)(2,1)}, bf16[64,2688]{1,0:T(8,128)(2,1)S(1)}, u32[]{:S(2)}, u32[]{:S(2)}) %collective-permute-start.4) | collective-permute-done | bytes 344096 | tf_op jit(solution)/shard_map/ppermute | solution.py:22
  55.4 2.7 %all-to-all-done.1 = bf16[8,32,1536]{2,1,0:T(8,128)(2,1)} async-done(((bf16[8,32,1536]{2,1,0:T(8,128)(2,1)}), bf16[8,32,1536]{2,1,0:T(8,128)(2,1)}, u32[]{:S(2)}, u32[]{:S(2)}) %all-to-all-start.1) | async-done | bytes 786464 | tf_op jit(solution)/shard_map/all_to_all | solution.py:30
  63.1 1.8 collective-permute-done.6
  66.1 2.2 fusion.56
  70.6 2.6 %fusion.21 = f32[256,161]{0,1:T(8,128)S(1)} fusion(bf16[256,4224]{1,0:T(8,128)(2,1)} %collective-permute-done.7, bf16[1536,161]{0,1:T(8,128)(2,1)S(1)} %copy-done.12, bf16[2560,161]{0,1:T(8,128)(2,1)S(1)} %copy-done.11, bf16[4224]{0:T(1024)(128)(2,1)S(1)} %pad.22.clone), kind=kOutput, calls=%fused_computation.39 | convolution fusion | flops 352273152 | bytes 3654912 | tf_op jit(solution)/shard_map/dot_general | solution.py:26
  74.1 1.7 broadcast_in_dim.115
  75.8 4.9 %all-to-all-start.3 = ((bf16[4,16,4096]{2,1,0:T(8,128)(2,1)}), bf16[4,16,4096]{2,1,0:T(8,128)(2,1)}, u32[]{:S(2)}, u32[]{:S(2)}) async-start(bf16[4,16,4096]{2,1,0:T(8,128)(2,1)} %broadcast_in_dim.115), calls=%async_computation.3 | async-start | bytes 1048576 | tf_op jit(solution)/shard_map/all_to_all | solution.py:30
  80.9 8.3 %all-to-all-done.3 = bf16[4,16,4096]{2,1,0:T(8,128)(2,1)} async-done(((bf16[4,16,4096]{2,1,0:T(8,128)(2,1)}), bf16[4,16,4096]{2,1,0:T(8,128)(2,1)}, u32[]{:S(2)}, u32[]{:S(2)}) %all-to-all-start.3) | async-done | bytes 524320 | tf_op jit(solution)/shard_map/all_to_all | solution.py:30
  89.9 6.8 %all-to-all-start.2 = ((f32[64,2,512]{2,1,0:T(2,128)}), f32[64,2,512]{2,1,0:T(2,128)}, u32[]{:S(2)}, u32[]{:S(2)}) async-start(f32[64,2,512]{2,1,0:T(2,128)} %broadcast_in_dim.111), calls=%async_computation.2 | async-start | bytes 524288 | tf_op jit(solution)/shard_map/all_to_all | solution.py:30
  96.7 1.5 fusion.15
  98.3 2.9 %fusion.6 = f32[64,7680]{1,0:T(8,128)S(1)} fusion(bf16[64,256]{1,0:T(8,128)(2,1)S(1)} %fusion.15, bf16[1,256,7680]{2,1,0:T(8,128)(2,1)} %param.19), kind=kOutput, calls=%fused_computation.13 | convolution fusion | flops 251658240 | bytes 5931008 | tf_op jit(solution)/shard_map/dot_general | solution.py:26
  103.6 2.0 collective-permute-start.14
  105.6 1.5 collective-permute-start.13
  108.5 2.0 fusion.116
  113.1 5.0 %collective-permute-done.12 = f32[16,7680]{1,0:T(8,128)} collective-permute-done((f32[16,7680]{1,0:T(8,128)}, f32[16,7680]{1,0:T(8,128)}, u32[]{:S(2)}, u32[]{:S(2)}) %collective-permute-start.12) | collective-permute-done | bytes 491552 | tf_op jit(solution)/shard_map/ppermute | solution.py:22
  118.0 11.1 %collective-permute-done.13 = f32[16,7680]{1,0:T(8,128)} collective-permute-done((f32[16,7680]{1,0:T(8,128)}, f32[16,7680]{1,0:T(8,128)}, u32[]{:S(2)}, u32[]{:S(2)}) %collective-permute-start.13) | collective-permute-done | bytes 491552 | tf_op jit(solution)/shard_map/ppermute | solution.py:22
  129.1 1.7 fusion.113
  131.4 3.2 %collective-permute-start.16 = (bf16[16,7680]{1,0:T(8,128)(2,1)S(1)}, bf16[16,7680]{1,0:T(8,128)(2,1)S(1)}, u32[]{:S(2)}, u32[]{:S(2)}) collective-permute-start(bf16[16,7680]{1,0:T(8,128)(2,1)S(1)} %multiply_convert_fusion), channel_id=1, source_target_pairs={{0,128},{64,192},{128,0},{192,64},{1,129},{65,193},{129,1},{193,65... | collective-permute-start | bytes 737288 | tf_op jit(solution)/shard_map/ppermute | solution.py:22
  134.6 2.3 %collective-permute-start.15 = (bf16[16,7680]{1,0:T(8,128)(2,1)S(1)}, bf16[16,7680]{1,0:T(8,128)(2,1)S(1)}, u32[]{:S(2)}, u32[]{:S(2)}) collective-permute-start(bf16[16,7680]{1,0:T(8,128)(2,1)S(1)} %multiply_convert_fusion), channel_id=1, source_target_pairs={{0,192},{64,0},{128,64},{192,128},{1,193},{65,1},{129,65},{193,129... | collective-permute-start | bytes 737288 | tf_op jit(solution)/shard_map/ppermute | solution.py:22
  137.8 2.4 %collective-permute-done.17 = bf16[16,7680]{1,0:T(8,128)(2,1)S(1)} collective-permute-done((bf16[16,7680]{1,0:T(8,128)(2,1)S(1)}, bf16[16,7680]{1,0:T(8,128)(2,1)S(1)}, u32[]{:S(2)}, u32[]{:S(2)}) %collective-permute-start.17) | collective-permute-done | bytes 245792 | tf_op jit(solution)/shard_map/ppermute | solution.py:22
  140.2 1.6 collective-permute-done.16
  141.8 3.4 %collective-permute-done.15 = bf16[16,7680]{1,0:T(8,128)(2,1)S(1)} collective-permute-done((bf16[16,7680]{1,0:T(8,128)(2,1)S(1)}, bf16[16,7680]{1,0:T(8,128)(2,1)S(1)}, u32[]{:S(2)}, u32[]{:S(2)}) %collective-permute-start.15) | collective-permute-done | bytes 245792 | tf_op jit(solution)/shard_map/ppermute | solution.py:22
  148.0 1.4 collective-permute-start.20
  149.4 2.3 %collective-permute-start.19 = (bf16[16,4096]{1,0:T(8,128)(2,1)S(1)}, bf16[16,4096]{1,0:T(8,128)(2,1)S(1)}, u32[]{:S(2)}, u32[]{:S(2)}) collective-permute-start(bf16[16,4096]{1,0:T(8,128)(2,1)S(1)} %get-tuple-element.59), channel_id=1, source_target_pairs={{0,128},{64,192},{128,0},{192,64},{1,129},{65,193},{129,1},{193,65... | collective-permute-start | bytes 393224 | tf_op jit(solution)/shard_map/ppermute | solution.py:22
  151.8 1.6 collective-permute-done.18
  153.7 3.5 %collective-permute-done.19 = bf16[16,4096]{1,0:T(8,128)(2,1)S(1)} collective-permute-done((bf16[16,4096]{1,0:T(8,128)(2,1)S(1)}, bf16[16,4096]{1,0:T(8,128)(2,1)S(1)}, u32[]{:S(2)}, u32[]{:S(2)}) %collective-permute-start.19) | collective-permute-done | bytes 131104 | tf_op jit(solution)/shard_map/ppermute | solution.py:22
  157.3 2.0 collective-permute-start.23
  159.3 2.9 %collective-permute-start.22 = (bf16[16,4096]{1,0:T(8,128)(2,1)S(1)}, bf16[16,4096]{1,0:T(8,128)(2,1)S(1)}, u32[]{:S(2)}, u32[]{:S(2)}) collective-permute-start(bf16[16,4096]{1,0:T(8,128)(2,1)S(1)} %fusion.35), channel_id=1, source_target_pairs={{0,32},{16,48},{32,0},{48,16},{1,33},{17,49},{33,1},{49,17},{2,34}... | collective-permute-start | bytes 393224 | tf_op jit(solution)/shard_map/ppermute | solution.py:22
  163.5 2.2 fusion.44
  169.9 2.3 %collective-permute-start.11 = (bf16[64,4096]{1,0:T(8,128)(2,1)S(1)}, bf16[64,4096]{1,0:T(8,128)(2,1)S(1)}, u32[]{:S(2)}, u32[]{:S(2)}) collective-permute-start(bf16[64,4096]{1,0:T(8,128)(2,1)S(1)} %get-tuple-element.49), channel_id=1, source_target_pairs={{0,48},{16,0},{32,16},{48,32},{1,49},{17,1},{33,17},{49,33},{2,50}... | collective-permute-start | bytes 1572872 | tf_op jit(solution)/shard_map/ppermute | solution.py:22
  175.6 8.9 %collective-permute-done.9 = bf16[64,4096]{1,0:T(8,128)(2,1)S(1)} collective-permute-done((bf16[64,4096]{1,0:T(8,128)(2,1)S(1)}, bf16[64,4096]{1,0:T(8,128)(2,1)S(1)}, u32[]{:S(2)}, u32[]{:S(2)}) %collective-permute-start.9) | collective-permute-done | bytes 524320 | tf_op jit(solution)/shard_map/ppermute | solution.py:22
  184.5 1.9 collective-permute-start.26
  186.4 8.6 %collective-permute-done.11 = bf16[64,4096]{1,0:T(8,128)(2,1)S(1)} collective-permute-done((bf16[64,4096]{1,0:T(8,128)(2,1)S(1)}, bf16[64,4096]{1,0:T(8,128)(2,1)S(1)}, u32[]{:S(2)}, u32[]{:S(2)}) %collective-permute-start.11) | collective-permute-done | bytes 524320 | tf_op jit(solution)/shard_map/ppermute | solution.py:22
  197.9 6.7 %all-to-all-start.4 = ((bf16[8,8,4096]{2,1,0:T(8,128)(2,1)}), bf16[8,8,4096]{2,1,0:T(8,128)(2,1)}, u32[]{:S(2)}, u32[]{:S(2)}) async-start(bf16[8,8,4096]{2,1,0:T(8,128)(2,1)} %fusion.25), calls=%async_computation.4 | async-start | bytes 1048576 | tf_op jit(solution)/shard_map/all_to_all | solution.py:30
  204.6 1.6 add_convert_fusion.1
  207.6 3.2 %fusion = bf16[1,256,7680]{2,1,0:T(8,128)(2,1)} fusion(bf16[16,7680]{1,0:T(8,128)(2,1)S(1)} %copy-done.14, bf16[16,7680]{1,0:T(8,128)(2,1)S(1)} %copy-done.16, bf16[16,7680]{1,0:T(8,128)(2,1)S(1)} %copy-done.18, bf16[16,7680]{1,0:T(8,128)(2,1)S(1)} %copy-done.10, s32[]{:T(128)S(6)} %select_n.217, bf16[64,256]{1,0:T(8,128)(2,1)S(1)} %fusion.15), kind=kOutput, calls=%fused_computation.1 | convolution fusion | flops 257622016 | bytes 4947972 | tf_op jit(solution)/shard_map/dot_general | solution.py:26
  210.8 3.1 %fusion.3 = bf16[1,4096,256]{2,1,0:T(8,128)(2,1)} fusion(bf16[64,256]{1,0:T(8,128)(2,1)S(1)} %fusion.12, s32[]{:T(128)S(6)} %select_n.217, bf16[64,4096]{1,0:T(8,128)(2,1)} %bitcast.9), kind=kOutput, calls=%fused_computation.8 | convolution fusion | flops 136314880 | bytes 2654212 | tf_op jit(solution)/shard_map/dot_general | solution.py:26
  213.9 8.1 %all-to-all-done.4 = bf16[8,8,4096]{2,1,0:T(8,128)(2,1)} async-done(((bf16[8,8,4096]{2,1,0:T(8,128)(2,1)}), bf16[8,8,4096]{2,1,0:T(8,128)(2,1)}, u32[]{:S(2)}, u32[]{:S(2)}) %all-to-all-start.4) | async-done | bytes 524320 | tf_op jit(solution)/shard_map/all_to_all | solution.py:30
  222.0 1.8 reduce_sum.75
  (160 shorter events, 44.6 us)
Async XLA Ops:
  0.6 96.1 %copy-start = (bf16[1,4096,256]{2,1,0:T(8,128)(2,1)S(1)}, bf16[1,4096,256]{2,1,0:T(8,128)(2,1)}, u32[]{:S(2)}) copy-start(bf16[1,4096,256]{2,1,0:T(8,128)(2,1)} %param.18) | copy-start | bytes 6291460
  1.5 17.9 %collective-permute-start.2 = (bf16[8,1536]{1,0:T(8,128)(2,1)S(1)}, bf16[8,1536]{1,0:T(8,128)(2,1)S(1)}, u32[]{:S(2)}, u32[]{:S(2)}) collective-permute-start(bf16[8,1536]{1,0:T(8,128)(2,1)S(1)} %slice.120), channel_id=1, source_target_pairs={{0,16},{16,32},{32,48},{48,0},{1,17},{17,33},{33,49},{49,1},{2,18}... | collective-permute-start | bytes 73736 | tf_op jit(solution)/shard_map/ppermute | solution.py:22
  3.0 16.4 %collective-permute-start.1 = (bf16[8,1536]{1,0:T(8,128)(2,1)S(1)}, bf16[8,1536]{1,0:T(8,128)(2,1)S(1)}, u32[]{:S(2)}, u32[]{:S(2)}) collective-permute-start(bf16[8,1536]{1,0:T(8,128)(2,1)S(1)} %slice.120), channel_id=1, source_target_pairs={{0,32},{16,48},{32,0},{48,16},{1,33},{17,49},{33,1},{49,17},{2,34}... | collective-permute-start | bytes 73736 | tf_op jit(solution)/shard_map/ppermute | solution.py:22
  5.8 13.7 %collective-permute-start = (bf16[8,1536]{1,0:T(8,128)(2,1)S(1)}, bf16[8,1536]{1,0:T(8,128)(2,1)}, u32[]{:S(2)}, u32[]{:S(2)}) collective-permute-start(bf16[8,1536]{1,0:T(8,128)(2,1)S(1)} %slice.120), channel_id=1, source_target_pairs={{0,48},{16,0},{32,16},{48,32},{1,49},{17,1},{33,17},{49,33},{2,50}... | collective-permute-start | bytes 73736 | tf_op jit(solution)/shard_map/ppermute | solution.py:22
  9.5 21.4 %all-to-all-start = ((bf16[8,8,2688]{2,1,0:T(8,128)(2,1)}), bf16[8,8,2688]{2,1,0:T(8,128)(2,1)}, u32[]{:S(2)}, u32[]{:S(2)}) async-start(bf16[8,8,2688]{2,1,0:T(8,128)(2,1)} %broadcast_in_dim.106), calls=%async_computation | async-start | bytes 688128 | tf_op jit(solution)/shard_map/all_to_all | solution.py:30
  30.9 10.2 %collective-permute-start.3 = (bf16[64,2688]{1,0:T(8,128)(2,1)}, bf16[64,2688]{1,0:T(8,128)(2,1)}, u32[]{:S(2)}, u32[]{:S(2)}) collective-permute-start(bf16[64,2688]{1,0:T(8,128)(2,1)} %bitcast), channel_id=1, source_target_pairs={{0,48},{16,0},{32,16},{48,32},{1,49},{17,1},{33,17},{49,33},{2,50}... | collective-permute-start | bytes 1032200 | tf_op jit(solution)/shard_map/ppermute | solution.py:22
  33.1 25.0 %all-to-all-start.1 = ((bf16[8,32,1536]{2,1,0:T(8,128)(2,1)}), bf16[8,32,1536]{2,1,0:T(8,128)(2,1)}, u32[]{:S(2)}, u32[]{:S(2)}) async-start(bf16[8,32,1536]{2,1,0:T(8,128)(2,1)} %broadcast_in_dim.107), calls=%async_computation.1 | async-start | bytes 1572864 | tf_op jit(solution)/shard_map/all_to_all | solution.py:30
  37.3 16.0 %collective-permute-start.5 = (bf16[64,2688]{1,0:T(8,128)(2,1)}, bf16[64,2688]{1,0:T(8,128)(2,1)S(1)}, u32[]{:S(2)}, u32[]{:S(2)}) collective-permute-start(bf16[64,2688]{1,0:T(8,128)(2,1)} %bitcast), channel_id=1, source_target_pairs={{0,16},{16,32},{32,48},{48,0},{1,17},{17,33},{33,49},{49,1},{2,18}... | collective-permute-start | bytes 1032200 | tf_op jit(solution)/shard_map/ppermute | solution.py:22
  39.1 13.7 %collective-permute-start.4 = (bf16[64,2688]{1,0:T(8,128)(2,1)}, bf16[64,2688]{1,0:T(8,128)(2,1)S(1)}, u32[]{:S(2)}, u32[]{:S(2)}) collective-permute-start(bf16[64,2688]{1,0:T(8,128)(2,1)} %bitcast), channel_id=1, source_target_pairs={{0,32},{16,48},{32,0},{48,16},{1,33},{17,49},{33,1},{49,17},{2,34}... | collective-permute-start | bytes 1032200 | tf_op jit(solution)/shard_map/ppermute | solution.py:22
  52.9 7.4 %copy-start.19 = (bf16[4096,1]{0,1:T(2,128)(2,1)S(1)}, bf16[4096,1]{0,1:T(2,128)(2,1)}, u32[]{:S(2)}) copy-start(bf16[4096,1]{0,1:T(2,128)(2,1)} %param.17) | copy-start | bytes 24580
  53.4 1.3 copy-start.1
  58.1 2.2 copy-start.6
  60.3 5.9 %collective-permute-start.7 = (bf16[256,4224]{1,0:T(8,128)(2,1)}, bf16[256,4224]{1,0:T(8,128)(2,1)}, u32[]{:S(2)}, u32[]{:S(2)}) collective-permute-start(bf16[256,4224]{1,0:T(8,128)(2,1)} %constant_dynamic-update-slice_fusion.6), channel_id=1, source_target_pairs={{0,1},{1,0},{2,3},{3,2},{4,5},{5,4},{6,7},{7,6},{8,9},{9,8},{10,11... | collective-permute-start | bytes 6488072 | tf_op jit(solution)/shard_map/ppermute | solution.py:22
  60.6 4.2 %collective-permute-start.6 = (f32[2,256]{1,0:T(2,128)S(1)}, f32[2,256]{1,0:T(2,128)S(1)}, u32[]{:S(2)}, u32[]{:S(2)}) collective-permute-start(f32[2,256]{1,0:T(2,128)S(1)} %get-tuple-element.69), channel_id=1, source_target_pairs={{0,1},{1,0},{2,3},{3,2},{4,5},{5,4},{6,7},{7,6},{8,9},{9,8},{10,11... | collective-permute-start | bytes 6152 | tf_op jit(solution)/shard_map/ppermute | solution.py:22
  65.7 2.7 %copy-start.2 = (bf16[256,4224]{1,0:T(8,128)(2,1)S(1)}, bf16[256,4224]{1,0:T(8,128)(2,1)}, u32[]{:S(2)}) copy-start(bf16[256,4224]{1,0:T(8,128)(2,1)} %constant_dynamic-update-slice_fusion.6) | copy-start | bytes 6488068
  70.6 2.7 %copy-start.7 = (f32[256,161]{0,1:T(8,128)}, f32[256,161]{0,1:T(8,128)S(1)}, u32[]{:S(2)}) copy-start(f32[256,161]{0,1:T(8,128)S(1)} %fusion.22) | copy-start | bytes 494596
  75.8 13.3 %all-to-all-start.3 = ((bf16[4,16,4096]{2,1,0:T(8,128)(2,1)}), bf16[4,16,4096]{2,1,0:T(8,128)(2,1)}, u32[]{:S(2)}, u32[]{:S(2)}) async-start(bf16[4,16,4096]{2,1,0:T(8,128)(2,1)} %broadcast_in_dim.115), calls=%async_computation.3 | async-start | bytes 1048576 | tf_op jit(solution)/shard_map/all_to_all | solution.py:30
  89.9 18.6 %all-to-all-start.2 = ((f32[64,2,512]{2,1,0:T(2,128)}), f32[64,2,512]{2,1,0:T(2,128)}, u32[]{:S(2)}, u32[]{:S(2)}) async-start(f32[64,2,512]{2,1,0:T(2,128)} %broadcast_in_dim.111), calls=%async_computation.2 | async-start | bytes 524288 | tf_op jit(solution)/shard_map/all_to_all | solution.py:30
  103.6 14.4 %collective-permute-start.12 = (f32[16,7680]{1,0:T(8,128)}, f32[16,7680]{1,0:T(8,128)}, u32[]{:S(2)}, u32[]{:S(2)}) collective-permute-start(f32[16,7680]{1,0:T(8,128)} %get-tuple-element.51), channel_id=1, source_target_pairs={{0,64},{64,128},{128,192},{192,0},{1,65},{65,129},{129,193},{193,1... | collective-permute-start | bytes 1474568 | tf_op jit(solution)/shard_map/ppermute | solution.py:22
  103.6 14.4 %collective-permute-start.14 = (f32[16,7680]{1,0:T(8,128)}, f32[16,7680]{1,0:T(8,128)}, u32[]{:S(2)}, u32[]{:S(2)}) collective-permute-start(f32[16,7680]{1,0:T(8,128)} %get-tuple-element.52), channel_id=1, source_target_pairs={{0,192},{64,0},{128,64},{192,128},{1,193},{65,1},{129,65},{193,129... | collective-permute-start | bytes 1474568 | tf_op jit(solution)/shard_map/ppermute | solution.py:22
  105.6 23.4 %collective-permute-start.13 = (f32[16,7680]{1,0:T(8,128)}, f32[16,7680]{1,0:T(8,128)}, u32[]{:S(2)}, u32[]{:S(2)}) collective-permute-start(f32[16,7680]{1,0:T(8,128)} %get-tuple-element.53), channel_id=1, source_target_pairs={{0,128},{64,192},{128,0},{192,64},{1,129},{65,193},{129,1},{193,65... | collective-permute-start | bytes 1474568 | tf_op jit(solution)/shard_map/ppermute | solution.py:22
  131.0 14.2 %copy-start.5 = (bf16[1,256,7680]{2,1,0:T(8,128)(2,1)S(1)}, bf16[1,256,7680]{2,1,0:T(8,128)(2,1)}, u32[]{:S(2)}) copy-start(bf16[1,256,7680]{2,1,0:T(8,128)(2,1)} %param.19) | copy-start | bytes 11796484
  131.3 15.2 %copy-start.9 = (bf16[16,7680]{1,0:T(8,128)(2,1)}, bf16[16,7680]{1,0:T(8,128)(2,1)S(1)}, u32[]{:S(2)}) copy-start(bf16[16,7680]{1,0:T(8,128)(2,1)S(1)} %multiply_convert_fusion) | copy-start | bytes 737284
  131.3 8.9 %collective-permute-start.17 = (bf16[16,7680]{1,0:T(8,128)(2,1)S(1)}, bf16[16,7680]{1,0:T(8,128)(2,1)S(1)}, u32[]{:S(2)}, u32[]{:S(2)}) collective-permute-start(bf16[16,7680]{1,0:T(8,128)(2,1)S(1)} %multiply_convert_fusion), channel_id=1, source_target_pairs={{0,64},{64,128},{128,192},{192,0},{1,65},{65,129},{129,193},{193,1... | collective-permute-start | bytes 737288 | tf_op jit(solution)/shard_map/ppermute | solution.py:22
  131.4 10.5 %collective-permute-start.16 = (bf16[16,7680]{1,0:T(8,128)(2,1)S(1)}, bf16[16,7680]{1,0:T(8,128)(2,1)S(1)}, u32[]{:S(2)}, u32[]{:S(2)}) collective-permute-start(bf16[16,7680]{1,0:T(8,128)(2,1)S(1)} %multiply_convert_fusion), channel_id=1, source_target_pairs={{0,128},{64,192},{128,0},{192,64},{1,129},{65,193},{129,1},{193,65... | collective-permute-start | bytes 737288 | tf_op jit(solution)/shard_map/ppermute | solution.py:22
  134.6 10.6 %collective-permute-start.15 = (bf16[16,7680]{1,0:T(8,128)(2,1)S(1)}, bf16[16,7680]{1,0:T(8,128)(2,1)S(1)}, u32[]{:S(2)}, u32[]{:S(2)}) collective-permute-start(bf16[16,7680]{1,0:T(8,128)(2,1)S(1)} %multiply_convert_fusion), channel_id=1, source_target_pairs={{0,192},{64,0},{128,64},{192,128},{1,193},{65,1},{129,65},{193,129... | collective-permute-start | bytes 737288 | tf_op jit(solution)/shard_map/ppermute | solution.py:22
  137.7 30.2 %collective-permute-start.8 = (bf16[256,4096]{1,0:T(8,128)(2,1)S(1)}, bf16[256,4096]{1,0:T(8,128)(2,1)S(1)}, u32[]{:S(2)}, u32[]{:S(2)}) collective-permute-start(bf16[256,4096]{1,0:T(8,128)(2,1)S(1)} %convolution_convert_fusion.2), channel_id=1, source_target_pairs={{0,1},{1,0},{2,3},{3,2},{4,5},{5,4},{6,7},{7,6},{8,9},{9,8},{10,11... | collective-permute-start | bytes 6291464 | tf_op jit(solution)/shard_map/ppermute | solution.py:22
  140.2 6.3 %copy-start.13 = (bf16[16,7680]{1,0:T(8,128)(2,1)}, bf16[16,7680]{1,0:T(8,128)(2,1)S(1)}, u32[]{:S(2)}) copy-start(bf16[16,7680]{1,0:T(8,128)(2,1)S(1)} %collective-permute-done.17) | copy-start | bytes 737284
  141.8 4.7 %copy-start.15 = (bf16[16,7680]{1,0:T(8,128)(2,1)}, bf16[16,7680]{1,0:T(8,128)(2,1)S(1)}, u32[]{:S(2)}) copy-start(bf16[16,7680]{1,0:T(8,128)(2,1)S(1)} %collective-permute-done.16) | copy-start | bytes 737284
  147.3 6.1 %collective-permute-start.18 = (bf16[16,4096]{1,0:T(8,128)(2,1)S(1)}, bf16[16,4096]{1,0:T(8,128)(2,1)S(1)}, u32[]{:S(2)}, u32[]{:S(2)}) collective-permute-start(bf16[16,4096]{1,0:T(8,128)(2,1)S(1)} %get-tuple-element.57), channel_id=1, source_target_pairs={{0,64},{64,128},{128,192},{192,0},{1,65},{65,129},{129,193},{193,1... | collective-permute-start | bytes 393224 | tf_op jit(solution)/shard_map/ppermute | solution.py:22
  148.0 5.7 %collective-permute-start.20 = (bf16[16,4096]{1,0:T(8,128)(2,1)S(1)}, bf16[16,4096]{1,0:T(8,128)(2,1)S(1)}, u32[]{:S(2)}, u32[]{:S(2)}) collective-permute-start(bf16[16,4096]{1,0:T(8,128)(2,1)S(1)} %get-tuple-element.58), channel_id=1, source_target_pairs={{0,192},{64,0},{128,64},{192,128},{1,193},{65,1},{129,65},{193,129... | collective-permute-start | bytes 393224 | tf_op jit(solution)/shard_map/ppermute | solution.py:22
  149.4 7.8 %collective-permute-start.19 = (bf16[16,4096]{1,0:T(8,128)(2,1)S(1)}, bf16[16,4096]{1,0:T(8,128)(2,1)S(1)}, u32[]{:S(2)}, u32[]{:S(2)}) collective-permute-start(bf16[16,4096]{1,0:T(8,128)(2,1)S(1)} %get-tuple-element.59), channel_id=1, source_target_pairs={{0,128},{64,192},{128,0},{192,64},{1,129},{65,193},{129,1},{193,65... | collective-permute-start | bytes 393224 | tf_op jit(solution)/shard_map/ppermute | solution.py:22
  157.3 8.4 %collective-permute-start.23 = (bf16[16,4096]{1,0:T(8,128)(2,1)S(1)}, bf16[16,4096]{1,0:T(8,128)(2,1)S(1)}, u32[]{:S(2)}, u32[]{:S(2)}) collective-permute-start(bf16[16,4096]{1,0:T(8,128)(2,1)S(1)} %fusion.35), channel_id=1, source_target_pairs={{0,16},{16,32},{32,48},{48,0},{1,17},{17,33},{33,49},{49,1},{2,18}... | collective-permute-start | bytes 393224 | tf_op jit(solution)/shard_map/ppermute | solution.py:22
  159.3 7.4 %collective-permute-start.22 = (bf16[16,4096]{1,0:T(8,128)(2,1)S(1)}, bf16[16,4096]{1,0:T(8,128)(2,1)S(1)}, u32[]{:S(2)}, u32[]{:S(2)}) collective-permute-start(bf16[16,4096]{1,0:T(8,128)(2,1)S(1)} %fusion.35), channel_id=1, source_target_pairs={{0,32},{16,48},{32,0},{48,16},{1,33},{17,49},{33,1},{49,17},{2,34}... | collective-permute-start | bytes 393224 | tf_op jit(solution)/shard_map/ppermute | solution.py:22
  162.2 5.0 %collective-permute-start.21 = (bf16[16,4096]{1,0:T(8,128)(2,1)S(1)}, bf16[16,4096]{1,0:T(8,128)(2,1)S(1)}, u32[]{:S(2)}, u32[]{:S(2)}) collective-permute-start(bf16[16,4096]{1,0:T(8,128)(2,1)S(1)} %fusion.35), channel_id=1, source_target_pairs={{0,48},{16,0},{32,16},{48,32},{1,49},{17,1},{33,17},{49,33},{2,50}... | collective-permute-start | bytes 393224 | tf_op jit(solution)/shard_map/ppermute | solution.py:22
  167.6 29.4 %collective-permute-start.24 = (bf16[64,4096]{1,0:T(8,128)(2,1)S(1)}, bf16[64,4096]{1,0:T(8,128)(2,1)S(1)}, u32[]{:S(2)}, u32[]{:S(2)}) collective-permute-start(bf16[64,4096]{1,0:T(8,128)(2,1)S(1)} %convolution_convert_fusion.3), channel_id=1, source_target_pairs={{0,1},{1,0},{2,3},{3,2},{4,5},{5,4},{6,7},{7,6},{8,9},{9,8},{10,11... | collective-permute-start | bytes 1572872 | tf_op jit(solution)/shard_map/ppermute | solution.py:22
  168.7 4.5 %copy-start.3 = (bf16[256,4224]{1,0:T(8,128)(2,1)S(1)}, bf16[256,4224]{1,0:T(8,128)(2,1)}, u32[]{:S(2)}) copy-start(bf16[256,4224]{1,0:T(8,128)(2,1)} %constant_dynamic-update-slice_fusion.6) | copy-start | bytes 6488068
  168.9 15.6 %collective-permute-start.9 = (bf16[64,4096]{1,0:T(8,128)(2,1)S(1)}, bf16[64,4096]{1,0:T(8,128)(2,1)S(1)}, u32[]{:S(2)}, u32[]{:S(2)}) collective-permute-start(bf16[64,4096]{1,0:T(8,128)(2,1)S(1)} %get-tuple-element.48), channel_id=1, source_target_pairs={{0,16},{16,32},{32,48},{48,0},{1,17},{17,33},{33,49},{49,1},{2,18}... | collective-permute-start | bytes 1572872 | tf_op jit(solution)/shard_map/ppermute | solution.py:22
  169.9 25.2 %collective-permute-start.11 = (bf16[64,4096]{1,0:T(8,128)(2,1)S(1)}, bf16[64,4096]{1,0:T(8,128)(2,1)S(1)}, u32[]{:S(2)}, u32[]{:S(2)}) collective-permute-start(bf16[64,4096]{1,0:T(8,128)(2,1)S(1)} %get-tuple-element.49), channel_id=1, source_target_pairs={{0,48},{16,0},{32,16},{48,32},{1,49},{17,1},{33,17},{49,33},{2,50}... | collective-permute-start | bytes 1572872 | tf_op jit(solution)/shard_map/ppermute | solution.py:22
  172.2 24.3 %collective-permute-start.10 = (bf16[64,4096]{1,0:T(8,128)(2,1)S(1)}, bf16[64,4096]{1,0:T(8,128)(2,1)S(1)}, u32[]{:S(2)}, u32[]{:S(2)}) collective-permute-start(bf16[64,4096]{1,0:T(8,128)(2,1)S(1)} %get-tuple-element.50), channel_id=1, source_target_pairs={{0,32},{16,48},{32,0},{48,16},{1,33},{17,49},{33,1},{49,17},{2,34}... | collective-permute-start | bytes 1572872 | tf_op jit(solution)/shard_map/ppermute | solution.py:22
  175.2 29.4 %collective-permute-start.25 = (bf16[161,1024]{1,0:T(8,128)(2,1)}, bf16[161,1024]{1,0:T(8,128)(2,1)}, u32[]{:S(2)}, u32[]{:S(2)}) collective-permute-start(bf16[161,1024]{1,0:T(8,128)(2,1)} %get-tuple-element.54), channel_id=1, source_target_pairs={{0,64},{64,128},{128,192},{192,0},{1,65},{65,129},{129,193},{193,1... | collective-permute-start | bytes 989192 | tf_op jit(solution)/shard_map/ppermute | solution.py:22
  184.5 20.1 %collective-permute-start.26 = (bf16[161,1024]{1,0:T(8,128)(2,1)}, bf16[161,1024]{1,0:T(8,128)(2,1)}, u32[]{:S(2)}, u32[]{:S(2)}) collective-permute-start(bf16[161,1024]{1,0:T(8,128)(2,1)} %get-tuple-element.55), channel_id=1, source_target_pairs={{0,128},{64,192},{128,0},{192,64},{1,129},{65,193},{129,1},{193,65... | collective-permute-start | bytes 989192 | tf_op jit(solution)/shard_map/ppermute | solution.py:22
  195.0 9.6 %collective-permute-start.27 = (bf16[161,1024]{1,0:T(8,128)(2,1)}, bf16[161,1024]{1,0:T(8,128)(2,1)}, u32[]{:S(2)}, u32[]{:S(2)}) collective-permute-start(bf16[161,1024]{1,0:T(8,128)(2,1)} %get-tuple-element.56), channel_id=1, source_target_pairs={{0,192},{64,0},{128,64},{192,128},{1,193},{65,1},{129,65},{193,129... | collective-permute-start | bytes 989192 | tf_op jit(solution)/shard_map/ppermute | solution.py:22
  197.9 24.1 %all-to-all-start.4 = ((bf16[8,8,4096]{2,1,0:T(8,128)(2,1)}), bf16[8,8,4096]{2,1,0:T(8,128)(2,1)}, u32[]{:S(2)}, u32[]{:S(2)}) async-start(bf16[8,8,4096]{2,1,0:T(8,128)(2,1)} %fusion.25), calls=%async_computation.4 | async-start | bytes 1048576 | tf_op jit(solution)/shard_map/all_to_all | solution.py:30
  204.6 3.0 %copy-start.10 = (bf16[16,7680]{1,0:T(8,128)(2,1)S(1)}, bf16[16,7680]{1,0:T(8,128)(2,1)}, u32[]{:S(2)}) copy-start(bf16[16,7680]{1,0:T(8,128)(2,1)} %copy-done.9) | copy-start | bytes 737284
  204.6 3.0 %copy-start.14 = (bf16[16,7680]{1,0:T(8,128)(2,1)S(1)}, bf16[16,7680]{1,0:T(8,128)(2,1)}, u32[]{:S(2)}) copy-start(bf16[16,7680]{1,0:T(8,128)(2,1)} %copy-done.13) | copy-start | bytes 737284
  204.6 3.0 %copy-start.16 = (bf16[16,7680]{1,0:T(8,128)(2,1)S(1)}, bf16[16,7680]{1,0:T(8,128)(2,1)}, u32[]{:S(2)}) copy-start(bf16[16,7680]{1,0:T(8,128)(2,1)} %copy-done.15) | copy-start | bytes 737284
  204.6 3.0 %copy-start.18 = (bf16[16,7680]{1,0:T(8,128)(2,1)S(1)}, bf16[16,7680]{1,0:T(8,128)(2,1)}, u32[]{:S(2)}) copy-start(bf16[16,7680]{1,0:T(8,128)(2,1)} %copy-done.17) | copy-start | bytes 737284
  (5 other events, 5.8 us)
